TPU v7x, 512 devices: a whole 4x8x8 slice. The times are simulated.
512 devices in a mesh: ctx: 16 (over z_hi, y), dp: 32 (over z_lo, x, core).
Axes of the slice: x: 4, y: 8, z: 8 (z_hi: 2, z_lo: 4; z = z_hi * 4 + z_lo), core: 2. Of those that a mesh axis runs over, the one named last changes fastest.
Arguments:
- queries: bfloat16 [32, 2048, 2048], P('dp', 'ctx'), may hold values from -8 to 8
- key_rows: bfloat16 [32, 2048, 256], P('dp', 'ctx'), may hold values from -8 to 8
- value_rows: bfloat16 [32, 2048, 256], P('dp', 'ctx'), may hold values from -6 to 6
- stream: bfloat16 [32, 2048, 2048], P('dp', 'ctx'), may hold values from -6 to 6
- norm_gain: float32 [2048], replicated, may hold values from 0.1 to 1.9
- expert_ids: int32 [32, 2048, 8], P('dp', 'ctx'), may hold values from 0 to 127, all different within a row; in each aligned block of 128 rows (0 to 127, 128 to 255, ..., all dimensions but the last counted through in order) at most 12 rows name the same one
- gate_values: float32 [32, 2048, 8], P('dp', 'ctx'), may hold values from 0.1 to 1
- w_gate: bfloat16 [32, 2048, 384], P('dp', 'ctx'), may hold values from -0.125 to 0.125
- w_up: bfloat16 [32, 2048, 384], P('dp', 'ctx'), may hold values from -0.125 to 0.125
- w_down: bfloat16 [32, 384, 2048], P('dp', None, 'ctx'), may hold values from -0.3125 to 0.3125
Outputs:
- attended: bfloat16 [32, 2048, 2048], P('dp', 'ctx')
- expert_out: bfloat16 [32, 2048, 2048], P('dp', 'ctx')
Inputs may be any that keep to these rules, and one draw needn't show every extreme that they name: `expert_ids`: among the rows of one device, no expert is chosen by more than 12 rows; some expert reaches 12.
All inputs are finite; a program needn't handle non-finite values.
Results may differ from a plain program's by a relative error of at most 0.012.
Values may be sent and summed in bfloat16 or wider, within the bound.
No kernel may reach another device: no remote copies, remote signals or barrier semaphores. Data moves between devices by JAX's collectives and lax.ppermute only.
A program may use at most 64 MiB of HBM per device.

v0:
```python
import math

import jax
import jax.numpy as jnp
from jax import lax
from jax.sharding import PartitionSpec as P

HD = 128
CAP = 12


masked_score = -1e30


def passed_along(block, axis, distance):
    devices = range(lax.axis_size(axis))
    route = [(i - distance, i) for i in devices if i - distance in devices]
    return lax.ppermute(block, axis, route)


def attend_block(state, query_blocks, key_block, value_block, query_pos, key_start):
    largest, total, accum = state
    scale = 1.0 / math.sqrt(query_blocks.shape[-1])
    scores = (
        jnp.einsum("hrd,hkd->hrk", query_blocks, key_block, preferred_element_type=jnp.float32)
        * scale
    )
    key_pos = key_start + jnp.arange(key_block.shape[1], dtype=jnp.int32)
    allowed = key_pos[None, None, :] <= query_pos[None, :, None]
    block_max = jnp.max(jnp.where(allowed, scores, masked_score), axis=-1)
    new_max = jnp.maximum(largest, block_max)
    weights = jnp.where(allowed, jnp.exp(scores - new_max[..., None]), 0.0)
    rescale = jnp.exp(largest - new_max)
    total = total * rescale + jnp.sum(weights, axis=-1)
    accum = accum * rescale[..., None] + jnp.einsum(
        "hrk,hkd->hrd",
        weights.astype(jnp.bfloat16),
        value_block,
        preferred_element_type=jnp.float32,
    )
    return (new_max, total, accum)


def shards(
    queries, key_rows, value_rows, stream, norm_gain, expert_ids, gate_values, w_gate, w_up, w_down
):
    tokens = queries.shape[1]
    heads_kv = key_rows.shape[2] // HD
    group = queries.shape[2] // key_rows.shape[2]
    query_blocks = (
        queries[0]
        .reshape(tokens, heads_kv, group, HD)
        .transpose(1, 2, 0, 3)
        .reshape(heads_kv, group * tokens, HD)
    )
    key_local = key_rows[0].reshape(tokens, heads_kv, HD).transpose(1, 0, 2)
    value_local = value_rows[0].reshape(tokens, heads_kv, HD).transpose(1, 0, 2)
    block_pos = lax.axis_index("ctx")
    block_count = lax.axis_size("ctx")
    query_pos = block_pos * tokens + jnp.arange(group * tokens, dtype=jnp.int32) % tokens
    last_query = block_pos * tokens + tokens - 1
    state = (
        jnp.full((heads_kv, group * tokens), masked_score, jnp.float32),
        jnp.zeros((heads_kv, group * tokens), jnp.float32),
        jnp.zeros((heads_kv, group * tokens, HD), jnp.float32),
    )

    def maybe_attend(current, key_block, value_block, key_start):

        def compute(inner):
            return attend_block(inner, query_blocks, key_block, value_block, query_pos, key_start)

        def unchanged(inner):
            return inner

        return lax.cond(key_start <= last_query, compute, unchanged, current)

    state = attend_block(state, query_blocks, key_local, value_local, query_pos, block_pos * tokens)

    def pass_turn(turn, carry):
        current, key_block, value_block = carry
        key_block, value_block = passed_along((key_block, value_block), "ctx", 1)
        source = (block_pos - turn - 1) % block_count
        current = maybe_attend(current, key_block, value_block, source * tokens)
        return (current, key_block, value_block)

    state, key_last, value_last = lax.fori_loop(
        0, block_count - 1, pass_turn, (state, key_local, value_local)
    )
    largest, total, accum = state
    attended = (accum / total[..., None]).reshape(heads_kv, group, tokens, HD).transpose(2, 0, 1, 3)
    attended = attended.reshape(1, tokens, heads_kv * group * HD).astype(jnp.bfloat16)
    width = stream.shape[2]
    rows_in = stream[0].astype(jnp.float32)
    normed = (
        rows_in * lax.rsqrt(jnp.mean(rows_in * rows_in, axis=-1, keepdims=True) + 1e-06) * norm_gain
    ).astype(jnp.bfloat16)
    owners = lax.axis_size("dp")
    slots = owners * CAP
    top_count = expert_ids.shape[2]
    chosen = expert_ids[0].reshape(-1)
    weights_flat = gate_values[0].reshape(-1)
    owner_hot = (chosen[:, None] == jnp.arange(owners, dtype=jnp.int32)[None, :]).astype(jnp.int32)
    ranks = jnp.sum((jnp.cumsum(owner_hot, axis=0) - 1) * owner_hot, axis=1)
    target = jnp.where(chosen < owners, chosen * CAP + ranks, -1)
    slot_hot = target[:, None] == jnp.arange(slots, dtype=jnp.int32)[None, :]
    placement = jnp.sum(
        slot_hot.astype(jnp.float32).reshape(tokens, top_count, slots), axis=1
    ).astype(jnp.bfloat16)
    slot_weight = jnp.sum(jnp.where(slot_hot, weights_flat[:, None], 0.0), axis=0)
    outgoing = jnp.einsum(
        "ts,td->sd", placement, normed, preferred_element_type=jnp.float32
    ).astype(jnp.bfloat16)
    arrived = lax.all_to_all(
        outgoing.reshape(owners, CAP, width), "dp", split_axis=0, concat_axis=0, tiled=True
    ).reshape(slots, width)
    gate_piece = lax.all_gather(w_gate, "ctx", axis=1, tiled=True)
    up_piece = lax.all_gather(w_up, "ctx", axis=1, tiled=True)
    gate_sum = jnp.dot(arrived, gate_piece[0], preferred_element_type=jnp.float32)
    up_sum = jnp.dot(arrived, up_piece[0], preferred_element_type=jnp.float32)
    hidden = (jax.nn.silu(gate_sum) * up_sum).astype(jnp.bfloat16)
    produced = jnp.dot(
        hidden,
        lax.all_gather(w_down, "ctx", axis=2, tiled=True)[0],
        preferred_element_type=jnp.float32,
    )
    answers = produced.astype(jnp.bfloat16).reshape(owners, CAP, width)
    returned = lax.all_to_all(answers, "dp", split_axis=0, concat_axis=0, tiled=True).reshape(
        slots, width
    )
    weighted = returned.astype(jnp.float32) * slot_weight[:, None]
    upper_part = weighted.astype(jnp.bfloat16)
    lower_part = (weighted - upper_part.astype(jnp.float32)).astype(jnp.bfloat16)
    mixed = jnp.dot(placement, upper_part, preferred_element_type=jnp.float32) + jnp.dot(
        placement, lower_part, preferred_element_type=jnp.float32
    )
    expert_out = mixed.astype(jnp.bfloat16).reshape(1, tokens, width)
    return (attended, expert_out)


def solution(mesh):
    placed = (
        P("dp", "ctx", None),
        P("dp", "ctx", None),
        P("dp", "ctx", None),
        P("dp", "ctx", None),
        P(),
        P("dp", "ctx", None),
        P("dp", "ctx", None),
        P("dp", "ctx", None),
        P("dp", "ctx", None),
        P("dp", None, "ctx"),
    )
    return jax.shard_map(
        shards,
        mesh=mesh,
        in_specs=placed,
        out_specs=(P("dp", "ctx", None), P("dp", "ctx", None)),
        check_vma=False,
    )
```

profile of v0, /device:TPU:62, one launch (start us, length us, event | category | flops | bytes accessed | tf_op | source)
XLA Modules:
  0.0 572.4 jit_solution(15209295898949841804)
XLA Ops:
  9.7 9.0 %reduce-window.6 = s32[32,8,128]{2,1,0:T(8,128)S(1)} reduce-window(s32[32,8,128]{2,1,0:T(8,128)S(1)} %fusion.49, s32[]{:T(128)} %constant.106.clone.1), window={size=1x1x128 pad=0_0x0_0x127_0}, to_apply=%region_8.9 | reduce-window | flops 4161536 | bytes 262148 | tf_op jit(solution)/shard_map/reduce-window
  22.2 10.5 %all-to-all-start = ((bf16[32,12,2048]{2,1,0:T(8,128)(2,1)}), bf16[32,12,2048]{2,1,0:T(8,128)(2,1)}, u32[]{:S(2)}, u32[]{:S(2)}) async-start(bf16[32,12,2048]{2,1,0:T(8,128)(2,1)} %reshape.192), calls=%async_computation | async-start | bytes 4194304 | tf_op jit(solution)/shard_map/all_to_all | solution.py:114
  35.1 64.5 %all-to-all-done = bf16[32,12,2048]{2,1,0:T(8,128)(2,1)} async-done(((bf16[32,12,2048]{2,1,0:T(8,128)(2,1)}), bf16[32,12,2048]{2,1,0:T(8,128)(2,1)}, u32[]{:S(2)}, u32[]{:S(2)}) %all-to-all-start) | async-done | bytes 1572896 | tf_op jit(solution)/shard_map/all_to_all | solution.py:114
  99.6 3.6 reshape.193
  103.2 3.9 all-gather.4.cloned.1.call-done
  107.1 2.8 fusion.16
  110.0 103.4 %all-gather.6.cloned.1.call-done = bf16[1,2048,384]{2,1,0:T(8,128)(2,1)} async-done(((bf16[1,128,384]{2,1,0:T(8,128)(2,1)}), bf16[1,2048,384]{2,1,0:T(8,128)(2,1)}) %all-gather.6.cloned.1.call-update) | async-done | bytes 1572880 | tf_op jit(solution)/shard_map/all_gather | solution.py:118
  213.4 97.3 %all-gather.8.cloned.1.call-done = bf16[1,384,2048]{2,1,0:T(8,128)(2,1)} async-done(((bf16[1,384,128]{2,1,0:T(8,128)(2,1)}), bf16[1,384,2048]{2,1,0:T(8,128)(2,1)}) %all-gather.8.cloned.1.call-update) | async-done | bytes 1572880 | tf_op jit(solution)/shard_map/all_gather | solution.py:124
  310.6 5.4 convolution_convert_fusion
  316.0 3.6 reshape.194
  319.6 5.4 all-to-all-start.1
  326.1 233.3 %while.24 = (s32[]{:T(128)}, f32[2,1024]{1,0:T(2,128)S(1)}, f32[2,1024]{1,0:T(2,128)S(1)}, f32[2,1024,128]{2,1,0:T(8,128)S(1)}, bf16[2,128,128]{2,1,0:T(8,128)(2...) while((s32[]{:T(128)}, f32[2,1024]{1,0:T(2,128)S(1)}, ...), condition=%wide.region_7.8_spmd.clone, body=%wide.region_2.7_spmd.clone.sunk | while | flops 137243792 | bytes 7378492 | solution.py:87
  326.1 4.6 collective-permute-start
  330.8 2.5 collective-permute-start.1
  333.3 3.6 collective-permute-done.1
  336.9 1.6 conditional.3
  338.6 10.2 %collective-permute-start = (bf16[2,128,128]{2,1,0:T(8,128)(2,1)S(1)}, bf16[2,128,128]{2,1,0:T(8,128)(2,1)S(1)}, u32[]{:S(2)}, u32[]{:S(2)}) collective-permute-start(bf16[2,128,128]{2,1,0:T(8,128)(2,1)S(1)} %get-tuple-element.508), channel_id=1, source_target_pairs={{0,32},{32,64},{64,96},{96,128},{128,160},{160,192},{192,224},{224... | collective-permute-start | bytes 196616 | tf_op jit(solution)/shard_map/while/body/eval_jaxpr/ppermute | solution.py:18
  348.8 1.9 collective-permute-start.1
  350.8 4.2 collective-permute-done.1
  355.0 1.6 conditional.3
  356.7 8.7 %collective-permute-start = (bf16[2,128,128]{2,1,0:T(8,128)(2,1)S(1)}, bf16[2,128,128]{2,1,0:T(8,128)(2,1)S(1)}, u32[]{:S(2)}, u32[]{:S(2)}) collective-permute-start(bf16[2,128,128]{2,1,0:T(8,128)(2,1)S(1)} %get-tuple-element.508), channel_id=1, source_target_pairs={{0,32},{32,64},{64,96},{96,128},{128,160},{160,192},{192,224},{224... | collective-permute-start | bytes 196616 | tf_op jit(solution)/shard_map/while/body/eval_jaxpr/ppermute | solution.py:18
  365.4 1.9 collective-permute-start.1
  367.4 4.2 collective-permute-done.1
  371.6 1.6 conditional.3
  373.3 8.7 %collective-permute-start = (bf16[2,128,128]{2,1,0:T(8,128)(2,1)S(1)}, bf16[2,128,128]{2,1,0:T(8,128)(2,1)S(1)}, u32[]{:S(2)}, u32[]{:S(2)}) collective-permute-start(bf16[2,128,128]{2,1,0:T(8,128)(2,1)S(1)} %get-tuple-element.508), channel_id=1, source_target_pairs={{0,32},{32,64},{64,96},{96,128},{128,160},{160,192},{192,224},{224... | collective-permute-start | bytes 196616 | tf_op jit(solution)/shard_map/while/body/eval_jaxpr/ppermute | solution.py:18
  382.0 1.9 collective-permute-start.1
  384.0 4.2 collective-permute-done.1
  388.2 1.6 conditional.3
  389.9 8.2 %collective-permute-start = (bf16[2,128,128]{2,1,0:T(8,128)(2,1)S(1)}, bf16[2,128,128]{2,1,0:T(8,128)(2,1)S(1)}, u32[]{:S(2)}, u32[]{:S(2)}) collective-permute-start(bf16[2,128,128]{2,1,0:T(8,128)(2,1)S(1)} %get-tuple-element.508), channel_id=1, source_target_pairs={{0,32},{32,64},{64,96},{96,128},{128,160},{160,192},{192,224},{224... | collective-permute-start | bytes 196616 | tf_op jit(solution)/shard_map/while/body/eval_jaxpr/ppermute | solution.py:18
  398.1 1.9 collective-permute-start.1
  400.0 4.2 collective-permute-done.1
  404.2 1.6 conditional.3
  405.9 8.2 %collective-permute-start = (bf16[2,128,128]{2,1,0:T(8,128)(2,1)S(1)}, bf16[2,128,128]{2,1,0:T(8,128)(2,1)S(1)}, u32[]{:S(2)}, u32[]{:S(2)}) collective-permute-start(bf16[2,128,128]{2,1,0:T(8,128)(2,1)S(1)} %get-tuple-element.508), channel_id=1, source_target_pairs={{0,32},{32,64},{64,96},{96,128},{128,160},{160,192},{192,224},{224... | collective-permute-start | bytes 196616 | tf_op jit(solution)/shard_map/while/body/eval_jaxpr/ppermute | solution.py:18
  414.1 1.9 collective-permute-start.1
  416.1 4.8 collective-permute-done.1
  422.6 7.6 %collective-permute-start = (bf16[2,128,128]{2,1,0:T(8,128)(2,1)S(1)}, bf16[2,128,128]{2,1,0:T(8,128)(2,1)S(1)}, u32[]{:S(2)}, u32[]{:S(2)}) collective-permute-start(bf16[2,128,128]{2,1,0:T(8,128)(2,1)S(1)} %get-tuple-element.508), channel_id=1, source_target_pairs={{0,32},{32,64},{64,96},{96,128},{128,160},{160,192},{192,224},{224... | collective-permute-start | bytes 196616 | tf_op jit(solution)/shard_map/while/body/eval_jaxpr/ppermute | solution.py:18
  430.2 1.9 collective-permute-start.1
  432.2 4.5 collective-permute-done.1
  436.6 1.6 conditional.3
  438.3 7.9 %collective-permute-start = (bf16[2,128,128]{2,1,0:T(8,128)(2,1)S(1)}, bf16[2,128,128]{2,1,0:T(8,128)(2,1)S(1)}, u32[]{:S(2)}, u32[]{:S(2)}) collective-permute-start(bf16[2,128,128]{2,1,0:T(8,128)(2,1)S(1)} %get-tuple-element.508), channel_id=1, source_target_pairs={{0,32},{32,64},{64,96},{96,128},{128,160},{160,192},{192,224},{224... | collective-permute-start | bytes 196616 | tf_op jit(solution)/shard_map/while/body/eval_jaxpr/ppermute | solution.py:18
  446.3 1.9 collective-permute-start.1
  448.2 4.2 collective-permute-done.1
  452.5 9.8 %collective-permute-start = (bf16[2,128,128]{2,1,0:T(8,128)(2,1)S(1)}, bf16[2,128,128]{2,1,0:T(8,128)(2,1)S(1)}, u32[]{:S(2)}, u32[]{:S(2)}) collective-permute-start(bf16[2,128,128]{2,1,0:T(8,128)(2,1)S(1)} %get-tuple-element.508), channel_id=1, source_target_pairs={{0,32},{32,64},{64,96},{96,128},{128,160},{160,192},{192,224},{224... | collective-permute-start | bytes 196616 | tf_op jit(solution)/shard_map/while/body/eval_jaxpr/ppermute | solution.py:18
  462.3 1.9 collective-permute-start.1
  464.3 4.2 collective-permute-done.1
  468.5 8.2 %collective-permute-start = (bf16[2,128,128]{2,1,0:T(8,128)(2,1)S(1)}, bf16[2,128,128]{2,1,0:T(8,128)(2,1)S(1)}, u32[]{:S(2)}, u32[]{:S(2)}) collective-permute-start(bf16[2,128,128]{2,1,0:T(8,128)(2,1)S(1)} %get-tuple-element.508), channel_id=1, source_target_pairs={{0,32},{32,64},{64,96},{96,128},{128,160},{160,192},{192,224},{224... | collective-permute-start | bytes 196616 | tf_op jit(solution)/shard_map/while/body/eval_jaxpr/ppermute | solution.py:18
  476.7 1.9 collective-permute-start.1
  478.7 4.2 collective-permute-done.1
  482.9 9.1 %collective-permute-start = (bf16[2,128,128]{2,1,0:T(8,128)(2,1)S(1)}, bf16[2,128,128]{2,1,0:T(8,128)(2,1)S(1)}, u32[]{:S(2)}, u32[]{:S(2)}) collective-permute-start(bf16[2,128,128]{2,1,0:T(8,128)(2,1)S(1)} %get-tuple-element.508), channel_id=1, source_target_pairs={{0,32},{32,64},{64,96},{96,128},{128,160},{160,192},{192,224},{224... | collective-permute-start | bytes 196616 | tf_op jit(solution)/shard_map/while/body/eval_jaxpr/ppermute | solution.py:18
  492.0 1.9 collective-permute-start.1
  494.0 4.4 collective-permute-done.1
  498.4 9.0 %collective-permute-start = (bf16[2,128,128]{2,1,0:T(8,128)(2,1)S(1)}, bf16[2,128,128]{2,1,0:T(8,128)(2,1)S(1)}, u32[]{:S(2)}, u32[]{:S(2)}) collective-permute-start(bf16[2,128,128]{2,1,0:T(8,128)(2,1)S(1)} %get-tuple-element.508), channel_id=1, source_target_pairs={{0,32},{32,64},{64,96},{96,128},{128,160},{160,192},{192,224},{224... | collective-permute-start | bytes 196616 | tf_op jit(solution)/shard_map/while/body/eval_jaxpr/ppermute | solution.py:18
  507.4 1.9 collective-permute-start.1
  509.7 4.1 collective-permute-done.1
  513.9 9.5 %collective-permute-start = (bf16[2,128,128]{2,1,0:T(8,128)(2,1)S(1)}, bf16[2,128,128]{2,1,0:T(8,128)(2,1)S(1)}, u32[]{:S(2)}, u32[]{:S(2)}) collective-permute-start(bf16[2,128,128]{2,1,0:T(8,128)(2,1)S(1)} %get-tuple-element.508), channel_id=1, source_target_pairs={{0,32},{32,64},{64,96},{96,128},{128,160},{160,192},{192,224},{224... | collective-permute-start | bytes 196616 | tf_op jit(solution)/shard_map/while/body/eval_jaxpr/ppermute | solution.py:18
  523.5 1.9 collective-permute-start.1
  525.4 4.2 collective-permute-done.1
  529.7 8.8 %collective-permute-start = (bf16[2,128,128]{2,1,0:T(8,128)(2,1)S(1)}, bf16[2,128,128]{2,1,0:T(8,128)(2,1)S(1)}, u32[]{:S(2)}, u32[]{:S(2)}) collective-permute-start(bf16[2,128,128]{2,1,0:T(8,128)(2,1)S(1)} %get-tuple-element.508), channel_id=1, source_target_pairs={{0,32},{32,64},{64,96},{96,128},{128,160},{160,192},{192,224},{224... | collective-permute-start | bytes 196616 | tf_op jit(solution)/shard_map/while/body/eval_jaxpr/ppermute | solution.py:18
  538.5 1.9 collective-permute-start.1
  540.9 3.8 collective-permute-done.1
  544.7 8.5 %collective-permute-start = (bf16[2,128,128]{2,1,0:T(8,128)(2,1)S(1)}, bf16[2,128,128]{2,1,0:T(8,128)(2,1)S(1)}, u32[]{:S(2)}, u32[]{:S(2)}) collective-permute-start(bf16[2,128,128]{2,1,0:T(8,128)(2,1)S(1)} %get-tuple-element.508), channel_id=1, source_target_pairs={{0,32},{32,64},{64,96},{96,128},{128,160},{160,192},{192,224},{224... | collective-permute-start | bytes 196616 | tf_op jit(solution)/shard_map/while/body/eval_jaxpr/ppermute | solution.py:18
  553.2 1.9 collective-permute-start.1
  555.2 4.2 collective-permute-done.1
  561.5 2.5 reshape.197
  (207 shorter events, 27.0 us)
Async XLA Ops:
  7.2 12.7 %copy-start = (bf16[1,128,2048]{2,1,0:T(8,128)(2,1)S(1)}, bf16[1,128,2048]{2,1,0:T(8,128)(2,1)}, u32[]{:S(2)}) copy-start(bf16[1,128,2048]{2,1,0:T(8,128)(2,1)} %param.17) | copy-start | bytes 1572868
  7.2 12.9 %copy-start.4 = (f32[2048]{0:T(1024)S(1)}, f32[2048]{0:T(1024)}, u32[]{:S(2)}) copy-start(f32[2048]{0:T(1024)} %param.18) | copy-start | bytes 24580
  7.2 99.9 %all-gather.4.cloned.1.call-start = ((), (), s32[]{:S(2)}) async-start(), calls=%async_computation.2 | async-start | bytes 1671168 | tf_op jit(solution)/shard_map/all_gather | solution.py:117
  7.9 205.5 %all-gather.6.cloned.1.call-start = ((), (), s32[]{:S(2)}) async-start(), calls=%async_computation.3 | async-start | bytes 1671168 | tf_op jit(solution)/shard_map/all_gather | solution.py:118
  22.2 11.3 %copy-start.5 = (f32[1,128,8]{1,2,0:T(8,128)S(1)}, f32[1,128,8]{1,2,0:T(8,128)}, u32[]{:S(2)}) copy-start(f32[1,128,8]{1,2,0:T(8,128)} %param.20) | copy-start | bytes 12292
  22.2 11.5 %copy-start.1 = (bf16[1,128,2048]{2,1,0:T(8,128)(2,1)S(1)}, bf16[1,128,2048]{2,1,0:T(8,128)(2,1)}, u32[]{:S(2)}) copy-start(bf16[1,128,2048]{2,1,0:T(8,128)(2,1)} %param.14) | copy-start | bytes 1572868
  22.2 77.4 %all-to-all-start = ((bf16[32,12,2048]{2,1,0:T(8,128)(2,1)}), bf16[32,12,2048]{2,1,0:T(8,128)(2,1)}, u32[]{:S(2)}, u32[]{:S(2)}) async-start(bf16[32,12,2048]{2,1,0:T(8,128)(2,1)} %reshape.192), calls=%async_computation | async-start | bytes 4194304 | tf_op jit(solution)/shard_map/all_to_all | solution.py:114
  32.8 1.2 copy-start.2
  32.8 1.4 copy-start.3
  32.8 277.9 %all-gather.8.cloned.1.call-start = ((), (), s32[]{:S(2)}) async-start(), calls=%async_computation.4 | async-start | bytes 1671168 | tf_op jit(solution)/shard_map/all_gather | solution.py:124
  319.6 241.9 %all-to-all-start.1 = ((bf16[32,12,2048]{2,1,0:T(8,128)(2,1)}), bf16[32,12,2048]{2,1,0:T(8,128)(2,1)}, u32[]{:S(2)}, u32[]{:S(2)}) async-start(bf16[32,12,2048]{2,1,0:T(8,128)(2,1)} %reshape.194), calls=%async_computation.1 | async-start | bytes 4194304 | tf_op jit(solution)/shard_map/all_to_all | solution.py:128
  326.1 7.2 %collective-permute-start = (bf16[2,128,128]{2,1,0:T(8,128)(2,1)S(1)}, bf16[2,128,128]{2,1,0:T(8,128)(2,1)S(1)}, u32[]{:S(2)}, u32[]{:S(2)}) collective-permute-start(bf16[2,128,128]{2,1,0:T(8,128)(2,1)S(1)} %get-tuple-element.508), channel_id=1, source_target_pairs={{0,32},{32,64},{64,96},{96,128},{128,160},{160,192},{192,224},{224... | collective-permute-start | bytes 196616 | tf_op jit(solution)/shard_map/while/body/eval_jaxpr/ppermute | solution.py:18
  330.8 6.2 %collective-permute-start.1 = (bf16[2,128,128]{2,1,0:T(8,128)(2,1)S(1)}, bf16[2,128,128]{2,1,0:T(8,128)(2,1)S(1)}, u32[]{:S(2)}, u32[]{:S(2)}) collective-permute-start(bf16[2,128,128]{2,1,0:T(8,128)(2,1)S(1)} %get-tuple-element.509), channel_id=1, source_target_pairs={{0,32},{32,64},{64,96},{96,128},{128,160},{160,192},{192,224},{224... | collective-permute-start | bytes 196616 | tf_op jit(solution)/shard_map/while/body/eval_jaxpr/ppermute | solution.py:18
  338.6 12.2 %collective-permute-start = (bf16[2,128,128]{2,1,0:T(8,128)(2,1)S(1)}, bf16[2,128,128]{2,1,0:T(8,128)(2,1)S(1)}, u32[]{:S(2)}, u32[]{:S(2)}) collective-permute-start(bf16[2,128,128]{2,1,0:T(8,128)(2,1)S(1)} %get-tuple-element.508), channel_id=1, source_target_pairs={{0,32},{32,64},{64,96},{96,128},{128,160},{160,192},{192,224},{224... | collective-permute-start | bytes 196616 | tf_op jit(solution)/shard_map/while/body/eval_jaxpr/ppermute | solution.py:18
  348.8 6.2 %collective-permute-start.1 = (bf16[2,128,128]{2,1,0:T(8,128)(2,1)S(1)}, bf16[2,128,128]{2,1,0:T(8,128)(2,1)S(1)}, u32[]{:S(2)}, u32[]{:S(2)}) collective-permute-start(bf16[2,128,128]{2,1,0:T(8,128)(2,1)S(1)} %get-tuple-element.509), channel_id=1, source_target_pairs={{0,32},{32,64},{64,96},{96,128},{128,160},{160,192},{192,224},{224... | collective-permute-start | bytes 196616 | tf_op jit(solution)/shard_map/while/body/eval_jaxpr/ppermute | solution.py:18
  356.7 10.7 %collective-permute-start = (bf16[2,128,128]{2,1,0:T(8,128)(2,1)S(1)}, bf16[2,128,128]{2,1,0:T(8,128)(2,1)S(1)}, u32[]{:S(2)}, u32[]{:S(2)}) collective-permute-start(bf16[2,128,128]{2,1,0:T(8,128)(2,1)S(1)} %get-tuple-element.508), channel_id=1, source_target_pairs={{0,32},{32,64},{64,96},{96,128},{128,160},{160,192},{192,224},{224... | collective-permute-start | bytes 196616 | tf_op jit(solution)/shard_map/while/body/eval_jaxpr/ppermute | solution.py:18
  365.4 6.2 %collective-permute-start.1 = (bf16[2,128,128]{2,1,0:T(8,128)(2,1)S(1)}, bf16[2,128,128]{2,1,0:T(8,128)(2,1)S(1)}, u32[]{:S(2)}, u32[]{:S(2)}) collective-permute-start(bf16[2,128,128]{2,1,0:T(8,128)(2,1)S(1)} %get-tuple-element.509), channel_id=1, source_target_pairs={{0,32},{32,64},{64,96},{96,128},{128,160},{160,192},{192,224},{224... | collective-permute-start | bytes 196616 | tf_op jit(solution)/shard_map/while/body/eval_jaxpr/ppermute | solution.py:18
  373.3 10.7 %collective-permute-start = (bf16[2,128,128]{2,1,0:T(8,128)(2,1)S(1)}, bf16[2,128,128]{2,1,0:T(8,128)(2,1)S(1)}, u32[]{:S(2)}, u32[]{:S(2)}) collective-permute-start(bf16[2,128,128]{2,1,0:T(8,128)(2,1)S(1)} %get-tuple-element.508), channel_id=1, source_target_pairs={{0,32},{32,64},{64,96},{96,128},{128,160},{160,192},{192,224},{224... | collective-permute-start | bytes 196616 | tf_op jit(solution)/shard_map/while/body/eval_jaxpr/ppermute | solution.py:18
  382.0 6.2 %collective-permute-start.1 = (bf16[2,128,128]{2,1,0:T(8,128)(2,1)S(1)}, bf16[2,128,128]{2,1,0:T(8,128)(2,1)S(1)}, u32[]{:S(2)}, u32[]{:S(2)}) collective-permute-start(bf16[2,128,128]{2,1,0:T(8,128)(2,1)S(1)} %get-tuple-element.509), channel_id=1, source_target_pairs={{0,32},{32,64},{64,96},{96,128},{128,160},{160,192},{192,224},{224... | collective-permute-start | bytes 196616 | tf_op jit(solution)/shard_map/while/body/eval_jaxpr/ppermute | solution.py:18
  389.9 10.2 %collective-permute-start = (bf16[2,128,128]{2,1,0:T(8,128)(2,1)S(1)}, bf16[2,128,128]{2,1,0:T(8,128)(2,1)S(1)}, u32[]{:S(2)}, u32[]{:S(2)}) collective-permute-start(bf16[2,128,128]{2,1,0:T(8,128)(2,1)S(1)} %get-tuple-element.508), channel_id=1, source_target_pairs={{0,32},{32,64},{64,96},{96,128},{128,160},{160,192},{192,224},{224... | collective-permute-start | bytes 196616 | tf_op jit(solution)/shard_map/while/body/eval_jaxpr/ppermute | solution.py:18
  398.1 6.2 %collective-permute-start.1 = (bf16[2,128,128]{2,1,0:T(8,128)(2,1)S(1)}, bf16[2,128,128]{2,1,0:T(8,128)(2,1)S(1)}, u32[]{:S(2)}, u32[]{:S(2)}) collective-permute-start(bf16[2,128,128]{2,1,0:T(8,128)(2,1)S(1)} %get-tuple-element.509), channel_id=1, source_target_pairs={{0,32},{32,64},{64,96},{96,128},{128,160},{160,192},{192,224},{224... | collective-permute-start | bytes 196616 | tf_op jit(solution)/shard_map/while/body/eval_jaxpr/ppermute | solution.py:18
  405.9 10.2 %collective-permute-start = (bf16[2,128,128]{2,1,0:T(8,128)(2,1)S(1)}, bf16[2,128,128]{2,1,0:T(8,128)(2,1)S(1)}, u32[]{:S(2)}, u32[]{:S(2)}) collective-permute-start(bf16[2,128,128]{2,1,0:T(8,128)(2,1)S(1)} %get-tuple-element.508), channel_id=1, source_target_pairs={{0,32},{32,64},{64,96},{96,128},{128,160},{160,192},{192,224},{224... | collective-permute-start | bytes 196616 | tf_op jit(solution)/shard_map/while/body/eval_jaxpr/ppermute | solution.py:18
  414.1 6.8 %collective-permute-start.1 = (bf16[2,128,128]{2,1,0:T(8,128)(2,1)S(1)}, bf16[2,128,128]{2,1,0:T(8,128)(2,1)S(1)}, u32[]{:S(2)}, u32[]{:S(2)}) collective-permute-start(bf16[2,128,128]{2,1,0:T(8,128)(2,1)S(1)} %get-tuple-element.509), channel_id=1, source_target_pairs={{0,32},{32,64},{64,96},{96,128},{128,160},{160,192},{192,224},{224... | collective-permute-start | bytes 196616 | tf_op jit(solution)/shard_map/while/body/eval_jaxpr/ppermute | solution.py:18
  422.6 9.6 %collective-permute-start = (bf16[2,128,128]{2,1,0:T(8,128)(2,1)S(1)}, bf16[2,128,128]{2,1,0:T(8,128)(2,1)S(1)}, u32[]{:S(2)}, u32[]{:S(2)}) collective-permute-start(bf16[2,128,128]{2,1,0:T(8,128)(2,1)S(1)} %get-tuple-element.508), channel_id=1, source_target_pairs={{0,32},{32,64},{64,96},{96,128},{128,160},{160,192},{192,224},{224... | collective-permute-start | bytes 196616 | tf_op jit(solution)/shard_map/while/body/eval_jaxpr/ppermute | solution.py:18
  430.2 6.4 %collective-permute-start.1 = (bf16[2,128,128]{2,1,0:T(8,128)(2,1)S(1)}, bf16[2,128,128]{2,1,0:T(8,128)(2,1)S(1)}, u32[]{:S(2)}, u32[]{:S(2)}) collective-permute-start(bf16[2,128,128]{2,1,0:T(8,128)(2,1)S(1)} %get-tuple-element.509), channel_id=1, source_target_pairs={{0,32},{32,64},{64,96},{96,128},{128,160},{160,192},{192,224},{224... | collective-permute-start | bytes 196616 | tf_op jit(solution)/shard_map/while/body/eval_jaxpr/ppermute | solution.py:18
  438.3 9.9 %collective-permute-start = (bf16[2,128,128]{2,1,0:T(8,128)(2,1)S(1)}, bf16[2,128,128]{2,1,0:T(8,128)(2,1)S(1)}, u32[]{:S(2)}, u32[]{:S(2)}) collective-permute-start(bf16[2,128,128]{2,1,0:T(8,128)(2,1)S(1)} %get-tuple-element.508), channel_id=1, source_target_pairs={{0,32},{32,64},{64,96},{96,128},{128,160},{160,192},{192,224},{224... | collective-permute-start | bytes 196616 | tf_op jit(solution)/shard_map/while/body/eval_jaxpr/ppermute | solution.py:18
  446.3 6.2 %collective-permute-start.1 = (bf16[2,128,128]{2,1,0:T(8,128)(2,1)S(1)}, bf16[2,128,128]{2,1,0:T(8,128)(2,1)S(1)}, u32[]{:S(2)}, u32[]{:S(2)}) collective-permute-start(bf16[2,128,128]{2,1,0:T(8,128)(2,1)S(1)} %get-tuple-element.509), channel_id=1, source_target_pairs={{0,32},{32,64},{64,96},{96,128},{128,160},{160,192},{192,224},{224... | collective-permute-start | bytes 196616 | tf_op jit(solution)/shard_map/while/body/eval_jaxpr/ppermute | solution.py:18
  452.5 11.8 %collective-permute-start = (bf16[2,128,128]{2,1,0:T(8,128)(2,1)S(1)}, bf16[2,128,128]{2,1,0:T(8,128)(2,1)S(1)}, u32[]{:S(2)}, u32[]{:S(2)}) collective-permute-start(bf16[2,128,128]{2,1,0:T(8,128)(2,1)S(1)} %get-tuple-element.508), channel_id=1, source_target_pairs={{0,32},{32,64},{64,96},{96,128},{128,160},{160,192},{192,224},{224... | collective-permute-start | bytes 196616 | tf_op jit(solution)/shard_map/while/body/eval_jaxpr/ppermute | solution.py:18
  462.3 6.2 %collective-permute-start.1 = (bf16[2,128,128]{2,1,0:T(8,128)(2,1)S(1)}, bf16[2,128,128]{2,1,0:T(8,128)(2,1)S(1)}, u32[]{:S(2)}, u32[]{:S(2)}) collective-permute-start(bf16[2,128,128]{2,1,0:T(8,128)(2,1)S(1)} %get-tuple-element.509), channel_id=1, source_target_pairs={{0,32},{32,64},{64,96},{96,128},{128,160},{160,192},{192,224},{224... | collective-permute-start | bytes 196616 | tf_op jit(solution)/shard_map/while/body/eval_jaxpr/ppermute | solution.py:18
  468.5 10.2 %collective-permute-start = (bf16[2,128,128]{2,1,0:T(8,128)(2,1)S(1)}, bf16[2,128,128]{2,1,0:T(8,128)(2,1)S(1)}, u32[]{:S(2)}, u32[]{:S(2)}) collective-permute-start(bf16[2,128,128]{2,1,0:T(8,128)(2,1)S(1)} %get-tuple-element.508), channel_id=1, source_target_pairs={{0,32},{32,64},{64,96},{96,128},{128,160},{160,192},{192,224},{224... | collective-permute-start | bytes 196616 | tf_op jit(solution)/shard_map/while/body/eval_jaxpr/ppermute | solution.py:18
  476.7 6.2 %collective-permute-start.1 = (bf16[2,128,128]{2,1,0:T(8,128)(2,1)S(1)}, bf16[2,128,128]{2,1,0:T(8,128)(2,1)S(1)}, u32[]{:S(2)}, u32[]{:S(2)}) collective-permute-start(bf16[2,128,128]{2,1,0:T(8,128)(2,1)S(1)} %get-tuple-element.509), channel_id=1, source_target_pairs={{0,32},{32,64},{64,96},{96,128},{128,160},{160,192},{192,224},{224... | collective-permute-start | bytes 196616 | tf_op jit(solution)/shard_map/while/body/eval_jaxpr/ppermute | solution.py:18
  482.9 11.0 %collective-permute-start = (bf16[2,128,128]{2,1,0:T(8,128)(2,1)S(1)}, bf16[2,128,128]{2,1,0:T(8,128)(2,1)S(1)}, u32[]{:S(2)}, u32[]{:S(2)}) collective-permute-start(bf16[2,128,128]{2,1,0:T(8,128)(2,1)S(1)} %get-tuple-element.508), channel_id=1, source_target_pairs={{0,32},{32,64},{64,96},{96,128},{128,160},{160,192},{192,224},{224... | collective-permute-start | bytes 196616 | tf_op jit(solution)/shard_map/while/body/eval_jaxpr/ppermute | solution.py:18
  492.0 6.4 %collective-permute-start.1 = (bf16[2,128,128]{2,1,0:T(8,128)(2,1)S(1)}, bf16[2,128,128]{2,1,0:T(8,128)(2,1)S(1)}, u32[]{:S(2)}, u32[]{:S(2)}) collective-permute-start(bf16[2,128,128]{2,1,0:T(8,128)(2,1)S(1)} %get-tuple-element.509), channel_id=1, source_target_pairs={{0,32},{32,64},{64,96},{96,128},{128,160},{160,192},{192,224},{224... | collective-permute-start | bytes 196616 | tf_op jit(solution)/shard_map/while/body/eval_jaxpr/ppermute | solution.py:18
  498.4 11.3 %collective-permute-start = (bf16[2,128,128]{2,1,0:T(8,128)(2,1)S(1)}, bf16[2,128,128]{2,1,0:T(8,128)(2,1)S(1)}, u32[]{:S(2)}, u32[]{:S(2)}) collective-permute-start(bf16[2,128,128]{2,1,0:T(8,128)(2,1)S(1)} %get-tuple-element.508), channel_id=1, source_target_pairs={{0,32},{32,64},{64,96},{96,128},{128,160},{160,192},{192,224},{224... | collective-permute-start | bytes 196616 | tf_op jit(solution)/shard_map/while/body/eval_jaxpr/ppermute | solution.py:18
  507.4 6.4 %collective-permute-start.1 = (bf16[2,128,128]{2,1,0:T(8,128)(2,1)S(1)}, bf16[2,128,128]{2,1,0:T(8,128)(2,1)S(1)}, u32[]{:S(2)}, u32[]{:S(2)}) collective-permute-start(bf16[2,128,128]{2,1,0:T(8,128)(2,1)S(1)} %get-tuple-element.509), channel_id=1, source_target_pairs={{0,32},{32,64},{64,96},{96,128},{128,160},{160,192},{192,224},{224... | collective-permute-start | bytes 196616 | tf_op jit(solution)/shard_map/while/body/eval_jaxpr/ppermute | solution.py:18
  513.9 11.5 %collective-permute-start = (bf16[2,128,128]{2,1,0:T(8,128)(2,1)S(1)}, bf16[2,128,128]{2,1,0:T(8,128)(2,1)S(1)}, u32[]{:S(2)}, u32[]{:S(2)}) collective-permute-start(bf16[2,128,128]{2,1,0:T(8,128)(2,1)S(1)} %get-tuple-element.508), channel_id=1, source_target_pairs={{0,32},{32,64},{64,96},{96,128},{128,160},{160,192},{192,224},{224... | collective-permute-start | bytes 196616 | tf_op jit(solution)/shard_map/while/body/eval_jaxpr/ppermute | solution.py:18
  523.5 6.2 %collective-permute-start.1 = (bf16[2,128,128]{2,1,0:T(8,128)(2,1)S(1)}, bf16[2,128,128]{2,1,0:T(8,128)(2,1)S(1)}, u32[]{:S(2)}, u32[]{:S(2)}) collective-permute-start(bf16[2,128,128]{2,1,0:T(8,128)(2,1)S(1)} %get-tuple-element.509), channel_id=1, source_target_pairs={{0,32},{32,64},{64,96},{96,128},{128,160},{160,192},{192,224},{224... | collective-permute-start | bytes 196616 | tf_op jit(solution)/shard_map/while/body/eval_jaxpr/ppermute | solution.py:18
  529.7 11.2 %collective-permute-start = (bf16[2,128,128]{2,1,0:T(8,128)(2,1)S(1)}, bf16[2,128,128]{2,1,0:T(8,128)(2,1)S(1)}, u32[]{:S(2)}, u32[]{:S(2)}) collective-permute-start(bf16[2,128,128]{2,1,0:T(8,128)(2,1)S(1)} %get-tuple-element.508), channel_id=1, source_target_pairs={{0,32},{32,64},{64,96},{96,128},{128,160},{160,192},{192,224},{224... | collective-permute-start | bytes 196616 | tf_op jit(solution)/shard_map/while/body/eval_jaxpr/ppermute | solution.py:18
  538.5 6.2 %collective-permute-start.1 = (bf16[2,128,128]{2,1,0:T(8,128)(2,1)S(1)}, bf16[2,128,128]{2,1,0:T(8,128)(2,1)S(1)}, u32[]{:S(2)}, u32[]{:S(2)}) collective-permute-start(bf16[2,128,128]{2,1,0:T(8,128)(2,1)S(1)} %get-tuple-element.509), channel_id=1, source_target_pairs={{0,32},{32,64},{64,96},{96,128},{128,160},{160,192},{192,224},{224... | collective-permute-start | bytes 196616 | tf_op jit(solution)/shard_map/while/body/eval_jaxpr/ppermute | solution.py:18
  544.7 10.5 %collective-permute-start = (bf16[2,128,128]{2,1,0:T(8,128)(2,1)S(1)}, bf16[2,128,128]{2,1,0:T(8,128)(2,1)S(1)}, u32[]{:S(2)}, u32[]{:S(2)}) collective-permute-start(bf16[2,128,128]{2,1,0:T(8,128)(2,1)S(1)} %get-tuple-element.508), channel_id=1, source_target_pairs={{0,32},{32,64},{64,96},{96,128},{128,160},{160,192},{192,224},{224... | collective-permute-start | bytes 196616 | tf_op jit(solution)/shard_map/while/body/eval_jaxpr/ppermute | solution.py:18
  553.2 6.2 %collective-permute-start.1 = (bf16[2,128,128]{2,1,0:T(8,128)(2,1)S(1)}, bf16[2,128,128]{2,1,0:T(8,128)(2,1)S(1)}, u32[]{:S(2)}, u32[]{:S(2)}) collective-permute-start(bf16[2,128,128]{2,1,0:T(8,128)(2,1)S(1)} %get-tuple-element.509), channel_id=1, source_target_pairs={{0,32},{32,64},{64,96},{96,128},{128,160},{160,192},{192,224},{224... | collective-permute-start | bytes 196616 | tf_op jit(solution)/shard_map/while/body/eval_jaxpr/ppermute | solution.py:18
Sparse Core Ops, SparseCore 0:
  11.2 95.8 all-gather.3
  110.3 103.0 all-gather.5
  216.4 94.1 all-gather.7
where the time goes:
time: 574 us; the launch traced here: 572 us
  waiting for transfers between devices  335 us (58%)
  starting transfers between devices  173 us (30%)
  matrix products  20.2 us (4%)
  local copies, waits for them, and re-layouts  15.1 us (3%)
  between operations  14.1 us (2%)
  other arithmetic  14 us (2%)
    ppermute x30, starting transfers between devices, passed_along(): return lax.ppermute(block, axis, route)  157 us
    all_gather x1, waiting for transfers between devices, shards(): up_piece = lax.all_gather(w_up, 'ctx', axis=1, tiled=True)  103 us
    all_gather x1, waiting for transfers between devices, shards(): lax.all_gather(w_down, 'ctx', axis=2, tiled=True)[0]  97.3 us
    all_to_all x1, waiting for transfers between devices, shards(): lax.all_to_all(outgoing.reshape(owners, CAP, width), 'dp', split_axis=0,...  64.5 us
    ppermute x30, waiting for transfers between devices, passed_along(): return lax.ppermute(block, axis, route)  63.6 us
  transfers between devices with their start and end apart: 35, of which 21 were waited for; matrix products, arithmetic and copies ran while one was open for 6% of the time, Pallas kernels for 0%

commit v1 on v0

v1 whole, which is shorter than its diff:
```python
import functools
import math

import jax
import jax.numpy as jnp
from jax import lax
from jax.experimental import pallas as pl
from jax.experimental.pallas import tpu as pltpu
from jax.sharding import Mesh, PartitionSpec as P

HD = 128
CAP = 12
LOW = 8
FOLD = CAP - LOW
CTX = ("zh", "y")
DP = ("zl", "x", "c")
MASKED = -1e30
F32 = jnp.float32
BF16 = jnp.bfloat16
VMEM = pl.BlockSpec(memory_space=pltpu.VMEM)


def natural_block(place, halves, ring):
    return (place % halves) * ring + place // halves


def dispatch_kernel(halves, ring, owners, x_ref, gain_ref, ids_ref, gates_ref, out_ref, mix_a_ref, mix_b_ref):
    tokens, width = x_ref.shape
    slots = owners * LOW
    half = width // 2
    x = x_ref[...].astype(F32)
    normed = (x * lax.rsqrt(jnp.mean(x * x, axis=-1, keepdims=True) + 1e-06) * gain_ref[...]).astype(BF16)
    step = width // (halves * ring)
    pieces = []
    for place in range(halves * ring):
        start = natural_block(place, halves, ring) * step
        pieces.append(normed[:, start : start + step])
    normed = jnp.concatenate(pieces, axis=1)

    lane = lax.broadcasted_iota(jnp.int32, (tokens, slots), 1)
    expert = lane // LOW
    place = lane % LOW
    ids = ids_ref[...]
    gates = gates_ref[...]
    hot = jnp.zeros((tokens, slots), F32)
    gate = jnp.zeros((tokens, slots), F32)
    for k in range(ids.shape[1]):
        hit = ids[:, k : k + 1] == expert
        hot = jnp.where(hit, 1.0, hot)
        gate = jnp.where(hit, gates[:, k : k + 1], gate)
    row = lax.broadcasted_iota(jnp.int32, (tokens, tokens), 0)
    col = lax.broadcasted_iota(jnp.int32, (tokens, tokens), 1)
    earlier = jnp.where(col < row, 1.0, 0.0).astype(BF16)
    rank = jnp.dot(earlier, hot.astype(BF16), preferred_element_type=F32)
    rank = jnp.where(hot > 0.5, rank, -1.0)
    in_a = rank == place.astype(F32)
    in_b = rank == (LOW + place % FOLD).astype(F32)
    in_lo = in_b & (place < FOLD)
    in_hi = in_b & (place >= FOLD)

    def put(chosen):
        return jnp.where(chosen, 1.0, 0.0).astype(BF16)

    contract = (((0,), (0,)), ((), ()))
    out_ref[:, :width] = lax.dot_general(put(in_a), normed, contract, preferred_element_type=F32).astype(BF16)
    pick = jnp.concatenate([put(in_lo), put(in_hi)], axis=0)
    stacked = jnp.concatenate([normed[:, :half], normed[:, half:]], axis=0)
    out_ref[:, width:] = lax.dot_general(pick, stacked, contract, preferred_element_type=F32).astype(BF16)

    top = gate.astype(BF16).astype(F32)
    rest = gate - top

    def mix(chosen):
        return jnp.concatenate(
            [jnp.where(chosen, top, 0.0).astype(BF16), jnp.where(chosen, rest, 0.0).astype(BF16)], axis=0
        )

    mix_a_ref[...] = mix(in_a)
    mix_b_ref[:, :slots] = mix(in_lo)
    mix_b_ref[:, slots:] = mix(in_hi)


def expert_kernel(hidden_units, x_ref, w_ref, out_ref):
    rows, cols = x_ref.shape
    width = w_ref.shape[0] * w_ref.shape[1]
    half = width // 2
    both = 2 * hidden_units
    block = w_ref.shape[1]
    count = w_ref.shape[0]

    def part(lo, hi):
        return w_ref[lo:hi, :, :both].reshape((hi - lo) * block, both)

    low_w = part(0, count // 2)
    high_w = part(count // 2, count)
    sums_a = jnp.dot(x_ref[:, :half], low_w, preferred_element_type=F32)
    sums_a = sums_a + jnp.dot(x_ref[:, half:width], high_w, preferred_element_type=F32)
    folded = x_ref[:, width:]
    first = lax.broadcasted_iota(jnp.int32, (rows, both), 0) % LOW < FOLD
    sums_b = jnp.where(
        first,
        jnp.dot(folded, low_w, preferred_element_type=F32),
        jnp.dot(folded, high_w, preferred_element_type=F32),
    )
    groups = sums_b.reshape(rows // LOW, LOW, both)
    sums_b = (groups + pltpu.roll(groups, FOLD, 1)).reshape(rows, both)

    def activate(sums):
        gate = sums[:, :hidden_units]
        return (gate / (1.0 + jnp.exp(-gate)) * sums[:, hidden_units:]).astype(BF16)

    hidden_a = activate(sums_a)
    hidden_b = activate(sums_b)

    def down(place):
        pieces = [w_ref[place, :, both + j * block : both + (j + 1) * block] for j in range(hidden_units // block)]
        return jnp.concatenate(pieces, axis=0)

    first_out = lax.broadcasted_iota(jnp.int32, (rows, 2 * block), 0) % LOW < FOLD
    for pair in range(count // 4):
        lo, hi = 2 * pair, count // 2 + 2 * pair
        low_d = jnp.concatenate([down(lo), down(lo + 1)], axis=1)
        high_d = jnp.concatenate([down(hi), down(hi + 1)], axis=1)
        out_ref[:, lo * block : (lo + 2) * block] = jnp.dot(
            hidden_a, low_d, preferred_element_type=F32
        ).astype(BF16)
        out_ref[:, hi * block : (hi + 2) * block] = jnp.dot(
            hidden_a, high_d, preferred_element_type=F32
        ).astype(BF16)
        out_ref[:, width + lo * block : width + (lo + 2) * block] = jnp.where(
            first_out,
            jnp.dot(hidden_b, low_d, preferred_element_type=F32),
            jnp.dot(hidden_b, high_d, preferred_element_type=F32),
        ).astype(BF16)


def combine_kernel(halves, ring, back_ref, mix_a_ref, mix_b_ref, out_ref):
    tokens, width = out_ref.shape
    half = width // 2
    slots = back_ref.shape[0]
    step = width // (halves * ring)
    folded = back_ref[:, width:]
    for side in range(2):
        both = jnp.dot(
            mix_a_ref[...], back_ref[:, side * half : (side + 1) * half], preferred_element_type=F32
        ) + jnp.dot(
            mix_b_ref[:, side * slots : (side + 1) * slots], folded, preferred_element_type=F32
        )
        total = (both[:tokens] + both[tokens:]).astype(BF16)
        for i in range(half // step):
            start = natural_block(side * (half // step) + i, halves, ring) * step
            out_ref[:, start : start + step] = total[:, i * step : (i + 1) * step]


def attend_kernel(halves, ring, heads_kv, q_ref, kv_ref, place_ref, out_ref):
    tokens, wide = q_ref.shape
    heads = wide // HD
    group = heads // heads_kv
    blocks = kv_ref.shape[0]
    keys = blocks * kv_ref.shape[1]
    scale = 1.0 / math.sqrt(HD)
    lane = lax.broadcasted_iota(jnp.int32, (tokens, keys), 1)
    row = lax.broadcasted_iota(jnp.int32, (tokens, keys), 0)
    block = lane // tokens
    key_pos = ((block % halves) * ring + block // halves) * tokens + lane % tokens
    allowed = key_pos <= row + place_ref[0] * tokens
    for g in range(heads_kv):
        key = kv_ref[:, :, g * HD : (g + 1) * HD].reshape(keys, HD)
        value = kv_ref[:, :, (heads_kv + g) * HD : (heads_kv + g + 1) * HD].reshape(keys, HD)

        @pl.loop(0, group)
        def _(i):
            at = pl.ds(pl.multiple_of((g * group + i) * HD, HD), HD)
            scores = lax.dot_general(
                q_ref[:, at], key, (((1,), (1,)), ((), ())), preferred_element_type=F32
            )
            scores = jnp.where(allowed, scores * scale, MASKED)
            largest = jnp.max(scores, axis=-1, keepdims=True)
            probs = jnp.exp(scores - largest)
            total = jnp.sum(probs, axis=-1, keepdims=True)
            mixed = jnp.dot(probs.astype(BF16), value, preferred_element_type=F32)
            out_ref[:, at] = (mixed / total).astype(BF16)


def estimate(flops, bytes_accessed, transcendentals=0):
    return pl.CostEstimate(flops=flops, bytes_accessed=bytes_accessed, transcendentals=transcendentals)


def shards(
    queries, key_rows, value_rows, stream, norm_gain, expert_ids, gate_values, w_gate, w_up, w_down
):
    tokens, width = stream.shape[1:]
    heads_kv = key_rows.shape[2] // HD
    hidden_units = w_gate.shape[2]
    halves, ring = lax.axis_size("zh"), lax.axis_size("y")
    owners = lax.axis_size(DP)
    slots = owners * LOW
    wide = width + width // 2
    params = pltpu.CompilerParams(vmem_limit_bytes=48 * 1024 * 1024)

    with jax.named_scope("weights"):
        down = w_down[0]
        pieces = [down[j * tokens : (j + 1) * tokens] for j in range(hidden_units // tokens)]
        packed = jnp.concatenate([w_gate[0], w_up[0]] + pieces, axis=1)
        pair = lax.all_gather(packed, "zh", axis=0)
        weights = lax.all_gather(pair, "y", axis=0, tiled=True)

    with jax.named_scope("dispatch"):
        ids, pair = lax.optimization_barrier((expert_ids[0], pair))
        outgoing, mix_a, mix_b = pl.pallas_call(
            functools.partial(dispatch_kernel, halves, ring, owners),
            out_shape=(
                jax.ShapeDtypeStruct((slots, wide), BF16),
                jax.ShapeDtypeStruct((2 * tokens, slots), BF16),
                jax.ShapeDtypeStruct((2 * tokens, 2 * slots), BF16),
            ),
            in_specs=[VMEM] * 4,
            out_specs=(VMEM,) * 3,
            compiler_params=params,
            cost_estimate=estimate(4 * 256 * 256 * 2048, 4 * 1024 * 1024),
            name="dispatch",
        )(stream[0], norm_gain[None, :], ids, gate_values[0])
        arrived = lax.all_to_all(
            outgoing.reshape(owners, LOW, wide), DP, split_axis=0, concat_axis=0, tiled=True
        ).reshape(slots, wide)

    with jax.named_scope("keys"):
        kv = jnp.concatenate([key_rows[0], value_rows[0]], axis=1)
        kv, outgoing = lax.optimization_barrier((kv, outgoing))
        kv_pair = lax.all_gather(kv, "zh", axis=0)
        kv_all = lax.all_gather(kv_pair, "y", axis=0, tiled=True)

    with jax.named_scope("experts"):
        answers = pl.pallas_call(
            functools.partial(expert_kernel, hidden_units),
            out_shape=jax.ShapeDtypeStruct((slots, wide), BF16),
            in_specs=[VMEM] * 2,
            out_specs=VMEM,
            compiler_params=params,
            cost_estimate=estimate(6 * 512 * 2048 * 384, 8 * 1024 * 1024),
            name="experts",
        )(arrived, weights)
        returned = lax.all_to_all(
            answers.reshape(owners, LOW, wide), DP, split_axis=0, concat_axis=0, tiled=True
        ).reshape(slots, wide)

    with jax.named_scope("attend"):
        place = lax.axis_index(CTX).astype(jnp.int32)[None]
        attended = pl.pallas_call(
            functools.partial(attend_kernel, halves, ring, heads_kv),
            out_shape=jax.ShapeDtypeStruct(queries.shape[1:], BF16),
            in_specs=[VMEM, VMEM, pl.BlockSpec(memory_space=pltpu.SMEM)],
            out_specs=VMEM,
            compiler_params=params,
            cost_estimate=estimate(4 * 2048 * 128 * 2048, 4 * 1024 * 1024, 16 * 128 * 2048),
            name="attend",
        )(queries[0], kv_all, place)

    with jax.named_scope("combine"):
        expert_out = pl.pallas_call(
            functools.partial(combine_kernel, halves, ring),
            out_shape=jax.ShapeDtypeStruct((tokens, width), BF16),
            in_specs=[VMEM] * 3,
            out_specs=VMEM,
            compiler_params=params,
            cost_estimate=estimate(2 * 256 * 512 * 2048, 3 * 1024 * 1024),
            name="combine",
        )(returned, mix_a, mix_b)
    return (attended[None], expert_out[None])


def solution(mesh):
    fine = Mesh(mesh.devices.reshape(2, 8, 4, 4, 2), CTX + DP)
    rows = P(DP, CTX, None)
    return jax.shard_map(
        shards,
        mesh=fine,
        in_specs=(rows, rows, rows, rows, P(), rows, rows, rows, rows, P(DP, None, CTX)),
        out_specs=(rows, rows),
        check_vma=False,
    )
```

time: 574 us -> 167 us (0.29)
  the two profiles are of different devices: /device:TPU:62 before, /device:TPU:6 now
where the time goes in v1:
time: 167 us; the launch traced here: 166 us
  blocking collectives  54.4 us (33%)
  waiting for transfers between devices  46.5 us (28%)
  Pallas kernels  23.6 us (14%)
  starting transfers between devices  21.6 us (13%)
  between operations  14.1 us (8%)
  local copies, waits for them, and re-layouts  6 us (4%)
    all_gather x1, blocking collectives, shards(): kv_pair = lax.all_gather(kv, 'zh', axis=0)  37.5 us
    all_gather x1, waiting for transfers between devices, shards(): kv_all = lax.all_gather(kv_pair, 'y', axis=0, tiled=True)  30.2 us
    all_gather x1, blocking collectives, shards(): pair = lax.all_gather(packed, 'zh', axis=0)  16.9 us
    pallas_call x1, Pallas kernels, shards(): pl.pallas_call(functools.partial(attend_kernel, halves, ring, heads_kv),...  13.4 us
    all_to_all x1, starting transfers between devices, shards(): lax.all_to_all(outgoing.reshape(owners, LOW, wide), DP, split_axis=0, con...  13.1 us
    all_gather x1, waiting for transfers between devices, shards(): weights = lax.all_gather(pair, 'y', axis=0, tiled=True)  11.1 us
    all_to_all x1, starting transfers between devices, shards(): lax.all_to_all(answers.reshape(owners, LOW, wide), DP, split_axis=0, conc...  8.33 us
    pallas_call x1, Pallas kernels, shards(): pl.pallas_call(functools.partial(expert_kernel, hidden_units), out_shape=...  6.43 us
  transfers between devices with their start and end apart: 4, of which 3 were waited for; matrix products, arithmetic and copies ran while one was open for 0% of the time, Pallas kernels for 13%

profile of v1, /device:TPU:6, one launch (start us, length us, event | category | flops | bytes accessed | tf_op | source)
XLA Modules:
  0.0 166.2 jit_solution(18339383741783550580)
XLA Ops:
  7.2 0.0 copy-start.6
  7.2 0.0 copy-start.7
  7.2 0.0 copy-start.3
  7.2 0.0 copy-start.1
  7.2 0.0 all-gather.7.cloned.1.call-start
  7.3 1.0 bitcast_dynamic-update-slice_fusion.1
  8.2 0.9 bitcast_dynamic-update-slice_fusion
  9.1 0.8 bitcast_dynamic-update-slice_fusion.4
  9.9 0.8 bitcast_dynamic-update-slice_fusion.3
  10.7 0.8 bitcast_dynamic-update-slice_fusion.2
  11.4 16.9 %all-gather = bf16[256,1152]{1,0:T(8,128)(2,1)} all-gather(bf16[128,1152]{1,0:T(8,128)(2,1)S(1)} %bitcast_dynamic-update-slice_fusion.2), channel_id=2, replica_groups=mesh['zh'=2,'y'=8,'zl'=4,'x'=4,'c'=2] {'zh'}, dimensions={0}, use_global_device_ids=true | all-gather | bytes 884736 | tf_op jit(solution)/shard_map/weights/all_gather | solution.py:205
  28.3 0.0 all-gather.7.cloned.1.call-update
  28.4 0.0 copy-done.6
  28.4 0.1 copy.14
  28.5 0.0 copy-done.7
  28.5 0.1 copy.15
  28.6 0.0 copy-done.3
  28.6 0.0 copy-done.1
  28.6 2.3 %dispatch.1 = (bf16[256,3072]{1,0:T(8,128)(2,1)}, bf16[256,256]{1,0:T(8,128)(2,1)S(1)}, bf16[256,512]{1,0:T(8,128)(2,1)S(1)}) custom-call(bf16[128,2048]{1,0:T(8,128)(2,1)S(1)} %bitcast.30, f32[1,2048]{1,0:T(1,128)S(1)} %bitcast.32, s32[128,8]{1,0:T(8,128)S(1)} %bitcast.28, f32[128,8]{1,0:T(8,128)S(1)} %bitcast.29), custom_call_target="tpu_custom_call" | custom-call | flops 536870912 | bytes 4194304 | tf_op jit(solution)/shard_map/dispatch/dispatch/pallas_call | solution.py:210
  30.9 0.0 copy-start.4
  30.9 0.0 copy-start.5
  30.9 13.1 %all-to-all-start = ((bf16[32,8,3072]{2,1,0:T(8,128)(2,1)}), bf16[32,8,3072]{2,1,0:T(8,128)(2,1)S(1)}, u32[]{:S(2)}, u32[]{:S(2)}) async-start(bf16[32,8,3072]{2,1,0:T(8,128)(2,1)} %bitcast.16), calls=%async_computation | async-start | bytes 3145728 | tf_op jit(solution)/shard_map/dispatch/all_to_all | solution.py:223
  44.1 0.0 all-gather.5.cloned.1.call-start
  44.1 0.0 copy-done.4
  44.1 0.0 copy-done.5
  44.1 37.5 %all-gather.1 = bf16[256,512]{1,0:T(8,128)(2,1)} all-gather(bf16[128,512]{1,0:T(8,128)(2,1)S(1)} %pad_maximum_fusion), channel_id=3, replica_groups=mesh['zh'=2,'y'=8,'zl'=4,'x'=4,'c'=2] {'zh'}, dimensions={0}, use_global_device_ids=true | all-gather | bytes 393216 | tf_op jit(solution)/shard_map/keys/all_gather | solution.py:230
  81.6 0.0 all-gather.5.cloned.1.call-update
  81.6 5.3 %all-to-all-done = bf16[32,8,3072]{2,1,0:T(8,128)(2,1)S(1)} async-done(((bf16[32,8,3072]{2,1,0:T(8,128)(2,1)}), bf16[32,8,3072]{2,1,0:T(8,128)(2,1)S(1)}, u32[]{:S(2)}, u32[]{:S(2)}) %all-to-all-start) | async-done | bytes 1572896 | tf_op jit(solution)/shard_map/dispatch/all_to_all | solution.py:223
  86.9 11.1 %all-gather.7.cloned.1.call-done.w_ref = bf16[16,128,1152]{2,1,0:T(8,128)(2,1)} async-done(((bf16[2,128,1152]{2,1,0:T(8,128)(2,1)}), bf16[16,128,1152]{2,1,0:T(8,128)(2,1)}) %all-gather.7.cloned.1.call-update) | async-done | bytes 4718608 | tf_op jit(solution)/shard_map/weights/all_gather | solution.py:206
  98.0 6.4 %experts.1 = bf16[256,3072]{1,0:T(8,128)(2,1)} custom-call(bf16[256,3072]{1,0:T(8,128)(2,1)S(1)} %bitcast.27, bf16[16,128,1152]{2,1,0:T(8,128)(2,1)} %all-gather.7.cloned.1.call-done.w_ref), custom_call_target="tpu_custom_call" | custom-call | flops 2415919104 | bytes 8388608 | tf_op jit(solution)/shard_map/experts/experts/pallas_call | solution.py:234
  104.4 0.0 copy-start.2
  104.4 8.3 %all-to-all-start.1 = ((bf16[32,8,3072]{2,1,0:T(8,128)(2,1)}), bf16[32,8,3072]{2,1,0:T(8,128)(2,1)S(1)}, u32[]{:S(2)}, u32[]{:S(2)}) async-start(bf16[32,8,3072]{2,1,0:T(8,128)(2,1)} %bitcast.18), calls=%async_computation.1 | async-start | bytes 3145728 | tf_op jit(solution)/shard_map/experts/all_to_all | solution.py:243
  112.8 30.2 %all-gather.5.cloned.1.call-done.kv_ref = bf16[16,128,512]{2,1,0:T(8,128)(2,1)} async-done(((bf16[2,128,512]{2,1,0:T(8,128)(2,1)}), bf16[16,128,512]{2,1,0:T(8,128)(2,1)}) %all-gather.5.cloned.1.call-update) | async-done | bytes 2097168 | tf_op jit(solution)/shard_map/keys/all_gather | solution.py:231
  142.9 0.0 copy-done.2
  142.9 0.0 copy-start
  142.9 1.6 copy-done
  144.5 13.4 %attend.1 = bf16[128,2048]{1,0:T(8,128)(2,1)} custom-call(bf16[128,2048]{1,0:T(8,128)(2,1)S(1)} %bitcast.31, bf16[16,128,512]{2,1,0:T(8,128)(2,1)S(1)} %copy-done, s32[1]{0:T(128)} %bitcast.14.place_ref), custom_call_target="tpu_custom_call" | custom-call | flops 2147483648 | bytes 4194304 | tf_op jit(solution)/shard_map/attend/attend/pallas_call | solution.py:249
  157.9 0.0 all-to-all-done.1
  157.9 1.5 combine.1
  (1 shorter events, 0.0 us)
Async XLA Ops:
  7.2 21.2 %copy-start.6 = (s32[1,128,8]{1,2,0:T(8,128)S(1)}, s32[1,128,8]{1,2,0:T(8,128)}, u32[]{:S(2)}) copy-start(s32[1,128,8]{1,2,0:T(8,128)} %param.15) | copy-start | bytes 12292
  7.2 21.3 %copy-start.7 = (f32[1,128,8]{1,2,0:T(8,128)S(1)}, f32[1,128,8]{1,2,0:T(8,128)}, u32[]{:S(2)}) copy-start(f32[1,128,8]{1,2,0:T(8,128)} %param.16) | copy-start | bytes 12292
  7.2 21.4 %copy-start.3 = (f32[2048]{0:T(1024)S(1)}, f32[2048]{0:T(1024)}, u32[]{:S(2)}) copy-start(f32[2048]{0:T(1024)} %param.14) | copy-start | bytes 24580
  7.2 21.4 %copy-start.1 = (bf16[1,128,2048]{2,1,0:T(8,128)(2,1)S(1)}, bf16[1,128,2048]{2,1,0:T(8,128)(2,1)}, u32[]{:S(2)}) copy-start(bf16[1,128,2048]{2,1,0:T(8,128)(2,1)} %param.13) | copy-start | bytes 1572868
  7.2 90.8 %all-gather.7.cloned.1.call-start = ((), (), s32[]{:S(2)}) async-start(), calls=%async_computation.3 | async-start | bytes 5308416 | tf_op jit(solution)/shard_map/weights/all_gather | solution.py:206
  30.9 13.2 %copy-start.4 = (bf16[1,128,256]{2,1,0:T(8,128)(2,1)S(1)}, bf16[1,128,256]{2,1,0:T(8,128)(2,1)}, u32[]{:S(2)}) copy-start(bf16[1,128,256]{2,1,0:T(8,128)(2,1)} %param.12) | copy-start | bytes 196612
  30.9 13.2 %copy-start.5 = (bf16[1,128,256]{2,1,0:T(8,128)(2,1)S(1)}, bf16[1,128,256]{2,1,0:T(8,128)(2,1)}, u32[]{:S(2)}) copy-start(bf16[1,128,256]{2,1,0:T(8,128)(2,1)} %param.11) | copy-start | bytes 196612
  30.9 56.0 %all-to-all-start = ((bf16[32,8,3072]{2,1,0:T(8,128)(2,1)}), bf16[32,8,3072]{2,1,0:T(8,128)(2,1)S(1)}, u32[]{:S(2)}, u32[]{:S(2)}) async-start(bf16[32,8,3072]{2,1,0:T(8,128)(2,1)} %bitcast.16), calls=%async_computation | async-start | bytes 3145728 | tf_op jit(solution)/shard_map/dispatch/all_to_all | solution.py:223
  44.1 98.9 %all-gather.5.cloned.1.call-start = ((), (), s32[]{:S(2)}) async-start(), calls=%async_computation.2 | async-start | bytes 2359296 | tf_op jit(solution)/shard_map/keys/all_gather | solution.py:231
  104.4 38.5 %copy-start.2 = (bf16[1,128,2048]{2,1,0:T(8,128)(2,1)S(1)}, bf16[1,128,2048]{2,1,0:T(8,128)(2,1)}, u32[]{:S(2)}) copy-start(bf16[1,128,2048]{2,1,0:T(8,128)(2,1)} %param.10) | copy-start | bytes 1572868
  104.4 53.5 %all-to-all-start.1 = ((bf16[32,8,3072]{2,1,0:T(8,128)(2,1)}), bf16[32,8,3072]{2,1,0:T(8,128)(2,1)S(1)}, u32[]{:S(2)}, u32[]{:S(2)}) async-start(bf16[32,8,3072]{2,1,0:T(8,128)(2,1)} %bitcast.18), calls=%async_computation.1 | async-start | bytes 3145728 | tf_op jit(solution)/shard_map/experts/all_to_all | solution.py:243
  142.9 1.6 copy-start
Sparse Core Ops, SparseCore 0:
  28.5 69.4 all-gather.6
  100.0 42.8 all-gather.4

commit v2 on v1

v2 whole, which is shorter than its diff:
```python
import functools
import math

import jax
import jax.numpy as jnp
from jax import lax
from jax.experimental import pallas as pl
from jax.experimental.pallas import tpu as pltpu
from jax.sharding import Mesh, PartitionSpec as P

HD = 128
CAP = 12
LOW = 8
FOLD = CAP - LOW
CTX = ("zh", "y")
DP = ("zl", "x", "c")
CHIPS = ("zh", "zl", "x")
MASKED = -1e30
F32 = jnp.float32
BF16 = jnp.bfloat16
VMEM = pl.BlockSpec(memory_space=pltpu.VMEM)
SMEM = pl.BlockSpec(memory_space=pltpu.SMEM)


def pack_kernel(gate_ref, up_ref, down_ref, out_ref):
    rows, units = gate_ref.shape
    out_ref[:, :units] = gate_ref[...]
    out_ref[:, units : 2 * units] = up_ref[...]
    for j in range(units // rows):
        out_ref[:, (2 * units + j * rows) : (2 * units + (j + 1) * rows)] = down_ref[j * rows : (j + 1) * rows, :]


def dispatch_kernel(halves, owners, x_ref, gain_ref, ids_ref, gates_ref, out_ref, mix_a_ref, mix_b_ref):
    tokens, width = x_ref.shape
    slots = owners * LOW
    half = width // 2
    x = x_ref[...].astype(F32)
    normed = (x * lax.rsqrt(jnp.mean(x * x, axis=-1, keepdims=True) + 1e-06) * gain_ref[...]).astype(BF16)
    lane = lax.broadcasted_iota(jnp.int32, (tokens, slots), 1)
    chip = lane // LOW
    per_half = owners // halves
    expert = chip % per_half * halves + chip // per_half
    place = lane % LOW
    ids = ids_ref[...]
    gates = gates_ref[...]
    hot = jnp.zeros((tokens, slots), F32)
    gate = jnp.zeros((tokens, slots), F32)
    for k in range(ids.shape[1]):
        hit = ids[:, k : k + 1] == expert
        hot = jnp.where(hit, 1.0, hot)
        gate = jnp.where(hit, gates[:, k : k + 1], gate)
    row = lax.broadcasted_iota(jnp.int32, (tokens, tokens), 0)
    col = lax.broadcasted_iota(jnp.int32, (tokens, tokens), 1)
    earlier = jnp.where(col < row, 1.0, 0.0).astype(BF16)
    rank = jnp.dot(earlier, hot.astype(BF16), preferred_element_type=F32)
    rank = jnp.where(hot > 0.5, rank, -1.0)
    in_a = rank == place.astype(F32)
    in_b = rank == (LOW + place % FOLD).astype(F32)
    in_lo = in_b & (place < FOLD)
    in_hi = in_b & (place >= FOLD)

    def put(chosen):
        return jnp.where(chosen, 1.0, 0.0).astype(BF16)

    contract = (((0,), (0,)), ((), ()))
    out_ref[:, :width] = lax.dot_general(put(in_a), normed, contract, preferred_element_type=F32).astype(BF16)
    pick = jnp.concatenate([put(in_lo), put(in_hi)], axis=0)
    stacked = jnp.concatenate([normed[:, :half], normed[:, half:]], axis=0)
    out_ref[:, width:] = lax.dot_general(pick, stacked, contract, preferred_element_type=F32).astype(BF16)

    top = gate.astype(BF16).astype(F32)
    rest = gate - top

    def mix(chosen):
        return jnp.concatenate(
            [jnp.where(chosen, top, 0.0).astype(BF16), jnp.where(chosen, rest, 0.0).astype(BF16)], axis=0
        )

    mix_a_ref[...] = mix(in_a)
    mix_b_ref[:, :slots] = mix(in_lo)
    mix_b_ref[:, slots:] = mix(in_hi)


def expert_kernel(hidden_units, x_ref, mine_ref, other_ref, core_ref, out_ref):
    rows, wide = x_ref.shape
    count, block = mine_ref.shape[:2]
    half = count * block
    width = 2 * half
    both = 2 * hidden_units
    core = core_ref[0]
    mine_at = pl.multiple_of(core * half, half)
    other_at = pl.multiple_of((1 - core) * half, half)

    mine_w = mine_ref[:, :, :both].reshape(half, both)
    other_w = other_ref[:, :, :both].reshape(half, both)
    sums_a = jnp.dot(x_ref[:, pl.ds(mine_at, half)], mine_w, preferred_element_type=F32)
    sums_a = sums_a + jnp.dot(x_ref[:, pl.ds(other_at, half)], other_w, preferred_element_type=F32)
    folded = x_ref[:, width:]

    def from_mine(columns):
        side = lax.broadcasted_iota(jnp.int32, (rows, columns), 0) % LOW // FOLD
        return side == core

    sums_b = jnp.where(
        from_mine(both),
        jnp.dot(folded, mine_w, preferred_element_type=F32),
        jnp.dot(folded, other_w, preferred_element_type=F32),
    )
    groups = sums_b.reshape(rows // LOW, LOW, both)
    sums_b = (groups + pltpu.roll(groups, FOLD, 1)).reshape(rows, both)

    def activate(sums):
        gate = sums[:, :hidden_units]
        return (gate / (1.0 + jnp.exp(-gate)) * sums[:, hidden_units:]).astype(BF16)

    hidden_a = activate(sums_a)
    hidden_b = activate(sums_b)

    def down(ref, place):
        pieces = [ref[place, :, both + j * block : both + (j + 1) * block] for j in range(hidden_units // block)]
        return jnp.concatenate(pieces, axis=0)

    for lo in range(0, count, 2):
        mine_d = jnp.concatenate([down(mine_ref, lo), down(mine_ref, lo + 1)], axis=1)
        other_d = jnp.concatenate([down(other_ref, lo), down(other_ref, lo + 1)], axis=1)
        at, columns = lo * block, 2 * block
        out_ref[:, pl.ds(pl.multiple_of(mine_at + at, columns), columns)] = jnp.dot(
            hidden_a, mine_d, preferred_element_type=F32
        ).astype(BF16)
        out_ref[:, pl.ds(pl.multiple_of(other_at + at, columns), columns)] = jnp.dot(
            hidden_a, other_d, preferred_element_type=F32
        ).astype(BF16)
        out_ref[:, width + at : width + at + columns] = jnp.where(
            from_mine(columns),
            jnp.dot(hidden_b, mine_d, preferred_element_type=F32),
            jnp.dot(hidden_b, other_d, preferred_element_type=F32),
        ).astype(BF16)


def combine_kernel(back_ref, mix_a_ref, mix_b_ref, out_ref):
    tokens, width = out_ref.shape
    half = width // 2
    slots = back_ref.shape[0]
    folded = back_ref[:, width:]
    for side in range(2):
        columns = slice(side * half, (side + 1) * half)
        both = jnp.dot(mix_a_ref[...], back_ref[:, columns], preferred_element_type=F32) + jnp.dot(
            mix_b_ref[:, side * slots : (side + 1) * slots], folded, preferred_element_type=F32
        )
        out_ref[:, columns] = (both[:tokens] + both[tokens:]).astype(BF16)


def attend_kernel(halves, ring, heads_kv, q_ref, kv_ref, place_ref, out_ref):
    tokens, wide = q_ref.shape
    heads = wide // HD
    group = heads // heads_kv
    blocks = kv_ref.shape[0]
    keys = blocks * kv_ref.shape[1]
    scale = 1.0 / math.sqrt(HD)
    lane = lax.broadcasted_iota(jnp.int32, (tokens, keys), 1)
    row = lax.broadcasted_iota(jnp.int32, (tokens, keys), 0)
    block = lane // tokens
    here = place_ref[0] // ring
    passed = jnp.where(here == 0, halves, 0)
    side = jnp.where(block % halves == 0, here, passed)
    key_pos = (side * ring + block // halves) * tokens + lane % tokens
    allowed = key_pos <= row + place_ref[0] * tokens
    for g in range(heads_kv):
        key = kv_ref[:, :, g * HD : (g + 1) * HD].reshape(keys, HD)
        value = kv_ref[:, :, (heads_kv + g) * HD : (heads_kv + g + 1) * HD].reshape(keys, HD)

        @pl.loop(0, group)
        def _(i):
            at = pl.ds(pl.multiple_of((g * group + i) * HD, HD), HD)
            scores = lax.dot_general(
                q_ref[:, at], key, (((1,), (1,)), ((), ())), preferred_element_type=F32
            )
            scores = jnp.where(allowed, scores * scale, MASKED)
            largest = jnp.max(scores, axis=-1, keepdims=True)
            probs = jnp.exp(scores - largest)
            total = jnp.sum(probs, axis=-1, keepdims=True)
            mixed = jnp.dot(probs.astype(BF16), value, preferred_element_type=F32)
            out_ref[:, at] = (mixed / total).astype(BF16)


def estimate(flops, bytes_accessed, transcendentals=0):
    return pl.CostEstimate(flops=flops, bytes_accessed=bytes_accessed, transcendentals=transcendentals)


def shards(
    queries, key_rows, value_rows, stream, norm_gain, expert_ids, gate_values, w_gate, w_up, w_down
):
    tokens, width = stream.shape[1:]
    heads_kv = key_rows.shape[2] // HD
    hidden_units = w_gate.shape[2]
    halves, ring, cores = lax.axis_size("zh"), lax.axis_size("y"), lax.axis_size("c")
    owners = lax.axis_size(DP)
    slots = owners * LOW
    wide = width + width // 2
    params = pltpu.CompilerParams(vmem_limit_bytes=48 * 1024 * 1024)

    with jax.named_scope("weights"):
        packed = pl.pallas_call(
            pack_kernel,
            out_shape=jax.ShapeDtypeStruct((w_gate.shape[1], 3 * hidden_units), BF16),
            in_specs=[VMEM] * 3,
            out_specs=VMEM,
            name="pack",
        )(w_gate[0], w_up[0], w_down[0])
        swap = [(h * cores + c, c * cores + h) for h in range(halves) for c in range(cores)]
        kv = jnp.concatenate([key_rows[0], value_rows[0]], axis=1)
        kv, packed = lax.optimization_barrier((kv, packed))
        mine_part = lax.ppermute(packed, ("zh", "c"), swap)
        kv_passed = lax.ppermute(kv, "zh", [(0, 1)])
        mine = lax.all_gather(mine_part, "y", axis=0)
        other = lax.ppermute(mine, "c", [(0, 1), (1, 0)])

    with jax.named_scope("dispatch"):
        ids, _, kv_passed = lax.optimization_barrier((expert_ids[0], mine_part, kv_passed))
        outgoing, mix_a, mix_b = pl.pallas_call(
            functools.partial(dispatch_kernel, halves, owners),
            out_shape=(
                jax.ShapeDtypeStruct((slots, wide), BF16),
                jax.ShapeDtypeStruct((2 * tokens, slots), BF16),
                jax.ShapeDtypeStruct((2 * tokens, 2 * slots), BF16),
            ),
            in_specs=[VMEM] * 4,
            out_specs=(VMEM,) * 3,
            compiler_params=params,
            cost_estimate=estimate(4 * 256 * 256 * 2048, 4 * 1024 * 1024),
            name="dispatch",
        )(stream[0], norm_gain[None, :], ids, gate_values[0])
        arrived = lax.all_to_all(
            outgoing.reshape(owners, LOW, wide), CHIPS, split_axis=0, concat_axis=0, tiled=True
        ).reshape(slots, wide)

    with jax.named_scope("keys"):
        kv_passed, outgoing = lax.optimization_barrier((kv_passed, outgoing))
        kv_pair = jnp.stack([kv, kv_passed])
        kv_all = lax.all_gather(kv_pair, "y", axis=0, tiled=True)

    with jax.named_scope("experts"):
        answers = pl.pallas_call(
            functools.partial(expert_kernel, hidden_units),
            out_shape=jax.ShapeDtypeStruct((slots, wide), BF16),
            in_specs=[VMEM, VMEM, VMEM, SMEM],
            out_specs=VMEM,
            compiler_params=params,
            cost_estimate=estimate(6 * 512 * 2048 * 384, 8 * 1024 * 1024),
            name="experts",
        )(arrived, mine, other, lax.axis_index("c").astype(jnp.int32)[None])
        returned = lax.all_to_all(
            answers.reshape(owners, LOW, wide), CHIPS, split_axis=0, concat_axis=0, tiled=True
        ).reshape(slots, wide)

    with jax.named_scope("attend"):
        place = lax.axis_index(CTX).astype(jnp.int32)[None]
        attended = pl.pallas_call(
            functools.partial(attend_kernel, halves, ring, heads_kv),
            out_shape=jax.ShapeDtypeStruct(queries.shape[1:], BF16),
            in_specs=[VMEM, VMEM, SMEM],
            out_specs=VMEM,
            compiler_params=params,
            cost_estimate=estimate(4 * 2048 * 128 * 2048, 4 * 1024 * 1024, 16 * 128 * 2048),
            name="attend",
        )(queries[0], kv_all, place)

    with jax.named_scope("combine"):
        expert_out = pl.pallas_call(
            combine_kernel,
            out_shape=jax.ShapeDtypeStruct((tokens, width), BF16),
            in_specs=[VMEM] * 3,
            out_specs=VMEM,
            compiler_params=params,
            cost_estimate=estimate(2 * 256 * 512 * 2048, 3 * 1024 * 1024),
            name="combine",
        )(returned, mix_a, mix_b)
    return (attended[None], expert_out[None])


def solution(mesh):
    fine = Mesh(mesh.devices.reshape(2, 8, 4, 4, 2), CTX + DP)
    rows = P(DP, CTX, None)
    return jax.shard_map(
        shards,
        mesh=fine,
        in_specs=(rows, rows, rows, rows, P(), rows, rows, rows, rows, P(DP, None, CTX)),
        out_specs=(rows, rows),
        check_vma=False,
    )
```

time: 167 us -> 148 us (0.89)
  blocking collectives: 54.4 us -> 0 us
  starting transfers between devices: 21.6 us -> 45.4 us
  waiting for transfers between devices: 46.5 us -> 54.7 us
    all_gather x2 -> x0, blocking collectives: 54.4 us -> none  [the longest x1 37.5 us: shards(): kv_pair = lax.all_gather(kv, 'zh', axis=0)]
    ppermute x0 -> x3, starting transfers between devices: none -> 25.1 us  [the longest x1 21.6 us: shards(): kv_passed = lax.ppermute(kv, 'zh', [(0, 1)])]
    all_gather x1, waiting for transfers between devices: 30.2 us -> 19.1 us  [shards(): kv_all = lax.all_gather(kv_pair, 'y', axis=0, tiled=True)]
    all_gather x1, waiting for transfers between devices: 11.1 us -> 20.6 us  [shards(): mine = lax.all_gather(mine_part, 'y', axis=0)]
    all_to_all x2, waiting for transfers between devices: 5.27 us -> 14 us  [the longest x1 9.83 us: shards(): lax.all_to_all(outgoing.reshape(owners, LOW, wide), CHIPS, split_axis=0,...]
    unnamed x22 -> x14, local copies, waits for them, and re-layouts: 5.23 us -> 7.29 us
    pallas_call x2 -> x3, Pallas kernels: 3.81 us -> 5.55 us  [the longest x1 2.31 us: shards(): pl.pallas_call(functools.partial(dispatch_kernel, halves, owners), out_sh...]
  transfers between devices with their start and end apart: 4 -> 7, of which waited for: 3 -> 5; matrix products, arithmetic and copies ran while one was open for 0% -> 2% of each run, Pallas kernels for 13% -> 15%
where the time goes in v2:
time: 148 us
  waiting for transfers between devices  54.7 us (37%)
  starting transfers between devices  45.4 us (31%)
  Pallas kernels  24.7 us (17%)
  between operations  14.1 us (10%)
  local copies, waits for them, and re-layouts  7.29 us (5%)
  other arithmetic  1.61 us (1%)
    ppermute x1, starting transfers between devices, shards(): kv_passed = lax.ppermute(kv, 'zh', [(0, 1)])  21.6 us
    all_gather x1, waiting for transfers between devices, shards(): mine = lax.all_gather(mine_part, 'y', axis=0)  20.6 us
    all_gather x1, waiting for transfers between devices, shards(): kv_all = lax.all_gather(kv_pair, 'y', axis=0, tiled=True)  19.1 us
    all_to_all x1, starting transfers between devices, shards(): lax.all_to_all(outgoing.reshape(owners, LOW, wide), CHIPS, split_axis=0,...  14 us
    pallas_call x1, Pallas kernels, shards(): pl.pallas_call(functools.partial(attend_kernel, halves, ring, heads_kv),...  13.3 us
    all_to_all x1, waiting for transfers between devices, shards(): lax.all_to_all(outgoing.reshape(owners, LOW, wide), CHIPS, split_axis=0,...  9.83 us
    unnamed x14, local copies, waits for them, and re-layouts  7.29 us
    all_to_all x1, starting transfers between devices, shards(): lax.all_to_all(answers.reshape(owners, LOW, wide), CHIPS, split_axis=0, c...  6.21 us
  transfers between devices with their start and end apart: 7, of which 5 were waited for; matrix products, arithmetic and copies ran while one was open for 2% of the time, Pallas kernels for 15%

profile of v2, /device:TPU:6, one launch (start us, length us, event | category | flops | bytes accessed | tf_op | source)
XLA Modules:
  0.0 147.7 jit_solution(14060586569777016572)
XLA Ops:
  7.2 0.0 all-gather.6.cloned.1.call-start
  7.2 0.9 pad_maximum_fusion.1
  8.1 1.7 %pack.1 = bf16[128,1152]{1,0:T(8,128)(2,1)} custom-call(bf16[128,384]{1,0:T(8,128)(2,1)} %bitcast.33, bf16[128,384]{1,0:T(8,128)(2,1)} %bitcast.34, bf16[384,128]{1,0:T(8,128)(2,1)} %bitcast.35), custom_call_target="tpu_custom_call" | custom-call | tf_op jit(solution)/shard_map/weights/pack/pallas_call | solution.py:203
  9.8 1.6 %collective-permute-start = (bf16[128,1152]{1,0:T(8,128)(2,1)}, bf16[128,1152]{1,0:T(8,128)(2,1)S(1)}, u32[]{:S(2)}, u32[]{:S(2)}) collective-permute-start(bf16[128,1152]{1,0:T(8,128)(2,1)} %pack.1), channel_id=1, source_target_pairs={{0,0},{1,256},{256,1},{257,257},{2,2},{3,258},{258,3},{259,259},{4... | collective-permute-start | bytes 884744 | tf_op jit(solution)/shard_map/weights/ppermute | solution.py:213
  11.4 0.0 collective-permute-done
  11.4 0.0 copy-start.5
  11.4 0.7 copy-done.5
  12.2 0.0 all-gather.6.cloned.1.call-update
  12.2 21.6 %collective-permute-start.1 = (bf16[128,512]{1,0:T(8,128)(2,1)S(1)}, bf16[128,512]{1,0:T(8,128)(2,1)S(1)}, u32[]{:S(2)}, u32[]{:S(2)}) collective-permute-start(bf16[128,512]{1,0:T(8,128)(2,1)S(1)} %pad_maximum_fusion.1), channel_id=1, source_target_pairs={{0,256},{1,257},{2,258},{3,259},{4,260},{5,261},{6,262},{7,263},{8... | collective-permute-start | bytes 393224 | tf_op jit(solution)/shard_map/weights/ppermute | solution.py:214
  33.7 0.8 copy.14
  34.5 0.8 copy.15
  35.3 0.9 collective-permute-done.1
  36.2 0.0 copy-start.2
  36.2 1.0 copy-done.2
  37.3 0.0 copy-start.4
  37.3 0.7 copy-done.4
  38.0 2.3 %dispatch.1 = (bf16[256,3072]{1,0:T(8,128)(2,1)}, bf16[256,256]{1,0:T(8,128)(2,1)S(1)}, bf16[256,512]{1,0:T(8,128)(2,1)S(1)}) custom-call(bf16[128,2048]{1,0:T(8,128)(2,1)S(1)} %bitcast.27, f32[1,2048]{1,0:T(1,128)S(1)} %bitcast.29, s32[128,8]{1,0:T(8,128)S(1)} %bitcast.23, f32[128,8]{1,0:T(8,128)S(1)} %bitcast.24), custom_call_target="tpu_custom_call" | custom-call | flops 536870912 | bytes 4194304 | tf_op jit(solution)/shard_map/dispatch/dispatch/pallas_call | solution.py:220
  40.3 14.0 %all-to-all-start = ((bf16[32,8,3072]{2,1,0:T(8,128)(2,1)}), bf16[32,8,3072]{2,1,0:T(8,128)(2,1)S(1)}, u32[]{:S(2)}, u32[]{:S(2)}) async-start(bf16[32,8,3072]{2,1,0:T(8,128)(2,1)} %bitcast.14), calls=%async_computation | async-start | bytes 3145728 | tf_op jit(solution)/shard_map/dispatch/all_to_all | solution.py:233
  54.3 0.0 all-gather.4.cloned.1.call-start
  54.3 20.6 %all-gather.6.cloned.1.call-done = bf16[1024,1152]{1,0:T(8,128)(2,1)} async-done(((bf16[128,1152]{1,0:T(8,128)(2,1)}), bf16[1024,1152]{1,0:T(8,128)(2,1)}) %all-gather.6.cloned.1.call-update) | async-done | bytes 2359312 | tf_op jit(solution)/shard_map/weights/all_gather | solution.py:215
  74.9 1.9 %collective-permute-start.2 = (bf16[8,128,1152]{2,1,0:T(8,128)(2,1)}, bf16[8,128,1152]{2,1,0:T(8,128)(2,1)}, u32[]{:S(2)}, u32[]{:S(2)}) collective-permute-start(bf16[8,128,1152]{2,1,0:T(8,128)(2,1)} %bitcast.25), channel_id=1, source_target_pairs={{0,1},{1,0},{2,3},{3,2},{4,5},{5,4},{6,7},{7,6},{8,9},{9,8},{10,11... | collective-permute-start | bytes 7077896 | tf_op jit(solution)/shard_map/weights/ppermute | solution.py:216
  76.9 0.7 pad_maximum_fusion
  77.6 0.0 all-gather.4.cloned.1.call-update
  77.6 9.8 %all-to-all-done = bf16[32,8,3072]{2,1,0:T(8,128)(2,1)S(1)} async-done(((bf16[32,8,3072]{2,1,0:T(8,128)(2,1)}), bf16[32,8,3072]{2,1,0:T(8,128)(2,1)S(1)}, u32[]{:S(2)}, u32[]{:S(2)}) %all-to-all-start) | async-done | bytes 1572896 | tf_op jit(solution)/shard_map/dispatch/all_to_all | solution.py:233
  87.4 0.0 collective-permute-done.2.other_ref
  87.4 0.0 copy-start
  87.4 1.7 %copy-done = bf16[1024,1152]{1,0:T(8,128)(2,1)S(1)} copy-done((bf16[1024,1152]{1,0:T(8,128)(2,1)S(1)}, bf16[1024,1152]{1,0:T(8,128)(2,1)}, u32[]{:S(2)}) %copy-start) | copy-done | bytes 2359320
  89.1 5.8 %experts.1 = bf16[256,3072]{1,0:T(8,128)(2,1)} custom-call(bf16[256,3072]{1,0:T(8,128)(2,1)S(1)} %bitcast.22, bf16[8,128,1152]{2,1,0:T(8,128)(2,1)S(1)} %bitcast.26, bf16[8,128,1152]{2,1,0:T(8,128)(2,1)} %collective-permute-done.2.other_ref, s32[1]{0:T(128)} %bitcast.17.core_ref), custom_call_target="tpu_custom_call" | custom-call | flops 2415919104 | bytes 8388608 | tf_op jit(solution)/shard_map/experts/experts/pallas_call | solution.py:243
  94.9 0.0 copy-start.3
  94.9 6.2 %all-to-all-start.1 = ((bf16[32,8,3072]{2,1,0:T(8,128)(2,1)}), bf16[32,8,3072]{2,1,0:T(8,128)(2,1)S(1)}, u32[]{:S(2)}, u32[]{:S(2)}) async-start(bf16[32,8,3072]{2,1,0:T(8,128)(2,1)} %bitcast.18), calls=%async_computation.1 | async-start | bytes 3145728 | tf_op jit(solution)/shard_map/experts/all_to_all | solution.py:252
  101.1 19.1 %all-gather.4.cloned.1.call-done.kv_ref = bf16[16,128,512]{2,1,0:T(8,128)(2,1)} async-done(((bf16[2,128,512]{2,1,0:T(8,128)(2,1)}), bf16[16,128,512]{2,1,0:T(8,128)(2,1)}) %all-gather.4.cloned.1.call-update) | async-done | bytes 2097168 | tf_op jit(solution)/shard_map/keys/all_gather | solution.py:240
  120.2 0.0 copy-done.3
  120.2 0.0 copy-start.1
  120.2 1.6 %copy-done.1 = bf16[16,128,512]{2,1,0:T(8,128)(2,1)S(1)} copy-done((bf16[16,128,512]{2,1,0:T(8,128)(2,1)S(1)}, bf16[16,128,512]{2,1,0:T(8,128)(2,1)}, u32[]{:S(2)}) %copy-start.1) | copy-done | bytes 2097176
  121.8 13.3 %attend.1 = bf16[128,2048]{1,0:T(8,128)(2,1)} custom-call(bf16[128,2048]{1,0:T(8,128)(2,1)S(1)} %bitcast.28, bf16[16,128,512]{2,1,0:T(8,128)(2,1)S(1)} %copy-done.1, s32[1]{0:T(128)} %bitcast.12.place_ref), custom_call_target="tpu_custom_call" | custom-call | flops 2147483648 | bytes 4194304 | tf_op jit(solution)/shard_map/attend/attend/pallas_call | solution.py:258
  135.2 4.2 %all-to-all-done.1 = bf16[32,8,3072]{2,1,0:T(8,128)(2,1)S(1)} async-done(((bf16[32,8,3072]{2,1,0:T(8,128)(2,1)}), bf16[32,8,3072]{2,1,0:T(8,128)(2,1)S(1)}, u32[]{:S(2)}, u32[]{:S(2)}) %all-to-all-start.1) | async-done | bytes 1572896 | tf_op jit(solution)/shard_map/experts/all_to_all | solution.py:252
  139.4 1.5 %combine.1 = bf16[128,2048]{1,0:T(8,128)(2,1)} custom-call(bf16[256,3072]{1,0:T(8,128)(2,1)S(1)} %bitcast.21, bf16[256,256]{1,0:T(8,128)(2,1)S(1)} %get-tuple-element.16.mix_a_ref, bf16[256,512]{1,0:T(8,128)(2,1)S(1)} %get-tuple-element.17.mix_b_ref), custom_call_target="tpu_custom_call" | custom-call | flops 536870912 | bytes 3145728 | tf_op jit(solution)/shard_map/combine/combine/pallas_call | solution.py:269
Async XLA Ops:
  7.2 67.8 %all-gather.6.cloned.1.call-start = ((), (), s32[]{:S(2)}) async-start(), calls=%async_computation.3 | async-start | bytes 2654208 | tf_op jit(solution)/shard_map/weights/all_gather | solution.py:215
  9.8 1.6 %collective-permute-start = (bf16[128,1152]{1,0:T(8,128)(2,1)}, bf16[128,1152]{1,0:T(8,128)(2,1)S(1)}, u32[]{:S(2)}, u32[]{:S(2)}) collective-permute-start(bf16[128,1152]{1,0:T(8,128)(2,1)} %pack.1), channel_id=1, source_target_pairs={{0,0},{1,256},{256,1},{257,257},{2,2},{3,258},{258,3},{259,259},{4... | collective-permute-start | bytes 884744 | tf_op jit(solution)/shard_map/weights/ppermute | solution.py:213
  11.4 0.7 copy-start.5
  12.2 24.1 %collective-permute-start.1 = (bf16[128,512]{1,0:T(8,128)(2,1)S(1)}, bf16[128,512]{1,0:T(8,128)(2,1)S(1)}, u32[]{:S(2)}, u32[]{:S(2)}) collective-permute-start(bf16[128,512]{1,0:T(8,128)(2,1)S(1)} %pad_maximum_fusion.1), channel_id=1, source_target_pairs={{0,256},{1,257},{2,258},{3,259},{4,260},{5,261},{6,262},{7,263},{8... | collective-permute-start | bytes 393224 | tf_op jit(solution)/shard_map/weights/ppermute | solution.py:214
  36.2 1.0 copy-start.2
  37.3 0.7 copy-start.4
  40.3 47.1 %all-to-all-start = ((bf16[32,8,3072]{2,1,0:T(8,128)(2,1)}), bf16[32,8,3072]{2,1,0:T(8,128)(2,1)S(1)}, u32[]{:S(2)}, u32[]{:S(2)}) async-start(bf16[32,8,3072]{2,1,0:T(8,128)(2,1)} %bitcast.14), calls=%async_computation | async-start | bytes 3145728 | tf_op jit(solution)/shard_map/dispatch/all_to_all | solution.py:233
  54.3 65.9 %all-gather.4.cloned.1.call-start = ((), (), s32[]{:S(2)}) async-start(), calls=%async_computation.2 | async-start | bytes 2359296 | tf_op jit(solution)/shard_map/keys/all_gather | solution.py:240
  74.9 12.5 %collective-permute-start.2 = (bf16[8,128,1152]{2,1,0:T(8,128)(2,1)}, bf16[8,128,1152]{2,1,0:T(8,128)(2,1)}, u32[]{:S(2)}, u32[]{:S(2)}) collective-permute-start(bf16[8,128,1152]{2,1,0:T(8,128)(2,1)} %bitcast.25), channel_id=1, source_target_pairs={{0,1},{1,0},{2,3},{3,2},{4,5},{5,4},{6,7},{7,6},{8,9},{9,8},{10,11... | collective-permute-start | bytes 7077896 | tf_op jit(solution)/shard_map/weights/ppermute | solution.py:216
  87.4 1.7 %copy-start = (bf16[1024,1152]{1,0:T(8,128)(2,1)S(1)}, bf16[1024,1152]{1,0:T(8,128)(2,1)}, u32[]{:S(2)}) copy-start(bf16[1024,1152]{1,0:T(8,128)(2,1)} %all-gather.6.cloned.1.call-done) | copy-start | bytes 7077892
  94.9 25.3 %copy-start.3 = (bf16[1,128,2048]{2,1,0:T(8,128)(2,1)S(1)}, bf16[1,128,2048]{2,1,0:T(8,128)(2,1)}, u32[]{:S(2)}) copy-start(bf16[1,128,2048]{2,1,0:T(8,128)(2,1)} %param.10) | copy-start | bytes 1572868
  94.9 44.5 %all-to-all-start.1 = ((bf16[32,8,3072]{2,1,0:T(8,128)(2,1)}), bf16[32,8,3072]{2,1,0:T(8,128)(2,1)S(1)}, u32[]{:S(2)}, u32[]{:S(2)}) async-start(bf16[32,8,3072]{2,1,0:T(8,128)(2,1)} %bitcast.18), calls=%async_computation.1 | async-start | bytes 3145728 | tf_op jit(solution)/shard_map/experts/all_to_all | solution.py:252
  120.2 1.6 %copy-start.1 = (bf16[16,128,512]{2,1,0:T(8,128)(2,1)S(1)}, bf16[16,128,512]{2,1,0:T(8,128)(2,1)}, u32[]{:S(2)}) copy-start(bf16[16,128,512]{2,1,0:T(8,128)(2,1)} %all-gather.4.cloned.1.call-done.kv_ref) | copy-start | bytes 6291460
Sparse Core Ops, SparseCore 0:
  12.3 62.5 all-gather.5
  77.7 42.4 all-gather.3

commit v3 on v1

--- a/solution.py
+++ b/solution.py
@@ -14,31 +14,43 @@
 FOLD = CAP - LOW
 CTX = ("zh", "y")
 DP = ("zl", "x", "c")
+CHIPS = ("zh", "zl", "x")
 MASKED = -1e30
 F32 = jnp.float32
 BF16 = jnp.bfloat16
 VMEM = pl.BlockSpec(memory_space=pltpu.VMEM)
-
-
-def natural_block(place, halves, ring):
-    return (place % halves) * ring + place // halves
-
-
-def dispatch_kernel(halves, ring, owners, x_ref, gain_ref, ids_ref, gates_ref, out_ref, mix_a_ref, mix_b_ref):
+SMEM = pl.BlockSpec(memory_space=pltpu.SMEM)
+
+
+def pack_kernel(gate_ref, up_ref, down_ref, out_ref):
+    rows, units = gate_ref.shape
+    out_ref[:, :units] = gate_ref[...]
+    out_ref[:, units : 2 * units] = up_ref[...]
+    for j in range(units // rows):
+        out_ref[:, (2 * units + j * rows) : (2 * units + (j + 1) * rows)] = down_ref[j * rows : (j + 1) * rows, :]
+
+
+def natural_block(place, cores, ring):
+    return (place % cores) * ring + place // cores
+
+
+def dispatch_kernel(halves, cores, ring, owners, x_ref, gain_ref, ids_ref, gates_ref, out_ref, mix_a_ref, mix_b_ref):
     tokens, width = x_ref.shape
     slots = owners * LOW
     half = width // 2
     x = x_ref[...].astype(F32)
     normed = (x * lax.rsqrt(jnp.mean(x * x, axis=-1, keepdims=True) + 1e-06) * gain_ref[...]).astype(BF16)
-    step = width // (halves * ring)
+    step = width // (cores * ring)
     pieces = []
-    for place in range(halves * ring):
-        start = natural_block(place, halves, ring) * step
+    for place in range(cores * ring):
+        start = natural_block(place, cores, ring) * step
         pieces.append(normed[:, start : start + step])
     normed = jnp.concatenate(pieces, axis=1)
 
     lane = lax.broadcasted_iota(jnp.int32, (tokens, slots), 1)
-    expert = lane // LOW
+    chip = lane // LOW
+    per_half = owners // halves
+    expert = chip % per_half * halves + chip // per_half
     place = lane % LOW
     ids = ids_ref[...]
     gates = gates_ref[...]
@@ -134,11 +146,11 @@
         ).astype(BF16)
 
 
-def combine_kernel(halves, ring, back_ref, mix_a_ref, mix_b_ref, out_ref):
+def combine_kernel(cores, ring, back_ref, mix_a_ref, mix_b_ref, out_ref):
     tokens, width = out_ref.shape
     half = width // 2
     slots = back_ref.shape[0]
-    step = width // (halves * ring)
+    step = width // (cores * ring)
     folded = back_ref[:, width:]
     for side in range(2):
         both = jnp.dot(
@@ -148,7 +160,7 @@
         )
         total = (both[:tokens] + both[tokens:]).astype(BF16)
         for i in range(half // step):
-            start = natural_block(side * (half // step) + i, halves, ring) * step
+            start = natural_block(side * (half // step) + i, cores, ring) * step
             out_ref[:, start : start + step] = total[:, i * step : (i + 1) * step]
 
 
@@ -162,7 +174,10 @@
     lane = lax.broadcasted_iota(jnp.int32, (tokens, keys), 1)
     row = lax.broadcasted_iota(jnp.int32, (tokens, keys), 0)
     block = lane // tokens
-    key_pos = ((block % halves) * ring + block // halves) * tokens + lane % tokens
+    here = place_ref[0] // ring
+    passed = jnp.where(here == 0, halves, 0)
+    side = jnp.where(block % halves == 0, here, passed)
+    key_pos = (side * ring + block // halves) * tokens + lane % tokens
     allowed = key_pos <= row + place_ref[0] * tokens
     for g in range(heads_kv):
         key = kv_ref[:, :, g * HD : (g + 1) * HD].reshape(keys, HD)
@@ -192,23 +207,26 @@
     tokens, width = stream.shape[1:]
     heads_kv = key_rows.shape[2] // HD
     hidden_units = w_gate.shape[2]
-    halves, ring = lax.axis_size("zh"), lax.axis_size("y")
+    halves, ring, cores = lax.axis_size("zh"), lax.axis_size("y"), lax.axis_size("c")
     owners = lax.axis_size(DP)
     slots = owners * LOW
     wide = width + width // 2
     params = pltpu.CompilerParams(vmem_limit_bytes=48 * 1024 * 1024)
 
     with jax.named_scope("weights"):
-        down = w_down[0]
-        pieces = [down[j * tokens : (j + 1) * tokens] for j in range(hidden_units // tokens)]
-        packed = jnp.concatenate([w_gate[0], w_up[0]] + pieces, axis=1)
-        pair = lax.all_gather(packed, "zh", axis=0)
-        weights = lax.all_gather(pair, "y", axis=0, tiled=True)
-
+        packed = pl.pallas_call(
+            pack_kernel,
+            out_shape=jax.ShapeDtypeStruct((w_gate.shape[1], 3 * hidden_units), BF16),
+            in_specs=[VMEM] * 3,
+            out_specs=VMEM,
+            name="pack",
+        )(w_gate[0], w_up[0], w_down[0])
+        swap = [(h * cores + c, c * cores + h) for h in range(halves) for c in range(cores)]
+        part = lax.ppermute(packed, ("zh", "c"), swap)
     with jax.named_scope("dispatch"):
-        ids, pair = lax.optimization_barrier((expert_ids[0], pair))
+        ids, _ = lax.optimization_barrier((expert_ids[0], packed))
         outgoing, mix_a, mix_b = pl.pallas_call(
-            functools.partial(dispatch_kernel, halves, ring, owners),
+            functools.partial(dispatch_kernel, halves, cores, ring, owners),
             out_shape=(
                 jax.ShapeDtypeStruct((slots, wide), BF16),
                 jax.ShapeDtypeStruct((2 * tokens, slots), BF16),
@@ -220,28 +238,34 @@
             cost_estimate=estimate(4 * 256 * 256 * 2048, 4 * 1024 * 1024),
             name="dispatch",
         )(stream[0], norm_gain[None, :], ids, gate_values[0])
+        part, outgoing = lax.optimization_barrier((part, outgoing))
+        weights = lax.all_gather(part, ("y", "c"), axis=0)
         arrived = lax.all_to_all(
-            outgoing.reshape(owners, LOW, wide), DP, split_axis=0, concat_axis=0, tiled=True
+            outgoing.reshape(owners, LOW, wide), CHIPS, split_axis=0, concat_axis=0, tiled=True
         ).reshape(slots, wide)
 
     with jax.named_scope("keys"):
-        kv = jnp.concatenate([key_rows[0], value_rows[0]], axis=1)
-        kv, outgoing = lax.optimization_barrier((kv, outgoing))
-        kv_pair = lax.all_gather(kv, "zh", axis=0)
+        key_local, value_local, outgoing, part = lax.optimization_barrier(
+            (key_rows[0], value_rows[0], outgoing, part)
+        )
+        kv = jnp.concatenate([key_local, value_local], axis=1)
+        kv_passed = lax.ppermute(kv, "zh", [(0, 1)])
+        kv_pair = jnp.stack([kv, kv_passed])
         kv_all = lax.all_gather(kv_pair, "y", axis=0, tiled=True)
+        arrived, kv_pair = lax.optimization_barrier((arrived, kv_pair))
 
     with jax.named_scope("experts"):
         answers = pl.pallas_call(
             functools.partial(expert_kernel, hidden_units),
             out_shape=jax.ShapeDtypeStruct((slots, wide), BF16),
-            in_specs=[VMEM] * 2,
+            in_specs=[VMEM, VMEM],
             out_specs=VMEM,
             compiler_params=params,
             cost_estimate=estimate(6 * 512 * 2048 * 384, 8 * 1024 * 1024),
             name="experts",
         )(arrived, weights)
         returned = lax.all_to_all(
-            answers.reshape(owners, LOW, wide), DP, split_axis=0, concat_axis=0, tiled=True
+            answers.reshape(owners, LOW, wide), CHIPS, split_axis=0, concat_axis=0, tiled=True
         ).reshape(slots, wide)
 
     with jax.named_scope("attend"):
@@ -249,7 +273,7 @@
         attended = pl.pallas_call(
             functools.partial(attend_kernel, halves, ring, heads_kv),
             out_shape=jax.ShapeDtypeStruct(queries.shape[1:], BF16),
-            in_specs=[VMEM, VMEM, pl.BlockSpec(memory_space=pltpu.SMEM)],
+            in_specs=[VMEM, VMEM, SMEM],
             out_specs=VMEM,
             compiler_params=params,
             cost_estimate=estimate(4 * 2048 * 128 * 2048, 4 * 1024 * 1024, 16 * 128 * 2048),
@@ -258,7 +282,7 @@
 
     with jax.named_scope("combine"):
         expert_out = pl.pallas_call(
-            functools.partial(combine_kernel, halves, ring),
+            functools.partial(combine_kernel, cores, ring),
             out_shape=jax.ShapeDtypeStruct((tokens, width), BF16),
             in_specs=[VMEM] * 3,
             out_specs=VMEM,

time: 167 us -> 145 us (0.87)
  blocking collectives: 54.4 us -> 0 us
  starting transfers between devices: 21.6 us -> 41.9 us
  waiting for transfers between devices: 46.5 us -> 56.8 us
  Pallas kernels: 23.6 us -> 25.3 us
    all_gather x2 -> x0, blocking collectives: 54.4 us -> none  [the longest x1 37.5 us: shards(): kv_pair = lax.all_gather(kv, 'zh', axis=0)]
    ppermute x0 -> x2, waiting for transfers between devices: none -> 25.4 us  [the longest x1 25.4 us: shards(): kv_passed = lax.ppermute(kv, 'zh', [(0, 1)])]
    all_to_all x2, starting transfers between devices: 21.5 us -> 32.9 us  [the longest x1 21.6 us: shards(): lax.all_to_all(outgoing.reshape(owners, LOW, wide), CHIPS, split_axis=0,...]
    all_gather x1, waiting for transfers between devices: 11.1 us -> 0.54 us  [shards(): weights = lax.all_gather(part, ('y', 'c'), axis=0)]
    ppermute x0 -> x2, starting transfers between devices: none -> 8.9 us  [the longest x1 7.29 us: shards(): kv_passed = lax.ppermute(kv, 'zh', [(0, 1)])]
    all_to_all x2, waiting for transfers between devices: 5.27 us -> 2.46 us  [the longest x1 2.46 us: shards(): lax.all_to_all(outgoing.reshape(owners, LOW, wide), CHIPS, split_axis=0,...]
    all_gather x1, waiting for transfers between devices: 30.2 us -> 28.4 us  [shards(): kv_all = lax.all_gather(kv_pair, 'y', axis=0, tiled=True)]
    pallas_call x2 -> x3, Pallas kernels: 3.81 us -> 5.54 us  [the longest x1 2.3 us: shards(): pl.pallas_call(functools.partial(dispatch_kernel, halves, cores, ring, ow...]
  transfers between devices with their start and end apart: 4 -> 6, of which waited for: 3 -> 4; matrix products, arithmetic and copies ran while one was open for 0% -> 2% of each run, Pallas kernels for 13% -> 15%
where the time goes in v3:
time: 145 us
  waiting for transfers between devices  56.8 us (39%)
  starting transfers between devices  41.9 us (29%)
  Pallas kernels  25.3 us (17%)
  between operations  14.1 us (10%)
  local copies, waits for them, and re-layouts  5.64 us (4%)
    all_gather x1, waiting for transfers between devices, shards(): kv_all = lax.all_gather(kv_pair, 'y', axis=0, tiled=True)  28.4 us
    ppermute x1, waiting for transfers between devices, shards(): kv_passed = lax.ppermute(kv, 'zh', [(0, 1)])  25.4 us
    all_to_all x1, starting transfers between devices, shards(): lax.all_to_all(outgoing.reshape(owners, LOW, wide), CHIPS, split_axis=0,...  21.6 us
    pallas_call x1, Pallas kernels, shards(): pl.pallas_call(functools.partial(attend_kernel, halves, ring, heads_kv),...  13.3 us
    all_to_all x1, starting transfers between devices, shards(): lax.all_to_all(answers.reshape(owners, LOW, wide), CHIPS, split_axis=0, c...  11.3 us
    ppermute x1, starting transfers between devices, shards(): kv_passed = lax.ppermute(kv, 'zh', [(0, 1)])  7.29 us
    pallas_call x1, Pallas kernels, shards(): pl.pallas_call(functools.partial(expert_kernel, hidden_units), out_shape=...  6.43 us
    unnamed x17, local copies, waits for them, and re-layouts  5.63 us
  transfers between devices with their start and end apart: 6, of which 4 were waited for; matrix products, arithmetic and copies ran while one was open for 2% of the time, Pallas kernels for 15%

profile of v3, /device:TPU:6, one launch (start us, length us, event | category | flops | bytes accessed | tf_op | source)
XLA Modules:
  0.0 144.5 jit_solution(10540667394412056911)
XLA Ops:
  7.2 0.0 all-gather.6.cloned.1.call-start
  7.2 1.7 %pack.1 = bf16[128,1152]{1,0:T(8,128)(2,1)} custom-call(bf16[128,384]{1,0:T(8,128)(2,1)} %bitcast.30, bf16[128,384]{1,0:T(8,128)(2,1)} %bitcast.31, bf16[384,128]{1,0:T(8,128)(2,1)} %bitcast.32), custom_call_target="tpu_custom_call" | custom-call | tf_op jit(solution)/shard_map/weights/pack/pallas_call | solution.py:217
  8.9 1.6 %collective-permute-start = (bf16[128,1152]{1,0:T(8,128)(2,1)}, bf16[128,1152]{1,0:T(8,128)(2,1)S(1)}, u32[]{:S(2)}, u32[]{:S(2)}) collective-permute-start(bf16[128,1152]{1,0:T(8,128)(2,1)} %pack.1), channel_id=1, source_target_pairs={{0,0},{1,256},{256,1},{257,257},{2,2},{3,258},{258,3},{259,259},{4... | collective-permute-start | bytes 884744 | tf_op jit(solution)/shard_map/weights/ppermute | solution.py:225
  10.6 0.8 copy.14
  11.3 0.8 copy.15
  12.1 0.0 copy-start.1
  12.1 1.0 copy-done.1
  13.2 0.0 copy-start.3
  13.2 0.7 copy-done.3
  13.9 2.3 %dispatch.1 = (bf16[256,3072]{1,0:T(8,128)(2,1)}, bf16[256,256]{1,0:T(8,128)(2,1)S(1)}, bf16[256,512]{1,0:T(8,128)(2,1)S(1)}) custom-call(bf16[128,2048]{1,0:T(8,128)(2,1)S(1)} %bitcast.24, f32[1,2048]{1,0:T(1,128)S(1)} %bitcast.26, s32[128,8]{1,0:T(8,128)S(1)} %bitcast.22, f32[128,8]{1,0:T(8,128)S(1)} %bitcast.23), custom_call_target="tpu_custom_call" | custom-call | flops 536870912 | bytes 4194304 | tf_op jit(solution)/shard_map/dispatch/dispatch/pallas_call | solution.py:228
  16.2 0.0 collective-permute-done
  16.2 0.0 copy-start.4
  16.2 0.7 copy-done.4
  16.9 0.0 all-gather.6.cloned.1.call-update
  16.9 0.0 copy-start.5
  16.9 0.0 copy-start.6
  16.9 21.6 %all-to-all-start = ((bf16[32,8,3072]{2,1,0:T(8,128)(2,1)}), bf16[32,8,3072]{2,1,0:T(8,128)(2,1)S(1)}, u32[]{:S(2)}, u32[]{:S(2)}) async-start(bf16[32,8,3072]{2,1,0:T(8,128)(2,1)} %bitcast.14), calls=%async_computation | async-start | bytes 3145728 | tf_op jit(solution)/shard_map/dispatch/all_to_all | solution.py:243
  38.6 0.0 all-gather.4.cloned.1.call-start
  38.6 0.0 copy-done.5
  38.6 0.0 copy-done.6
  38.7 7.3 %collective-permute-start.1 = (bf16[128,512]{1,0:T(8,128)(2,1)S(1)}, bf16[128,512]{1,0:T(8,128)(2,1)S(1)}, u32[]{:S(2)}, u32[]{:S(2)}) collective-permute-start(bf16[128,512]{1,0:T(8,128)(2,1)S(1)} %constant_dynamic-update-slice_fusion), channel_id=1, source_target_pairs={{0,256},{1,257},{2,258},{3,259},{4,260},{5,261},{6,262},{7,263},{8... | collective-permute-start | bytes 393224 | tf_op jit(solution)/shard_map/keys/ppermute | solution.py:252
  46.0 25.4 %collective-permute-done.1 = bf16[128,512]{1,0:T(8,128)(2,1)S(1)} collective-permute-done((bf16[128,512]{1,0:T(8,128)(2,1)S(1)}, bf16[128,512]{1,0:T(8,128)(2,1)S(1)}, u32[]{:S(2)}, u32[]{:S(2)}) %collective-permute-start.1) | collective-permute-done | bytes 131104 | tf_op jit(solution)/shard_map/keys/ppermute | solution.py:252
  71.3 0.7 pad_maximum_fusion
  72.1 0.0 all-gather.4.cloned.1.call-update
  72.1 2.5 %all-to-all-done = bf16[32,8,3072]{2,1,0:T(8,128)(2,1)S(1)} async-done(((bf16[32,8,3072]{2,1,0:T(8,128)(2,1)}), bf16[32,8,3072]{2,1,0:T(8,128)(2,1)S(1)}, u32[]{:S(2)}, u32[]{:S(2)}) %all-to-all-start) | async-done | bytes 1572896 | tf_op jit(solution)/shard_map/dispatch/all_to_all | solution.py:243
  74.6 0.5 all-gather.6.cloned.1.call-done
  75.1 6.4 %experts.1 = bf16[256,3072]{1,0:T(8,128)(2,1)} custom-call(bf16[256,3072]{1,0:T(8,128)(2,1)S(1)} %bitcast.21, bf16[16,128,1152]{2,1,0:T(8,128)(2,1)} %bitcast.35), custom_call_target="tpu_custom_call" | custom-call | flops 2415919104 | bytes 8388608 | tf_op jit(solution)/shard_map/experts/experts/pallas_call | solution.py:258
  81.5 0.0 copy-start.2
  81.5 11.3 %all-to-all-start.1 = ((bf16[32,8,3072]{2,1,0:T(8,128)(2,1)}), bf16[32,8,3072]{2,1,0:T(8,128)(2,1)S(1)}, u32[]{:S(2)}, u32[]{:S(2)}) async-start(bf16[32,8,3072]{2,1,0:T(8,128)(2,1)} %bitcast.17), calls=%async_computation.1 | async-start | bytes 3145728 | tf_op jit(solution)/shard_map/experts/all_to_all | solution.py:267
  92.8 28.4 %all-gather.4.cloned.1.call-done.kv_ref = bf16[16,128,512]{2,1,0:T(8,128)(2,1)} async-done(((bf16[2,128,512]{2,1,0:T(8,128)(2,1)}), bf16[16,128,512]{2,1,0:T(8,128)(2,1)}) %all-gather.4.cloned.1.call-update) | async-done | bytes 2097168 | tf_op jit(solution)/shard_map/keys/all_gather | solution.py:254
  121.2 0.0 copy-done.2
  121.2 0.0 copy-start
  121.2 1.6 %copy-done = bf16[16,128,512]{2,1,0:T(8,128)(2,1)S(1)} copy-done((bf16[16,128,512]{2,1,0:T(8,128)(2,1)S(1)}, bf16[16,128,512]{2,1,0:T(8,128)(2,1)}, u32[]{:S(2)}) %copy-start) | copy-done | bytes 2097176
  122.8 13.3 %attend.1 = bf16[128,2048]{1,0:T(8,128)(2,1)} custom-call(bf16[128,2048]{1,0:T(8,128)(2,1)S(1)} %bitcast.25, bf16[16,128,512]{2,1,0:T(8,128)(2,1)S(1)} %copy-done, s32[1]{0:T(128)} %bitcast.12.place_ref), custom_call_target="tpu_custom_call" | custom-call | flops 2147483648 | bytes 4194304 | tf_op jit(solution)/shard_map/attend/attend/pallas_call | solution.py:273
  136.2 0.0 all-to-all-done.1
  136.2 1.5 %combine.1 = bf16[128,2048]{1,0:T(8,128)(2,1)} custom-call(bf16[256,3072]{1,0:T(8,128)(2,1)S(1)} %bitcast.20, bf16[256,256]{1,0:T(8,128)(2,1)S(1)} %get-tuple-element.18.mix_a_ref, bf16[256,512]{1,0:T(8,128)(2,1)S(1)} %get-tuple-element.19.mix_b_ref), custom_call_target="tpu_custom_call" | custom-call | flops 536870912 | bytes 3145728 | tf_op jit(solution)/shard_map/combine/combine/pallas_call | solution.py:284
  (2 shorter events, 0.0 us)
Async XLA Ops:
  7.2 67.9 %all-gather.6.cloned.1.call-start = ((), (), s32[]{:S(2)}) async-start(), calls=%async_computation.3 | async-start | bytes 5013504 | tf_op jit(solution)/shard_map/dispatch/all_gather | solution.py:242
  8.9 7.2 %collective-permute-start = (bf16[128,1152]{1,0:T(8,128)(2,1)}, bf16[128,1152]{1,0:T(8,128)(2,1)S(1)}, u32[]{:S(2)}, u32[]{:S(2)}) collective-permute-start(bf16[128,1152]{1,0:T(8,128)(2,1)} %pack.1), channel_id=1, source_target_pairs={{0,0},{1,256},{256,1},{257,257},{2,2},{3,258},{258,3},{259,259},{4... | collective-permute-start | bytes 884744 | tf_op jit(solution)/shard_map/weights/ppermute | solution.py:225
  12.1 1.0 copy-start.1
  13.2 0.7 copy-start.3
  16.2 0.7 copy-start.4
  16.9 21.7 %copy-start.5 = (bf16[1,128,256]{2,1,0:T(8,128)(2,1)S(1)}, bf16[1,128,256]{2,1,0:T(8,128)(2,1)}, u32[]{:S(2)}) copy-start(bf16[1,128,256]{2,1,0:T(8,128)(2,1)} %param.11) | copy-start | bytes 196612
  16.9 21.7 %copy-start.6 = (bf16[1,128,256]{2,1,0:T(8,128)(2,1)S(1)}, bf16[1,128,256]{2,1,0:T(8,128)(2,1)}, u32[]{:S(2)}) copy-start(bf16[1,128,256]{2,1,0:T(8,128)(2,1)} %param.12) | copy-start | bytes 196612
  16.9 57.6 %all-to-all-start = ((bf16[32,8,3072]{2,1,0:T(8,128)(2,1)}), bf16[32,8,3072]{2,1,0:T(8,128)(2,1)S(1)}, u32[]{:S(2)}, u32[]{:S(2)}) async-start(bf16[32,8,3072]{2,1,0:T(8,128)(2,1)} %bitcast.14), calls=%async_computation | async-start | bytes 3145728 | tf_op jit(solution)/shard_map/dispatch/all_to_all | solution.py:243
  38.6 82.7 %all-gather.4.cloned.1.call-start = ((), (), s32[]{:S(2)}) async-start(), calls=%async_computation.2 | async-start | bytes 2359296 | tf_op jit(solution)/shard_map/keys/all_gather | solution.py:254
  38.7 32.7 %collective-permute-start.1 = (bf16[128,512]{1,0:T(8,128)(2,1)S(1)}, bf16[128,512]{1,0:T(8,128)(2,1)S(1)}, u32[]{:S(2)}, u32[]{:S(2)}) collective-permute-start(bf16[128,512]{1,0:T(8,128)(2,1)S(1)} %constant_dynamic-update-slice_fusion), channel_id=1, source_target_pairs={{0,256},{1,257},{2,258},{3,259},{4,260},{5,261},{6,262},{7,263},{8... | collective-permute-start | bytes 393224 | tf_op jit(solution)/shard_map/keys/ppermute | solution.py:252
  81.5 39.7 %copy-start.2 = (bf16[1,128,2048]{2,1,0:T(8,128)(2,1)S(1)}, bf16[1,128,2048]{2,1,0:T(8,128)(2,1)}, u32[]{:S(2)}) copy-start(bf16[1,128,2048]{2,1,0:T(8,128)(2,1)} %param.10) | copy-start | bytes 1572868
  81.5 54.6 %all-to-all-start.1 = ((bf16[32,8,3072]{2,1,0:T(8,128)(2,1)}), bf16[32,8,3072]{2,1,0:T(8,128)(2,1)S(1)}, u32[]{:S(2)}, u32[]{:S(2)}) async-start(bf16[32,8,3072]{2,1,0:T(8,128)(2,1)} %bitcast.17), calls=%async_computation.1 | async-start | bytes 3145728 | tf_op jit(solution)/shard_map/experts/all_to_all | solution.py:267
  121.2 1.6 %copy-start = (bf16[16,128,512]{2,1,0:T(8,128)(2,1)S(1)}, bf16[16,128,512]{2,1,0:T(8,128)(2,1)}, u32[]{:S(2)}) copy-start(bf16[16,128,512]{2,1,0:T(8,128)(2,1)} %all-gather.4.cloned.1.call-done.kv_ref) | copy-start | bytes 6291460
Sparse Core Ops, SparseCore 0:
  17.0 58.0 all-gather.5
  77.7 43.4 all-gather.3

commit v4 on v3

--- a/solution.py
+++ b/solution.py
@@ -19,6 +19,7 @@
 F32 = jnp.float32
 BF16 = jnp.bfloat16
 VMEM = pl.BlockSpec(memory_space=pltpu.VMEM)
+HBM = pl.BlockSpec(memory_space=pltpu.HBM)
 SMEM = pl.BlockSpec(memory_space=pltpu.SMEM)
 
 
@@ -92,7 +93,7 @@
     mix_b_ref[:, slots:] = mix(in_hi)
 
 
-def expert_kernel(hidden_units, x_ref, w_ref, out_ref):
+def expert_kernel(hidden_units, x_ref, w_hbm, out_ref, w_ref, sems):
     rows, cols = x_ref.shape
     width = w_ref.shape[0] * w_ref.shape[1]
     half = width // 2
@@ -100,20 +101,25 @@
     block = w_ref.shape[1]
     count = w_ref.shape[0]
 
-    def part(lo, hi):
-        return w_ref[lo:hi, :, :both].reshape((hi - lo) * block, both)
-
-    low_w = part(0, count // 2)
-    high_w = part(count // 2, count)
-    sums_a = jnp.dot(x_ref[:, :half], low_w, preferred_element_type=F32)
-    sums_a = sums_a + jnp.dot(x_ref[:, half:width], high_w, preferred_element_type=F32)
-    folded = x_ref[:, width:]
+    chunks = sems.shape[0]
+    per = count // chunks
+    copies = []
+    for i in range(chunks):
+        at = pl.ds(i * per, per)
+        copies.append(pltpu.make_async_copy(w_hbm.at[at], w_ref.at[at], sems.at[i]))
+        copies[-1].start()
+    sums_a, folds = None, [None, None]
+    for i in range(chunks):
+        copies[i].wait()
+        piece = w_ref[i * per : (i + 1) * per, :, :both].reshape(per * block, both)
+        start, side = i * per * block, 2 * i // chunks
+        more = jnp.dot(x_ref[:, start : start + per * block], piece, preferred_element_type=F32)
+        sums_a = more if sums_a is None else sums_a + more
+        start = width + start - side * half
+        more = jnp.dot(x_ref[:, start : start + per * block], piece, preferred_element_type=F32)
+        folds[side] = more if folds[side] is None else folds[side] + more
     first = lax.broadcasted_iota(jnp.int32, (rows, both), 0) % LOW < FOLD
-    sums_b = jnp.where(
-        first,
-        jnp.dot(folded, low_w, preferred_element_type=F32),
-        jnp.dot(folded, high_w, preferred_element_type=F32),
-    )
+    sums_b = jnp.where(first, folds[0], folds[1])
     groups = sums_b.reshape(rows // LOW, LOW, both)
     sums_b = (groups + pltpu.roll(groups, FOLD, 1)).reshape(rows, both)
 
@@ -164,13 +170,14 @@
             out_ref[:, start : start + step] = total[:, i * step : (i + 1) * step]
 
 
-def attend_kernel(halves, ring, heads_kv, q_ref, kv_ref, place_ref, out_ref):
+def attend_kernel(halves, ring, heads_kv, q_ref, kv_hbm, place_ref, out_ref, kv_ref, sem):
     tokens, wide = q_ref.shape
-    heads = wide // HD
-    group = heads // heads_kv
-    blocks = kv_ref.shape[0]
-    keys = blocks * kv_ref.shape[1]
-    scale = 1.0 / math.sqrt(HD)
+    group = wide // HD // heads_kv
+    blocks = halves * ring
+    keys = blocks * tokens
+    factor = math.log2(math.e) / math.sqrt(HD)
+    copy = pltpu.make_async_copy(kv_hbm, kv_ref, sem)
+    copy.start()
     lane = lax.broadcasted_iota(jnp.int32, (tokens, keys), 1)
     row = lax.broadcasted_iota(jnp.int32, (tokens, keys), 0)
     block = lane // tokens
@@ -178,23 +185,22 @@
     passed = jnp.where(here == 0, halves, 0)
     side = jnp.where(block % halves == 0, here, passed)
     key_pos = (side * ring + block // halves) * tokens + lane % tokens
-    allowed = key_pos <= row + place_ref[0] * tokens
+    bias = jnp.where(key_pos <= row + place_ref[0] * tokens, 0.0, MASKED)
+    ones = jnp.ones((keys, HD), BF16)
+    copy.wait()
     for g in range(heads_kv):
         key = kv_ref[:, :, g * HD : (g + 1) * HD].reshape(keys, HD)
         value = kv_ref[:, :, (heads_kv + g) * HD : (heads_kv + g + 1) * HD].reshape(keys, HD)
-
-        @pl.loop(0, group)
-        def _(i):
-            at = pl.ds(pl.multiple_of((g * group + i) * HD, HD), HD)
+        value = jnp.concatenate([value, ones], axis=1)
+        for i in range(g * group, (g + 1) * group):
+            at = slice(i * HD, (i + 1) * HD)
             scores = lax.dot_general(
                 q_ref[:, at], key, (((1,), (1,)), ((), ())), preferred_element_type=F32
             )
-            scores = jnp.where(allowed, scores * scale, MASKED)
-            largest = jnp.max(scores, axis=-1, keepdims=True)
-            probs = jnp.exp(scores - largest)
-            total = jnp.sum(probs, axis=-1, keepdims=True)
+            scores = scores * factor + bias
+            probs = jnp.exp2(scores - jnp.max(scores, axis=-1, keepdims=True))
             mixed = jnp.dot(probs.astype(BF16), value, preferred_element_type=F32)
-            out_ref[:, at] = (mixed / total).astype(BF16)
+            out_ref[:, at] = (mixed[:, :HD] / mixed[:, HD:]).astype(BF16)
 
 
 def estimate(flops, bytes_accessed, transcendentals=0):
@@ -258,8 +264,9 @@
         answers = pl.pallas_call(
             functools.partial(expert_kernel, hidden_units),
             out_shape=jax.ShapeDtypeStruct((slots, wide), BF16),
-            in_specs=[VMEM, VMEM],
+            in_specs=[VMEM, HBM],
             out_specs=VMEM,
+            scratch_shapes=[pltpu.VMEM(weights.shape, BF16), pltpu.SemaphoreType.DMA((4,))],
             compiler_params=params,
             cost_estimate=estimate(6 * 512 * 2048 * 384, 8 * 1024 * 1024),
             name="experts",
@@ -273,9 +280,13 @@
         attended = pl.pallas_call(
             functools.partial(attend_kernel, halves, ring, heads_kv),
             out_shape=jax.ShapeDtypeStruct(queries.shape[1:], BF16),
-            in_specs=[VMEM, VMEM, SMEM],
+            in_specs=[VMEM, HBM, SMEM],
             out_specs=VMEM,
-            compiler_params=params,
+            scratch_shapes=[
+                pltpu.VMEM((halves * ring, tokens, 2 * heads_kv * HD), BF16),
+                pltpu.SemaphoreType.DMA,
+            ],
+            compiler_params=pltpu.CompilerParams(vmem_limit_bytes=60 * 1024 * 1024),
             cost_estimate=estimate(4 * 2048 * 128 * 2048, 4 * 1024 * 1024, 16 * 128 * 2048),
             name="attend",
         )(queries[0], kv_all, place)

time: 145 us -> 140 us (0.966)
  Pallas kernels: 25.3 us -> 20.9 us
  local copies, waits for them, and re-layouts: 5.64 us -> 4.05 us
    pallas_call x1, Pallas kernels: 13.3 us -> 9.3 us  [shards(): pl.pallas_call(functools.partial(attend_kernel, halves, ring, heads_kv),...]
    unnamed x17 -> x13, local copies, waits for them, and re-layouts: 5.63 us -> 4.04 us
  transfers between devices with their start and end apart: 6 -> 6, of which waited for: 4 -> 5; matrix products, arithmetic and copies ran while one was open for 2% -> 2% of each run, Pallas kernels for 15% -> 13%
where the time goes in v4:
time: 140 us
  waiting for transfers between devices  58.2 us (42%)
  starting transfers between devices  41.7 us (30%)
  Pallas kernels  20.9 us (15%)
  between operations  14.1 us (10%)
  local copies, waits for them, and re-layouts  4.05 us (3%)
    all_gather x1, waiting for transfers between devices, shards(): kv_all = lax.all_gather(kv_pair, 'y', axis=0, tiled=True)  28.8 us
    ppermute x1, waiting for transfers between devices, shards(): kv_passed = lax.ppermute(kv, 'zh', [(0, 1)])  25.4 us
    all_to_all x1, starting transfers between devices, shards(): lax.all_to_all(outgoing.reshape(owners, LOW, wide), CHIPS, split_axis=0,...  21.6 us
    all_to_all x1, starting transfers between devices, shards(): lax.all_to_all(answers.reshape(owners, LOW, wide), CHIPS, split_axis=0, c...  11.1 us
    pallas_call x1, Pallas kernels, shards(): pl.pallas_call(functools.partial(attend_kernel, halves, ring, heads_kv),...  9.3 us
    ppermute x1, starting transfers between devices, shards(): kv_passed = lax.ppermute(kv, 'zh', [(0, 1)])  7.29 us
    pallas_call x1, Pallas kernels, shards(): pl.pallas_call(functools.partial(expert_kernel, hidden_units), out_shape=...  6.12 us
    unnamed x13, local copies, waits for them, and re-layouts  4.04 us
  transfers between devices with their start and end apart: 6, of which 5 were waited for; matrix products, arithmetic and copies ran while one was open for 2% of the time, Pallas kernels for 13%

profile of v4, /device:TPU:6, one launch (start us, length us, event | category | flops | bytes accessed | tf_op | source)
XLA Modules:
  0.0 139.8 jit_solution(1616209434893589484)
XLA Ops:
  7.2 0.0 all-gather.6.cloned.1.call-start
  7.2 1.7 %pack.1 = bf16[128,1152]{1,0:T(8,128)(2,1)} custom-call(bf16[128,384]{1,0:T(8,128)(2,1)} %bitcast.29, bf16[128,384]{1,0:T(8,128)(2,1)} %bitcast.30, bf16[384,128]{1,0:T(8,128)(2,1)} %bitcast.31), custom_call_target="tpu_custom_call" | custom-call | tf_op jit(solution)/shard_map/weights/pack/pallas_call | solution.py:223
  8.9 1.6 %collective-permute-start = (bf16[128,1152]{1,0:T(8,128)(2,1)}, bf16[128,1152]{1,0:T(8,128)(2,1)S(1)}, u32[]{:S(2)}, u32[]{:S(2)}) collective-permute-start(bf16[128,1152]{1,0:T(8,128)(2,1)} %pack.1), channel_id=1, source_target_pairs={{0,0},{1,256},{256,1},{257,257},{2,2},{3,258},{258,3},{259,259},{4... | collective-permute-start | bytes 884744 | tf_op jit(solution)/shard_map/weights/ppermute | solution.py:231
  10.6 0.8 copy.14
  11.3 0.8 copy.15
  12.1 0.0 copy-start
  12.1 1.0 copy-done
  13.2 0.0 copy-start.1
  13.2 0.7 copy-done.1
  13.9 2.3 %dispatch.1 = (bf16[256,3072]{1,0:T(8,128)(2,1)}, bf16[256,256]{1,0:T(8,128)(2,1)S(1)}, bf16[256,512]{1,0:T(8,128)(2,1)S(1)}) custom-call(bf16[128,2048]{1,0:T(8,128)(2,1)S(1)} %bitcast.24, f32[1,2048]{1,0:T(1,128)S(1)} %bitcast.25, s32[128,8]{1,0:T(8,128)S(1)} %bitcast.22, f32[128,8]{1,0:T(8,128)S(1)} %bitcast.23), custom_call_target="tpu_custom_call" | custom-call | flops 536870912 | bytes 4194304 | tf_op jit(solution)/shard_map/dispatch/dispatch/pallas_call | solution.py:234
  16.2 0.0 collective-permute-done
  16.2 0.0 copy-start.2
  16.2 0.7 copy-done.2
  16.9 0.0 all-gather.6.cloned.1.call-update
  16.9 0.0 copy-start.3
  16.9 0.0 copy-start.4
  16.9 21.6 %all-to-all-start = ((bf16[32,8,3072]{2,1,0:T(8,128)(2,1)}), bf16[32,8,3072]{2,1,0:T(8,128)(2,1)S(1)}, u32[]{:S(2)}, u32[]{:S(2)}) async-start(bf16[32,8,3072]{2,1,0:T(8,128)(2,1)} %bitcast.14), calls=%async_computation | async-start | bytes 3145728 | tf_op jit(solution)/shard_map/dispatch/all_to_all | solution.py:249
  38.6 0.0 all-gather.4.cloned.1.call-start
  38.6 0.0 copy-done.3
  38.6 0.0 copy-done.4
  38.7 7.3 %collective-permute-start.1 = (bf16[128,512]{1,0:T(8,128)(2,1)S(1)}, bf16[128,512]{1,0:T(8,128)(2,1)S(1)}, u32[]{:S(2)}, u32[]{:S(2)}) collective-permute-start(bf16[128,512]{1,0:T(8,128)(2,1)S(1)} %constant_dynamic-update-slice_fusion), channel_id=1, source_target_pairs={{0,256},{1,257},{2,258},{3,259},{4,260},{5,261},{6,262},{7,263},{8... | collective-permute-start | bytes 393224 | tf_op jit(solution)/shard_map/keys/ppermute | solution.py:258
  46.0 25.4 %collective-permute-done.1 = bf16[128,512]{1,0:T(8,128)(2,1)S(1)} collective-permute-done((bf16[128,512]{1,0:T(8,128)(2,1)S(1)}, bf16[128,512]{1,0:T(8,128)(2,1)S(1)}, u32[]{:S(2)}, u32[]{:S(2)}) %collective-permute-start.1) | collective-permute-done | bytes 131104 | tf_op jit(solution)/shard_map/keys/ppermute | solution.py:258
  71.3 0.7 pad_maximum_fusion
  72.1 0.0 all-gather.4.cloned.1.call-update
  72.1 2.5 %all-to-all-done = bf16[32,8,3072]{2,1,0:T(8,128)(2,1)S(1)} async-done(((bf16[32,8,3072]{2,1,0:T(8,128)(2,1)}), bf16[32,8,3072]{2,1,0:T(8,128)(2,1)S(1)}, u32[]{:S(2)}, u32[]{:S(2)}) %all-to-all-start) | async-done | bytes 1572896 | tf_op jit(solution)/shard_map/dispatch/all_to_all | solution.py:249
  74.6 0.5 all-gather.6.cloned.1.call-done
  75.1 6.1 %experts.1 = bf16[256,3072]{1,0:T(8,128)(2,1)} custom-call(bf16[256,3072]{1,0:T(8,128)(2,1)S(1)} %bitcast.21, bf16[16,128,1152]{2,1,0:T(8,128)(2,1)} %bitcast.34), custom_call_target="tpu_custom_call" | custom-call | flops 2415919104 | bytes 8388608 | tf_op jit(solution)/shard_map/experts/experts/pallas_call | solution.py:264
  81.2 11.1 %all-to-all-start.1 = ((bf16[32,8,3072]{2,1,0:T(8,128)(2,1)}), bf16[32,8,3072]{2,1,0:T(8,128)(2,1)S(1)}, u32[]{:S(2)}, u32[]{:S(2)}) async-start(bf16[32,8,3072]{2,1,0:T(8,128)(2,1)} %bitcast.17), calls=%async_computation.1 | async-start | bytes 3145728 | tf_op jit(solution)/shard_map/experts/all_to_all | solution.py:274
  92.4 28.8 %all-gather.4.cloned.1.call-done.kv_hbm = bf16[16,128,512]{2,1,0:T(8,128)(2,1)} async-done(((bf16[2,128,512]{2,1,0:T(8,128)(2,1)}), bf16[16,128,512]{2,1,0:T(8,128)(2,1)}) %all-gather.4.cloned.1.call-update) | async-done | bytes 2097168 | tf_op jit(solution)/shard_map/keys/all_gather | solution.py:260
  121.2 9.3 %attend.1 = bf16[128,2048]{1,0:T(8,128)(2,1)} custom-call(bf16[128,2048]{1,0:T(8,128)(2,1)} %bitcast.35, bf16[16,128,512]{2,1,0:T(8,128)(2,1)} %all-gather.4.cloned.1.call-done.kv_hbm, s32[1]{0:T(128)} %bitcast.12.place_ref), custom_call_target="tpu_custom_call" | custom-call | flops 2147483648 | bytes 4194304 | tf_op jit(solution)/shard_map/attend/attend/pallas_call | solution.py:280
  130.5 0.9 all-to-all-done.1
  131.4 1.5 %combine.1 = bf16[128,2048]{1,0:T(8,128)(2,1)} custom-call(bf16[256,3072]{1,0:T(8,128)(2,1)S(1)} %bitcast.20, bf16[256,256]{1,0:T(8,128)(2,1)S(1)} %get-tuple-element.18.mix_a_ref, bf16[256,512]{1,0:T(8,128)(2,1)S(1)} %get-tuple-element.19.mix_b_ref), custom_call_target="tpu_custom_call" | custom-call | flops 536870912 | bytes 3145728 | tf_op jit(solution)/shard_map/combine/combine/pallas_call | solution.py:295
  (2 shorter events, 0.0 us)
Async XLA Ops:
  7.2 67.9 %all-gather.6.cloned.1.call-start = ((), (), s32[]{:S(2)}) async-start(), calls=%async_computation.3 | async-start | bytes 5013504 | tf_op jit(solution)/shard_map/dispatch/all_gather | solution.py:248
  8.9 7.2 %collective-permute-start = (bf16[128,1152]{1,0:T(8,128)(2,1)}, bf16[128,1152]{1,0:T(8,128)(2,1)S(1)}, u32[]{:S(2)}, u32[]{:S(2)}) collective-permute-start(bf16[128,1152]{1,0:T(8,128)(2,1)} %pack.1), channel_id=1, source_target_pairs={{0,0},{1,256},{256,1},{257,257},{2,2},{3,258},{258,3},{259,259},{4... | collective-permute-start | bytes 884744 | tf_op jit(solution)/shard_map/weights/ppermute | solution.py:231
  12.1 1.0 copy-start
  13.2 0.7 copy-start.1
  16.2 0.7 copy-start.2
  16.9 21.7 %copy-start.3 = (bf16[1,128,256]{2,1,0:T(8,128)(2,1)S(1)}, bf16[1,128,256]{2,1,0:T(8,128)(2,1)}, u32[]{:S(2)}) copy-start(bf16[1,128,256]{2,1,0:T(8,128)(2,1)} %param.11) | copy-start | bytes 196612
  16.9 21.7 %copy-start.4 = (bf16[1,128,256]{2,1,0:T(8,128)(2,1)S(1)}, bf16[1,128,256]{2,1,0:T(8,128)(2,1)}, u32[]{:S(2)}) copy-start(bf16[1,128,256]{2,1,0:T(8,128)(2,1)} %param.12) | copy-start | bytes 196612
  16.9 57.6 %all-to-all-start = ((bf16[32,8,3072]{2,1,0:T(8,128)(2,1)}), bf16[32,8,3072]{2,1,0:T(8,128)(2,1)S(1)}, u32[]{:S(2)}, u32[]{:S(2)}) async-start(bf16[32,8,3072]{2,1,0:T(8,128)(2,1)} %bitcast.14), calls=%async_computation | async-start | bytes 3145728 | tf_op jit(solution)/shard_map/dispatch/all_to_all | solution.py:249
  38.6 82.7 %all-gather.4.cloned.1.call-start = ((), (), s32[]{:S(2)}) async-start(), calls=%async_computation.2 | async-start | bytes 2359296 | tf_op jit(solution)/shard_map/keys/all_gather | solution.py:260
  38.7 32.7 %collective-permute-start.1 = (bf16[128,512]{1,0:T(8,128)(2,1)S(1)}, bf16[128,512]{1,0:T(8,128)(2,1)S(1)}, u32[]{:S(2)}, u32[]{:S(2)}) collective-permute-start(bf16[128,512]{1,0:T(8,128)(2,1)S(1)} %constant_dynamic-update-slice_fusion), channel_id=1, source_target_pairs={{0,256},{1,257},{2,258},{3,259},{4,260},{5,261},{6,262},{7,263},{8... | collective-permute-start | bytes 393224 | tf_op jit(solution)/shard_map/keys/ppermute | solution.py:258
  81.2 50.2 %all-to-all-start.1 = ((bf16[32,8,3072]{2,1,0:T(8,128)(2,1)}), bf16[32,8,3072]{2,1,0:T(8,128)(2,1)S(1)}, u32[]{:S(2)}, u32[]{:S(2)}) async-start(bf16[32,8,3072]{2,1,0:T(8,128)(2,1)} %bitcast.17), calls=%async_computation.1 | async-start | bytes 3145728 | tf_op jit(solution)/shard_map/experts/all_to_all | solution.py:274
Sparse Core Ops, SparseCore 0:
  17.0 58.0 all-gather.5
  77.7 43.4 all-gather.3

commit v5 on v4

--- a/solution.py
+++ b/solution.py
@@ -31,11 +31,15 @@
         out_ref[:, (2 * units + j * rows) : (2 * units + (j + 1) * rows)] = down_ref[j * rows : (j + 1) * rows, :]
 
 
+def host_place(z, core, depth, halves):
+    return (z + depth // 2 + core * depth) % (depth * halves)
+
+
 def natural_block(place, cores, ring):
     return (place % cores) * ring + place // cores
 
 
-def dispatch_kernel(halves, cores, ring, owners, x_ref, gain_ref, ids_ref, gates_ref, out_ref, mix_a_ref, mix_b_ref):
+def dispatch_kernel(halves, depth, cores, ring, owners, x_ref, gain_ref, ids_ref, gates_ref, out_ref, mix_a_ref, mix_b_ref):
     tokens, width = x_ref.shape
     slots = owners * LOW
     half = width // 2
@@ -50,8 +54,9 @@
 
     lane = lax.broadcasted_iota(jnp.int32, (tokens, slots), 1)
     chip = lane // LOW
-    per_half = owners // halves
-    expert = chip % per_half * halves + chip // per_half
+    across = owners // (halves * depth)
+    turn = (chip // across + halves * depth - depth // 2) % (halves * depth)
+    expert = (turn % depth * across + chip % across) * cores + turn // depth
     place = lane % LOW
     ids = ids_ref[...]
     gates = gates_ref[...]
@@ -214,6 +219,7 @@
     heads_kv = key_rows.shape[2] // HD
     hidden_units = w_gate.shape[2]
     halves, ring, cores = lax.axis_size("zh"), lax.axis_size("y"), lax.axis_size("c")
+    depth = lax.axis_size("zl")
     owners = lax.axis_size(DP)
     slots = owners * LOW
     wide = width + width // 2
@@ -227,12 +233,17 @@
             out_specs=VMEM,
             name="pack",
         )(w_gate[0], w_up[0], w_down[0])
-        swap = [(h * cores + c, c * cores + h) for h in range(halves) for c in range(cores)]
-        part = lax.ppermute(packed, ("zh", "c"), swap)
+        route = []
+        for h in range(halves):
+            for z in range(depth):
+                for c in range(cores):
+                    to = host_place(z, c, depth, halves)
+                    route.append(((h * depth + z) * cores + c, to * cores + h))
+        part = lax.ppermute(packed, ("zh", "zl", "c"), route)
     with jax.named_scope("dispatch"):
         ids, _ = lax.optimization_barrier((expert_ids[0], packed))
         outgoing, mix_a, mix_b = pl.pallas_call(
-            functools.partial(dispatch_kernel, halves, cores, ring, owners),
+            functools.partial(dispatch_kernel, halves, depth, cores, ring, owners),
             out_shape=(
                 jax.ShapeDtypeStruct((slots, wide), BF16),
                 jax.ShapeDtypeStruct((2 * tokens, slots), BF16),

time: 140 us -> 140 us (level)
  starting transfers between devices: 41.7 us -> 39.8 us
    all_to_all x1, starting transfers between devices: 21.6 us -> 14.4 us  [shards(): lax.all_to_all(outgoing.reshape(owners, LOW, wide), CHIPS, split_axis=0,...]
    ppermute x1, starting transfers between devices: 1.61 us -> 6.08 us  [shards(): part = lax.ppermute(packed, ('zh', 'zl', 'c'), route)]
    ppermute x1, waiting for transfers between devices: 0.01 us -> 1.59 us  [shards(): part = lax.ppermute(packed, ('zh', 'zl', 'c'), route)]
    ppermute x1, waiting for transfers between devices: 25.4 us -> 26.9 us  [shards(): kv_passed = lax.ppermute(kv, 'zh', [(0, 1)])]
  transfers between devices with their start and end apart: 6 -> 6, of which waited for: 5 -> 4; matrix products, arithmetic and copies ran while one was open for 2% -> 2% of each run, Pallas kernels for 13% -> 13%
where the time goes in v5:
time: 140 us; the launch traced here: 139 us
  waiting for transfers between devices  59.5 us (42%)
  starting transfers between devices  39.8 us (28%)
  Pallas kernels  21 us (15%)
  between operations  14.2 us (10%)
  local copies, waits for them, and re-layouts  4.05 us (3%)
    all_gather x1, waiting for transfers between devices, shards(): kv_all = lax.all_gather(kv_pair, 'y', axis=0, tiled=True)  28.9 us
    ppermute x1, waiting for transfers between devices, shards(): kv_passed = lax.ppermute(kv, 'zh', [(0, 1)])  26.9 us
    all_to_all x1, starting transfers between devices, shards(): lax.all_to_all(outgoing.reshape(owners, LOW, wide), CHIPS, split_axis=0,...  14.4 us
    all_to_all x1, starting transfers between devices, shards(): lax.all_to_all(answers.reshape(owners, LOW, wide), CHIPS, split_axis=0, c...  12 us
    pallas_call x1, Pallas kernels, shards(): pl.pallas_call(functools.partial(attend_kernel, halves, ring, heads_kv),...  9.3 us
    ppermute x1, starting transfers between devices, shards(): kv_passed = lax.ppermute(kv, 'zh', [(0, 1)])  7.29 us
    pallas_call x1, Pallas kernels, shards(): pl.pallas_call(functools.partial(expert_kernel, hidden_units), out_shape=...  6.12 us
    ppermute x1, starting transfers between devices, shards(): part = lax.ppermute(packed, ('zh', 'zl', 'c'), route)  6.08 us
  transfers between devices with their start and end apart: 6, of which 4 were waited for; matrix products, arithmetic and copies ran while one was open for 2% of the time, Pallas kernels for 13%

profile of v5, /device:TPU:6, one launch (start us, length us, event | category | flops | bytes accessed | tf_op | source)
XLA Modules:
  0.0 139.2 jit_solution(763119374824102252)
XLA Ops:
  7.2 0.0 all-gather.6.cloned.1.call-start
  7.2 1.7 %pack.1 = bf16[128,1152]{1,0:T(8,128)(2,1)} custom-call(bf16[128,384]{1,0:T(8,128)(2,1)} %bitcast.29, bf16[128,384]{1,0:T(8,128)(2,1)} %bitcast.30, bf16[384,128]{1,0:T(8,128)(2,1)} %bitcast.31), custom_call_target="tpu_custom_call" | custom-call | tf_op jit(solution)/shard_map/weights/pack/pallas_call | solution.py:229
  8.9 6.1 %collective-permute-start = (bf16[128,1152]{1,0:T(8,128)(2,1)}, bf16[128,1152]{1,0:T(8,128)(2,1)S(1)}, u32[]{:S(2)}, u32[]{:S(2)}) collective-permute-start(bf16[128,1152]{1,0:T(8,128)(2,1)} %pack.1), channel_id=1, source_target_pairs={{0,16},{1,272},{8,24},{9,280},{16,256},{17,0},{24,264},{25,8},{256... | collective-permute-start | bytes 884744 | tf_op jit(solution)/shard_map/weights/ppermute | solution.py:242
  15.0 0.8 copy.14
  15.8 0.8 copy.15
  16.6 0.0 copy-start
  16.6 1.0 copy-done
  17.6 0.0 copy-start.1
  17.7 0.7 copy-done.1
  18.3 2.3 %dispatch.1 = (bf16[256,3072]{1,0:T(8,128)(2,1)}, bf16[256,256]{1,0:T(8,128)(2,1)S(1)}, bf16[256,512]{1,0:T(8,128)(2,1)S(1)}) custom-call(bf16[128,2048]{1,0:T(8,128)(2,1)S(1)} %bitcast.24, f32[1,2048]{1,0:T(1,128)S(1)} %bitcast.25, s32[128,8]{1,0:T(8,128)S(1)} %bitcast.22, f32[128,8]{1,0:T(8,128)S(1)} %bitcast.23), custom_call_target="tpu_custom_call" | custom-call | flops 536870912 | bytes 4194304 | tf_op jit(solution)/shard_map/dispatch/dispatch/pallas_call | solution.py:245
  20.6 1.6 %collective-permute-done = bf16[128,1152]{1,0:T(8,128)(2,1)S(1)} collective-permute-done((bf16[128,1152]{1,0:T(8,128)(2,1)}, bf16[128,1152]{1,0:T(8,128)(2,1)S(1)}, u32[]{:S(2)}, u32[]{:S(2)}) %collective-permute-start) | collective-permute-done | bytes 294944 | tf_op jit(solution)/shard_map/weights/ppermute | solution.py:242
  22.2 0.0 copy-start.2
  22.2 0.7 copy-done.2
  22.9 0.0 all-gather.6.cloned.1.call-update
  23.0 0.0 copy-start.3
  23.0 0.0 copy-start.4
  23.0 14.4 %all-to-all-start = ((bf16[32,8,3072]{2,1,0:T(8,128)(2,1)}), bf16[32,8,3072]{2,1,0:T(8,128)(2,1)S(1)}, u32[]{:S(2)}, u32[]{:S(2)}) async-start(bf16[32,8,3072]{2,1,0:T(8,128)(2,1)} %bitcast.14), calls=%async_computation | async-start | bytes 3145728 | tf_op jit(solution)/shard_map/dispatch/all_to_all | solution.py:260
  37.4 0.0 all-gather.4.cloned.1.call-start
  37.4 0.0 copy-done.3
  37.4 0.0 copy-done.4
  37.5 7.3 %collective-permute-start.1 = (bf16[128,512]{1,0:T(8,128)(2,1)S(1)}, bf16[128,512]{1,0:T(8,128)(2,1)S(1)}, u32[]{:S(2)}, u32[]{:S(2)}) collective-permute-start(bf16[128,512]{1,0:T(8,128)(2,1)S(1)} %constant_dynamic-update-slice_fusion), channel_id=1, source_target_pairs={{0,256},{1,257},{2,258},{3,259},{4,260},{5,261},{6,262},{7,263},{8... | collective-permute-start | bytes 393224 | tf_op jit(solution)/shard_map/keys/ppermute | solution.py:269
  44.8 26.9 %collective-permute-done.1 = bf16[128,512]{1,0:T(8,128)(2,1)S(1)} collective-permute-done((bf16[128,512]{1,0:T(8,128)(2,1)S(1)}, bf16[128,512]{1,0:T(8,128)(2,1)S(1)}, u32[]{:S(2)}, u32[]{:S(2)}) %collective-permute-start.1) | collective-permute-done | bytes 131104 | tf_op jit(solution)/shard_map/keys/ppermute | solution.py:269
  71.7 0.7 pad_maximum_fusion
  72.4 0.0 all-gather.4.cloned.1.call-update
  72.4 2.1 %all-to-all-done = bf16[32,8,3072]{2,1,0:T(8,128)(2,1)S(1)} async-done(((bf16[32,8,3072]{2,1,0:T(8,128)(2,1)}), bf16[32,8,3072]{2,1,0:T(8,128)(2,1)S(1)}, u32[]{:S(2)}, u32[]{:S(2)}) %all-to-all-start) | async-done | bytes 1572896 | tf_op jit(solution)/shard_map/dispatch/all_to_all | solution.py:260
  74.5 0.0 all-gather.6.cloned.1.call-done
  74.5 6.1 %experts.1 = bf16[256,3072]{1,0:T(8,128)(2,1)} custom-call(bf16[256,3072]{1,0:T(8,128)(2,1)S(1)} %bitcast.21, bf16[16,128,1152]{2,1,0:T(8,128)(2,1)} %bitcast.34), custom_call_target="tpu_custom_call" | custom-call | flops 2415919104 | bytes 8388608 | tf_op jit(solution)/shard_map/experts/experts/pallas_call | solution.py:275
  80.7 12.0 %all-to-all-start.1 = ((bf16[32,8,3072]{2,1,0:T(8,128)(2,1)}), bf16[32,8,3072]{2,1,0:T(8,128)(2,1)S(1)}, u32[]{:S(2)}, u32[]{:S(2)}) async-start(bf16[32,8,3072]{2,1,0:T(8,128)(2,1)} %bitcast.17), calls=%async_computation.1 | async-start | bytes 3145728 | tf_op jit(solution)/shard_map/experts/all_to_all | solution.py:285
  92.7 28.9 %all-gather.4.cloned.1.call-done.kv_hbm = bf16[16,128,512]{2,1,0:T(8,128)(2,1)} async-done(((bf16[2,128,512]{2,1,0:T(8,128)(2,1)}), bf16[16,128,512]{2,1,0:T(8,128)(2,1)}) %all-gather.4.cloned.1.call-update) | async-done | bytes 2097168 | tf_op jit(solution)/shard_map/keys/all_gather | solution.py:271
  121.5 9.3 %attend.1 = bf16[128,2048]{1,0:T(8,128)(2,1)} custom-call(bf16[128,2048]{1,0:T(8,128)(2,1)} %bitcast.35, bf16[16,128,512]{2,1,0:T(8,128)(2,1)} %all-gather.4.cloned.1.call-done.kv_hbm, s32[1]{0:T(128)} %bitcast.12.place_ref), custom_call_target="tpu_custom_call" | custom-call | flops 2147483648 | bytes 4194304 | tf_op jit(solution)/shard_map/attend/attend/pallas_call | solution.py:291
  130.8 0.0 all-to-all-done.1
  130.9 1.5 %combine.1 = bf16[128,2048]{1,0:T(8,128)(2,1)} custom-call(bf16[256,3072]{1,0:T(8,128)(2,1)S(1)} %bitcast.20, bf16[256,256]{1,0:T(8,128)(2,1)S(1)} %get-tuple-element.18.mix_a_ref, bf16[256,512]{1,0:T(8,128)(2,1)S(1)} %get-tuple-element.19.mix_b_ref), custom_call_target="tpu_custom_call" | custom-call | flops 536870912 | bytes 3145728 | tf_op jit(solution)/shard_map/combine/combine/pallas_call | solution.py:306
  (2 shorter events, 0.0 us)
Async XLA Ops:
  7.2 67.4 %all-gather.6.cloned.1.call-start = ((), (), s32[]{:S(2)}) async-start(), calls=%async_computation.3 | async-start | bytes 5013504 | tf_op jit(solution)/shard_map/dispatch/all_gather | solution.py:259
  8.9 13.3 %collective-permute-start = (bf16[128,1152]{1,0:T(8,128)(2,1)}, bf16[128,1152]{1,0:T(8,128)(2,1)S(1)}, u32[]{:S(2)}, u32[]{:S(2)}) collective-permute-start(bf16[128,1152]{1,0:T(8,128)(2,1)} %pack.1), channel_id=1, source_target_pairs={{0,16},{1,272},{8,24},{9,280},{16,256},{17,0},{24,264},{25,8},{256... | collective-permute-start | bytes 884744 | tf_op jit(solution)/shard_map/weights/ppermute | solution.py:242
  16.6 1.0 copy-start
  17.6 0.7 copy-start.1
  22.2 0.7 copy-start.2
  23.0 14.4 %copy-start.3 = (bf16[1,128,256]{2,1,0:T(8,128)(2,1)S(1)}, bf16[1,128,256]{2,1,0:T(8,128)(2,1)}, u32[]{:S(2)}) copy-start(bf16[1,128,256]{2,1,0:T(8,128)(2,1)} %param.11) | copy-start | bytes 196612
  23.0 14.5 %copy-start.4 = (bf16[1,128,256]{2,1,0:T(8,128)(2,1)S(1)}, bf16[1,128,256]{2,1,0:T(8,128)(2,1)}, u32[]{:S(2)}) copy-start(bf16[1,128,256]{2,1,0:T(8,128)(2,1)} %param.12) | copy-start | bytes 196612
  23.0 51.5 %all-to-all-start = ((bf16[32,8,3072]{2,1,0:T(8,128)(2,1)}), bf16[32,8,3072]{2,1,0:T(8,128)(2,1)S(1)}, u32[]{:S(2)}, u32[]{:S(2)}) async-start(bf16[32,8,3072]{2,1,0:T(8,128)(2,1)} %bitcast.14), calls=%async_computation | async-start | bytes 3145728 | tf_op jit(solution)/shard_map/dispatch/all_to_all | solution.py:260
  37.4 84.2 %all-gather.4.cloned.1.call-start = ((), (), s32[]{:S(2)}) async-start(), calls=%async_computation.2 | async-start | bytes 2359296 | tf_op jit(solution)/shard_map/keys/all_gather | solution.py:271
  37.5 34.2 %collective-permute-start.1 = (bf16[128,512]{1,0:T(8,128)(2,1)S(1)}, bf16[128,512]{1,0:T(8,128)(2,1)S(1)}, u32[]{:S(2)}, u32[]{:S(2)}) collective-permute-start(bf16[128,512]{1,0:T(8,128)(2,1)S(1)} %constant_dynamic-update-slice_fusion), channel_id=1, source_target_pairs={{0,256},{1,257},{2,258},{3,259},{4,260},{5,261},{6,262},{7,263},{8... | collective-permute-start | bytes 393224 | tf_op jit(solution)/shard_map/keys/ppermute | solution.py:269
  80.7 50.2 %all-to-all-start.1 = ((bf16[32,8,3072]{2,1,0:T(8,128)(2,1)}), bf16[32,8,3072]{2,1,0:T(8,128)(2,1)S(1)}, u32[]{:S(2)}, u32[]{:S(2)}) async-start(bf16[32,8,3072]{2,1,0:T(8,128)(2,1)} %bitcast.17), calls=%async_computation.1 | async-start | bytes 3145728 | tf_op jit(solution)/shard_map/experts/all_to_all | solution.py:285
Sparse Core Ops, SparseCore 0:
  23.1 50.7 all-gather.5
  76.6 44.9 all-gather.3

commit v6 on v5

--- a/solution.py
+++ b/solution.py
@@ -23,12 +23,24 @@
 SMEM = pl.BlockSpec(memory_space=pltpu.SMEM)
 
 
-def pack_kernel(gate_ref, up_ref, down_ref, out_ref):
+def pack_kernel(gate_ref, up_ref, down_ref, out_ref, sems):
     rows, units = gate_ref.shape
-    out_ref[:, :units] = gate_ref[...]
-    out_ref[:, units : 2 * units] = up_ref[...]
+    copies = [
+        pltpu.make_async_copy(gate_ref, out_ref.at[:, pl.ds(0, units)], sems.at[0]),
+        pltpu.make_async_copy(up_ref, out_ref.at[:, pl.ds(units, units)], sems.at[1]),
+    ]
     for j in range(units // rows):
-        out_ref[:, (2 * units + j * rows) : (2 * units + (j + 1) * rows)] = down_ref[j * rows : (j + 1) * rows, :]
+        copies.append(
+            pltpu.make_async_copy(
+                down_ref.at[pl.ds(j * rows, rows)],
+                out_ref.at[:, pl.ds(2 * units + j * rows, rows)],
+                sems.at[2 + j],
+            )
+        )
+    for copy in copies:
+        copy.start()
+    for copy in copies:
+        copy.wait()
 
 
 def host_place(z, core, depth, halves):
@@ -58,8 +70,8 @@
     turn = (chip // across + halves * depth - depth // 2) % (halves * depth)
     expert = (turn % depth * across + chip % across) * cores + turn // depth
     place = lane % LOW
-    ids = ids_ref[...]
-    gates = gates_ref[...]
+    ids = ids_ref[...].T
+    gates = gates_ref[...].T
     hot = jnp.zeros((tokens, slots), F32)
     gate = jnp.zeros((tokens, slots), F32)
     for k in range(ids.shape[1]):
@@ -175,14 +187,18 @@
             out_ref[:, start : start + step] = total[:, i * step : (i + 1) * step]
 
 
-def attend_kernel(halves, ring, heads_kv, q_ref, kv_hbm, place_ref, out_ref, kv_ref, sem):
+def attend_kernel(halves, ring, heads_kv, q_ref, kv_hbm, place_ref, out_ref, kv_ref, sems):
     tokens, wide = q_ref.shape
     group = wide // HD // heads_kv
     blocks = halves * ring
     keys = blocks * tokens
     factor = math.log2(math.e) / math.sqrt(HD)
-    copy = pltpu.make_async_copy(kv_hbm, kv_ref, sem)
-    copy.start()
+    kind = heads_kv * HD
+    copies = []
+    for i in range(2):
+        at = (slice(None), slice(None), pl.ds(i * kind, kind))
+        copies.append(pltpu.make_async_copy(kv_hbm.at[at], kv_ref.at[at], sems.at[i]))
+        copies[i].start()
     lane = lax.broadcasted_iota(jnp.int32, (tokens, keys), 1)
     row = lax.broadcasted_iota(jnp.int32, (tokens, keys), 0)
     block = lane // tokens
@@ -192,11 +208,9 @@
     key_pos = (side * ring + block // halves) * tokens + lane % tokens
     bias = jnp.where(key_pos <= row + place_ref[0] * tokens, 0.0, MASKED)
     ones = jnp.ones((keys, HD), BF16)
-    copy.wait()
+    copies[0].wait()
     for g in range(heads_kv):
         key = kv_ref[:, :, g * HD : (g + 1) * HD].reshape(keys, HD)
-        value = kv_ref[:, :, (heads_kv + g) * HD : (heads_kv + g + 1) * HD].reshape(keys, HD)
-        value = jnp.concatenate([value, ones], axis=1)
         for i in range(g * group, (g + 1) * group):
             at = slice(i * HD, (i + 1) * HD)
             scores = lax.dot_general(
@@ -204,6 +218,11 @@
             )
             scores = scores * factor + bias
             probs = jnp.exp2(scores - jnp.max(scores, axis=-1, keepdims=True))
+            if i == 0:
+                copies[1].wait()
+            if i == g * group:
+                value = kv_ref[:, :, kind + g * HD : kind + (g + 1) * HD].reshape(keys, HD)
+                value = jnp.concatenate([value, ones], axis=1)
             mixed = jnp.dot(probs.astype(BF16), value, preferred_element_type=F32)
             out_ref[:, at] = (mixed[:, :HD] / mixed[:, HD:]).astype(BF16)
 
@@ -229,8 +248,9 @@
         packed = pl.pallas_call(
             pack_kernel,
             out_shape=jax.ShapeDtypeStruct((w_gate.shape[1], 3 * hidden_units), BF16),
-            in_specs=[VMEM] * 3,
-            out_specs=VMEM,
+            in_specs=[HBM] * 3,
+            out_specs=HBM,
+            scratch_shapes=[pltpu.SemaphoreType.DMA((2 + hidden_units // tokens,))],
             name="pack",
         )(w_gate[0], w_up[0], w_down[0])
         route = []
@@ -241,7 +261,7 @@
                     route.append(((h * depth + z) * cores + c, to * cores + h))
         part = lax.ppermute(packed, ("zh", "zl", "c"), route)
     with jax.named_scope("dispatch"):
-        ids, _ = lax.optimization_barrier((expert_ids[0], packed))
+        ids, _ = lax.optimization_barrier((expert_ids[0].T, packed))
         outgoing, mix_a, mix_b = pl.pallas_call(
             functools.partial(dispatch_kernel, halves, depth, cores, ring, owners),
             out_shape=(
@@ -251,11 +271,11 @@
             ),
             in_specs=[VMEM] * 4,
             out_specs=(VMEM,) * 3,
-            compiler_params=params,
+            compiler_params=pltpu.CompilerParams(vmem_limit_bytes=65200 * 1024),
             cost_estimate=estimate(4 * 256 * 256 * 2048, 4 * 1024 * 1024),
             name="dispatch",
-        )(stream[0], norm_gain[None, :], ids, gate_values[0])
-        part, outgoing = lax.optimization_barrier((part, outgoing))
+        )(stream[0], norm_gain[None, :], ids, gate_values[0].T)
+        part, _ = lax.optimization_barrier((part, outgoing))
         weights = lax.all_gather(part, ("y", "c"), axis=0)
         arrived = lax.all_to_all(
             outgoing.reshape(owners, LOW, wide), CHIPS, split_axis=0, concat_axis=0, tiled=True
@@ -295,7 +315,7 @@
             out_specs=VMEM,
             scratch_shapes=[
                 pltpu.VMEM((halves * ring, tokens, 2 * heads_kv * HD), BF16),
-                pltpu.SemaphoreType.DMA,
+                pltpu.SemaphoreType.DMA((2,)),
             ],
             compiler_params=pltpu.CompilerParams(vmem_limit_bytes=60 * 1024 * 1024),
             cost_estimate=estimate(4 * 2048 * 128 * 2048, 4 * 1024 * 1024, 16 * 128 * 2048),

time: 140 us -> 148 us (1.057)
  Pallas kernels: 21 us -> 30.4 us
  local copies, waits for them, and re-layouts: 4.05 us -> 0.03 us
  waiting for transfers between devices: 59.5 us -> 61.8 us
    pallas_call x1, Pallas kernels: 1.74 us -> 10.1 us  [shards(): pl.pallas_call(pack_kernel, out_shape=jax.ShapeDtypeStruct((w_gate.shape[...]
    unnamed x13 -> x9, local copies, waits for them, and re-layouts: 4.04 us -> 0.03 us
    ppermute x1, waiting for transfers between devices: 1.59 us -> 3.87 us  [shards(): part = lax.ppermute(packed, ('zh', 'zl', 'c'), route)]
  transfers between devices with their start and end apart: 6 -> 6, of which waited for: 4 -> 4; matrix products, arithmetic and copies ran while one was open for 2% -> 1% of each run, Pallas kernels for 13% -> 13%
where the time goes in v6:
time: 148 us; the launch traced here: 147 us
  waiting for transfers between devices  61.8 us (42%)
  starting transfers between devices  39.9 us (27%)
  Pallas kernels  30.4 us (21%)
  between operations  14.2 us (10%)
    all_gather x1, waiting for transfers between devices, shards(): kv_all = lax.all_gather(kv_pair, 'y', axis=0, tiled=True)  28.8 us
    ppermute x1, waiting for transfers between devices, shards(): kv_passed = lax.ppermute(kv, 'zh', [(0, 1)])  26.9 us
    all_to_all x1, starting transfers between devices, shards(): lax.all_to_all(outgoing.reshape(owners, LOW, wide), CHIPS, split_axis=0,...  14.4 us
    all_to_all x1, starting transfers between devices, shards(): lax.all_to_all(answers.reshape(owners, LOW, wide), CHIPS, split_axis=0, c...  12 us
    pallas_call x1, Pallas kernels, shards(): pl.pallas_call(pack_kernel, out_shape=jax.ShapeDtypeStruct((w_gate.shape[...  10.1 us
    pallas_call x1, Pallas kernels, shards(): pl.pallas_call(functools.partial(attend_kernel, halves, ring, heads_kv),...  9.3 us
    ppermute x1, starting transfers between devices, shards(): kv_passed = lax.ppermute(kv, 'zh', [(0, 1)])  7.29 us
    pallas_call x1, Pallas kernels, shards(): pl.pallas_call(functools.partial(expert_kernel, hidden_units), out_shape=...  6.12 us
  transfers between devices with their start and end apart: 6, of which 4 were waited for; matrix products, arithmetic and copies ran while one was open for 1% of the time, Pallas kernels for 13%

profile of v6, /device:TPU:6, one launch (start us, length us, event | category | flops | bytes accessed | tf_op | source)
XLA Modules:
  0.0 147.0 jit_solution(14854797394566125121)
XLA Ops:
  7.2 0.0 all-gather.6.cloned.1.call-start
  7.2 10.1 %pack.1 = bf16[128,1152]{1,0:T(8,128)(2,1)} custom-call(bf16[128,384]{1,0:T(8,128)(2,1)} %bitcast.30, bf16[128,384]{1,0:T(8,128)(2,1)} %bitcast.31, bf16[384,128]{1,0:T(8,128)(2,1)} %bitcast.32), custom_call_target="tpu_custom_call" | custom-call | tf_op jit(solution)/shard_map/weights/pack/pallas_call | solution.py:248
  17.3 6.1 %collective-permute-start = (bf16[128,1152]{1,0:T(8,128)(2,1)}, bf16[128,1152]{1,0:T(8,128)(2,1)}, u32[]{:S(2)}, u32[]{:S(2)}) collective-permute-start(bf16[128,1152]{1,0:T(8,128)(2,1)} %pack.1), channel_id=1, source_target_pairs={{0,16},{1,272},{8,24},{9,280},{16,256},{17,0},{24,264},{25,8},{256... | collective-permute-start | bytes 884744 | tf_op jit(solution)/shard_map/weights/ppermute | solution.py:262
  23.4 3.4 %dispatch.1 = (bf16[256,3072]{1,0:T(8,128)(2,1)}, bf16[256,256]{1,0:T(8,128)(2,1)}, bf16[256,512]{1,0:T(8,128)(2,1)}) custom-call(bf16[128,2048]{1,0:T(8,128)(2,1)} %bitcast.36, f32[1,2048]{1,0:T(1,128)} %bitcast.38, s32[8,128]{1,0:T(8,128)} %bitcast.39, f32[8,128]{1,0:T(8,128)} %bitcast.40), custom_call_target="tpu_custom_call" | custom-call | flops 536870912 | bytes 4194304 | tf_op jit(solution)/shard_map/dispatch/dispatch/pallas_call | solution.py:265
  26.8 3.9 %collective-permute-done = bf16[128,1152]{1,0:T(8,128)(2,1)} collective-permute-done((bf16[128,1152]{1,0:T(8,128)(2,1)}, bf16[128,1152]{1,0:T(8,128)(2,1)}, u32[]{:S(2)}, u32[]{:S(2)}) %collective-permute-start) | collective-permute-done | bytes 294944 | tf_op jit(solution)/shard_map/weights/ppermute | solution.py:262
  30.7 0.0 all-gather.6.cloned.1.call-update
  30.7 0.0 copy-start.2
  30.7 0.0 copy-start.3
  30.8 14.4 %all-to-all-start = ((bf16[32,8,3072]{2,1,0:T(8,128)(2,1)}), bf16[32,8,3072]{2,1,0:T(8,128)(2,1)S(1)}, u32[]{:S(2)}, u32[]{:S(2)}) async-start(bf16[32,8,3072]{2,1,0:T(8,128)(2,1)} %bitcast.26), calls=%async_computation | async-start | bytes 3145728 | tf_op jit(solution)/shard_map/dispatch/all_to_all | solution.py:280
  45.1 0.0 all-gather.4.cloned.1.call-start
  45.2 0.0 copy-done.2
  45.2 0.0 copy-done.3
  45.2 7.3 %collective-permute-start.1 = (bf16[128,512]{1,0:T(8,128)(2,1)S(1)}, bf16[128,512]{1,0:T(8,128)(2,1)S(1)}, u32[]{:S(2)}, u32[]{:S(2)}) collective-permute-start(bf16[128,512]{1,0:T(8,128)(2,1)S(1)} %constant_dynamic-update-slice_fusion), channel_id=1, source_target_pairs={{0,256},{1,257},{2,258},{3,259},{4,260},{5,261},{6,262},{7,263},{8... | collective-permute-start | bytes 393224 | tf_op jit(solution)/shard_map/keys/ppermute | solution.py:289
  52.5 26.9 %collective-permute-done.1 = bf16[128,512]{1,0:T(8,128)(2,1)S(1)} collective-permute-done((bf16[128,512]{1,0:T(8,128)(2,1)S(1)}, bf16[128,512]{1,0:T(8,128)(2,1)S(1)}, u32[]{:S(2)}, u32[]{:S(2)}) %collective-permute-start.1) | collective-permute-done | bytes 131104 | tf_op jit(solution)/shard_map/keys/ppermute | solution.py:289
  79.4 0.7 pad_maximum_fusion
  80.1 0.0 all-gather.4.cloned.1.call-update
  80.2 2.1 %all-to-all-done = bf16[32,8,3072]{2,1,0:T(8,128)(2,1)S(1)} async-done(((bf16[32,8,3072]{2,1,0:T(8,128)(2,1)}), bf16[32,8,3072]{2,1,0:T(8,128)(2,1)S(1)}, u32[]{:S(2)}, u32[]{:S(2)}) %all-to-all-start) | async-done | bytes 1572896 | tf_op jit(solution)/shard_map/dispatch/all_to_all | solution.py:280
  82.3 0.0 all-gather.6.cloned.1.call-done
  82.3 6.1 %experts.1 = bf16[256,3072]{1,0:T(8,128)(2,1)} custom-call(bf16[256,3072]{1,0:T(8,128)(2,1)S(1)} %bitcast.25, bf16[16,128,1152]{2,1,0:T(8,128)(2,1)} %bitcast.35), custom_call_target="tpu_custom_call" | custom-call | flops 2415919104 | bytes 8388608 | tf_op jit(solution)/shard_map/experts/experts/pallas_call | solution.py:295
  88.4 12.0 %all-to-all-start.1 = ((bf16[32,8,3072]{2,1,0:T(8,128)(2,1)}), bf16[32,8,3072]{2,1,0:T(8,128)(2,1)S(1)}, u32[]{:S(2)}, u32[]{:S(2)}) async-start(bf16[32,8,3072]{2,1,0:T(8,128)(2,1)} %bitcast.19), calls=%async_computation.1 | async-start | bytes 3145728 | tf_op jit(solution)/shard_map/experts/all_to_all | solution.py:305
  100.5 28.8 %all-gather.4.cloned.1.call-done.kv_hbm = bf16[16,128,512]{2,1,0:T(8,128)(2,1)} async-done(((bf16[2,128,512]{2,1,0:T(8,128)(2,1)}), bf16[16,128,512]{2,1,0:T(8,128)(2,1)}) %all-gather.4.cloned.1.call-update) | async-done | bytes 2097168 | tf_op jit(solution)/shard_map/keys/all_gather | solution.py:291
  129.3 0.0 copy-start
  129.3 0.0 copy-start.1
  129.3 9.3 %attend.1 = bf16[128,2048]{1,0:T(8,128)(2,1)} custom-call(bf16[128,2048]{1,0:T(8,128)(2,1)} %bitcast.37, bf16[16,128,512]{2,1,0:T(8,128)(2,1)} %all-gather.4.cloned.1.call-done.kv_hbm, s32[1]{0:T(128)} %bitcast.14.place_ref), custom_call_target="tpu_custom_call" | custom-call | flops 2147483648 | bytes 4194304 | tf_op jit(solution)/shard_map/attend/attend/pallas_call | solution.py:311
  138.6 0.0 all-to-all-done.1
  138.6 0.0 copy-done
  138.6 0.0 copy-done.1
  138.6 1.5 %combine.1 = bf16[128,2048]{1,0:T(8,128)(2,1)} custom-call(bf16[256,3072]{1,0:T(8,128)(2,1)S(1)} %bitcast.24, bf16[256,256]{1,0:T(8,128)(2,1)S(1)} %copy-done.1, bf16[256,512]{1,0:T(8,128)(2,1)S(1)} %copy-done), custom_call_target="tpu_custom_call" | custom-call | flops 536870912 | bytes 3145728 | tf_op jit(solution)/shard_map/combine/combine/pallas_call | solution.py:326
  (2 shorter events, 0.0 us)
Async XLA Ops:
  7.2 75.1 %all-gather.6.cloned.1.call-start = ((), (), s32[]{:S(2)}) async-start(), calls=%async_computation.3 | async-start | bytes 5013504 | tf_op jit(solution)/shard_map/dispatch/all_gather | solution.py:279
  17.3 13.4 %collective-permute-start = (bf16[128,1152]{1,0:T(8,128)(2,1)}, bf16[128,1152]{1,0:T(8,128)(2,1)}, u32[]{:S(2)}, u32[]{:S(2)}) collective-permute-start(bf16[128,1152]{1,0:T(8,128)(2,1)} %pack.1), channel_id=1, source_target_pairs={{0,16},{1,272},{8,24},{9,280},{16,256},{17,0},{24,264},{25,8},{256... | collective-permute-start | bytes 884744 | tf_op jit(solution)/shard_map/weights/ppermute | solution.py:262
  30.7 14.4 %copy-start.2 = (bf16[1,128,256]{2,1,0:T(8,128)(2,1)S(1)}, bf16[1,128,256]{2,1,0:T(8,128)(2,1)}, u32[]{:S(2)}) copy-start(bf16[1,128,256]{2,1,0:T(8,128)(2,1)} %param.11) | copy-start | bytes 196612
  30.7 14.5 %copy-start.3 = (bf16[1,128,256]{2,1,0:T(8,128)(2,1)S(1)}, bf16[1,128,256]{2,1,0:T(8,128)(2,1)}, u32[]{:S(2)}) copy-start(bf16[1,128,256]{2,1,0:T(8,128)(2,1)} %param.12) | copy-start | bytes 196612
  30.8 51.5 %all-to-all-start = ((bf16[32,8,3072]{2,1,0:T(8,128)(2,1)}), bf16[32,8,3072]{2,1,0:T(8,128)(2,1)S(1)}, u32[]{:S(2)}, u32[]{:S(2)}) async-start(bf16[32,8,3072]{2,1,0:T(8,128)(2,1)} %bitcast.26), calls=%async_computation | async-start | bytes 3145728 | tf_op jit(solution)/shard_map/dispatch/all_to_all | solution.py:280
  45.1 84.2 %all-gather.4.cloned.1.call-start = ((), (), s32[]{:S(2)}) async-start(), calls=%async_computation.2 | async-start | bytes 2359296 | tf_op jit(solution)/shard_map/keys/all_gather | solution.py:291
  45.2 34.2 %collective-permute-start.1 = (bf16[128,512]{1,0:T(8,128)(2,1)S(1)}, bf16[128,512]{1,0:T(8,128)(2,1)S(1)}, u32[]{:S(2)}, u32[]{:S(2)}) collective-permute-start(bf16[128,512]{1,0:T(8,128)(2,1)S(1)} %constant_dynamic-update-slice_fusion), channel_id=1, source_target_pairs={{0,256},{1,257},{2,258},{3,259},{4,260},{5,261},{6,262},{7,263},{8... | collective-permute-start | bytes 393224 | tf_op jit(solution)/shard_map/keys/ppermute | solution.py:289
  88.4 50.2 %all-to-all-start.1 = ((bf16[32,8,3072]{2,1,0:T(8,128)(2,1)}), bf16[32,8,3072]{2,1,0:T(8,128)(2,1)S(1)}, u32[]{:S(2)}, u32[]{:S(2)}) async-start(bf16[32,8,3072]{2,1,0:T(8,128)(2,1)} %bitcast.19), calls=%async_computation.1 | async-start | bytes 3145728 | tf_op jit(solution)/shard_map/experts/all_to_all | solution.py:305
  129.3 9.3 %copy-start = (bf16[256,512]{1,0:T(8,128)(2,1)S(1)}, bf16[256,512]{1,0:T(8,128)(2,1)}, u32[]{:S(2)}) copy-start(bf16[256,512]{1,0:T(8,128)(2,1)} %get-tuple-element.17.mix_b_ref) | copy-start | bytes 786436
  129.3 9.3 %copy-start.1 = (bf16[256,256]{1,0:T(8,128)(2,1)S(1)}, bf16[256,256]{1,0:T(8,128)(2,1)}, u32[]{:S(2)}) copy-start(bf16[256,256]{1,0:T(8,128)(2,1)} %get-tuple-element.16.mix_a_ref) | copy-start | bytes 393220
Sparse Core Ops, SparseCore 0:
  30.9 50.7 all-gather.5
  84.3 44.9 all-gather.3

commit v7 on v6

--- a/solution.py
+++ b/solution.py
@@ -190,41 +190,46 @@
 def attend_kernel(halves, ring, heads_kv, q_ref, kv_hbm, place_ref, out_ref, kv_ref, sems):
     tokens, wide = q_ref.shape
     group = wide // HD // heads_kv
-    blocks = halves * ring
-    keys = blocks * tokens
+    keys = ring * tokens
+    kind = heads_kv * HD
     factor = math.log2(math.e) / math.sqrt(HD)
-    kind = heads_kv * HD
     copies = []
-    for i in range(2):
-        at = (slice(None), slice(None), pl.ds(i * kind, kind))
-        copies.append(pltpu.make_async_copy(kv_hbm.at[at], kv_ref.at[at], sems.at[i]))
-        copies[i].start()
+    for side in range(halves):
+        copies.append(pltpu.make_async_copy(kv_hbm.at[:, side], kv_ref.at[side], sems.at[side]))
+        copies[side].start()
+    here = place_ref[0] // ring
+    mine = place_ref[0] % ring
     lane = lax.broadcasted_iota(jnp.int32, (tokens, keys), 1)
     row = lax.broadcasted_iota(jnp.int32, (tokens, keys), 0)
-    block = lane // tokens
-    here = place_ref[0] // ring
-    passed = jnp.where(here == 0, halves, 0)
-    side = jnp.where(block % halves == 0, here, passed)
-    key_pos = (side * ring + block // halves) * tokens + lane % tokens
-    bias = jnp.where(key_pos <= row + place_ref[0] * tokens, 0.0, MASKED)
-    ones = jnp.ones((keys, HD), BF16)
-    copies[0].wait()
-    for g in range(heads_kv):
-        key = kv_ref[:, :, g * HD : (g + 1) * HD].reshape(keys, HD)
-        for i in range(g * group, (g + 1) * group):
-            at = slice(i * HD, (i + 1) * HD)
-            scores = lax.dot_general(
-                q_ref[:, at], key, (((1,), (1,)), ((), ())), preferred_element_type=F32
-            )
-            scores = scores * factor + bias
-            probs = jnp.exp2(scores - jnp.max(scores, axis=-1, keepdims=True))
-            if i == 0:
-                copies[1].wait()
-            if i == g * group:
-                value = kv_ref[:, :, kind + g * HD : kind + (g + 1) * HD].reshape(keys, HD)
-                value = jnp.concatenate([value, ones], axis=1)
-            mixed = jnp.dot(probs.astype(BF16), value, preferred_element_type=F32)
-            out_ref[:, at] = (mixed[:, :HD] / mixed[:, HD:]).astype(BF16)
+    bias = jnp.where(lane <= row + mine * tokens, 0.0, MASKED)
+    for copy in copies:
+        copy.wait()
+
+    def attend(sides):
+        ones = jnp.ones((sides * keys, HD), BF16)
+        for g in range(heads_kv):
+            key = kv_ref[:sides, :, :, g * HD : (g + 1) * HD].reshape(sides * keys, HD)
+            value = kv_ref[:sides, :, :, kind + g * HD : kind + (g + 1) * HD].reshape(sides * keys, HD)
+            value = jnp.concatenate([value, ones], axis=1)
+            for i in range(g * group, (g + 1) * group):
+                at = slice(i * HD, (i + 1) * HD)
+                scores = lax.dot_general(
+                    q_ref[:, at], key, (((1,), (1,)), ((), ())), preferred_element_type=F32
+                )
+                scores = scores * factor
+                masked = scores[:, :keys] + bias
+                scores = masked if sides == 1 else jnp.concatenate([masked, scores[:, keys:]], axis=1)
+                probs = jnp.exp2(scores - jnp.max(scores, axis=-1, keepdims=True))
+                mixed = jnp.dot(probs.astype(BF16), value, preferred_element_type=F32)
+                out_ref[:, at] = (mixed[:, :HD] / mixed[:, HD:]).astype(BF16)
+
+    @pl.when(here == 0)
+    def _():
+        attend(1)
+
+    @pl.when(here > 0)
+    def _():
+        attend(halves)
 
 
 def estimate(flops, bytes_accessed, transcendentals=0):
@@ -249,7 +254,7 @@
             pack_kernel,
             out_shape=jax.ShapeDtypeStruct((w_gate.shape[1], 3 * hidden_units), BF16),
             in_specs=[HBM] * 3,
-            out_specs=HBM,
+            out_specs=VMEM,
             scratch_shapes=[pltpu.SemaphoreType.DMA((2 + hidden_units // tokens,))],
             name="pack",
         )(w_gate[0], w_up[0], w_down[0])
@@ -275,20 +280,18 @@
             cost_estimate=estimate(4 * 256 * 256 * 2048, 4 * 1024 * 1024),
             name="dispatch",
         )(stream[0], norm_gain[None, :], ids, gate_values[0].T)
-        part, _ = lax.optimization_barrier((part, outgoing))
-        weights = lax.all_gather(part, ("y", "c"), axis=0)
         arrived = lax.all_to_all(
             outgoing.reshape(owners, LOW, wide), CHIPS, split_axis=0, concat_axis=0, tiled=True
         ).reshape(slots, wide)
 
     with jax.named_scope("keys"):
-        key_local, value_local, outgoing, part = lax.optimization_barrier(
-            (key_rows[0], value_rows[0], outgoing, part)
-        )
+        key_local, value_local, _ = lax.optimization_barrier((key_rows[0], value_rows[0], outgoing))
         kv = jnp.concatenate([key_local, value_local], axis=1)
+        part, kv = lax.optimization_barrier((part, kv))
+        weights = lax.all_gather(part, ("y", "c"), axis=0)
         kv_passed = lax.ppermute(kv, "zh", [(0, 1)])
         kv_pair = jnp.stack([kv, kv_passed])
-        kv_all = lax.all_gather(kv_pair, "y", axis=0, tiled=True)
+        kv_all = lax.all_gather(kv_pair, "y", axis=0)
         arrived, kv_pair = lax.optimization_barrier((arrived, kv_pair))
 
     with jax.named_scope("experts"):
@@ -314,7 +317,7 @@
             in_specs=[VMEM, HBM, SMEM],
             out_specs=VMEM,
             scratch_shapes=[
-                pltpu.VMEM((halves * ring, tokens, 2 * heads_kv * HD), BF16),
+                pltpu.VMEM((halves, ring, tokens, 2 * heads_kv * HD), BF16),
                 pltpu.SemaphoreType.DMA((2,)),
             ],
             compiler_params=pltpu.CompilerParams(vmem_limit_bytes=60 * 1024 * 1024),

time: 148 us -> 139 us (0.939)
  Pallas kernels: 30.4 us -> 19.3 us
  waiting for transfers between devices: 61.8 us -> 64.4 us
    pallas_call x1, Pallas kernels: 10.1 us -> 1.7 us  [shards(): pl.pallas_call(pack_kernel, out_shape=jax.ShapeDtypeStruct((w_gate.shape[...]
    pallas_call x1, Pallas kernels: 9.3 us -> 6.57 us  [shards(): pl.pallas_call(functools.partial(attend_kernel, halves, ring, heads_kv),...]
    all_to_all x1, waiting for transfers between devices: 0.01 us -> 2.64 us  [shards(): lax.all_to_all(answers.reshape(owners, LOW, wide), CHIPS, split_axis=0, c...]
  transfers between devices with their start and end apart: 6 -> 6, of which waited for: 4 -> 5; matrix products, arithmetic and copies ran while one was open for 1% -> 1% of each run, Pallas kernels for 13% -> 12%
where the time goes in v7:
time: 139 us; the launch traced here: 138 us
  waiting for transfers between devices  64.4 us (46%)
  starting transfers between devices  39.7 us (29%)
  Pallas kernels  19.3 us (14%)
  between operations  14.1 us (10%)
    all_gather x1, waiting for transfers between devices, shards(): kv_all = lax.all_gather(kv_pair, 'y', axis=0)  28.9 us
    ppermute x1, waiting for transfers between devices, shards(): kv_passed = lax.ppermute(kv, 'zh', [(0, 1)])  26.9 us
    all_to_all x1, starting transfers between devices, shards(): lax.all_to_all(outgoing.reshape(owners, LOW, wide), CHIPS, split_axis=0,...  14.2 us
    all_to_all x1, starting transfers between devices, shards(): lax.all_to_all(answers.reshape(owners, LOW, wide), CHIPS, split_axis=0, c...  12 us
    ppermute x1, starting transfers between devices, shards(): kv_passed = lax.ppermute(kv, 'zh', [(0, 1)])  7.29 us
    pallas_call x1, Pallas kernels, shards(): pl.pallas_call(functools.partial(attend_kernel, halves, ring, heads_kv),...  6.57 us
    pallas_call x1, Pallas kernels, shards(): pl.pallas_call(functools.partial(expert_kernel, hidden_units), out_shape=...  6.12 us
    ppermute x1, starting transfers between devices, shards(): part = lax.ppermute(packed, ('zh', 'zl', 'c'), route)  6.09 us
  transfers between devices with their start and end apart: 6, of which 5 were waited for; matrix products, arithmetic and copies ran while one was open for 1% of the time, Pallas kernels for 12%

profile of v7, /device:TPU:6, one launch (start us, length us, event | category | flops | bytes accessed | tf_op | source)
XLA Modules:
  0.0 138.4 jit_solution(7094279241709923850)
XLA Ops:
  7.2 0.0 copy-start.3
  7.2 0.0 copy-start.2
  7.2 0.0 all-gather.7.cloned.1.call-start
  7.2 1.7 %pack.1 = bf16[128,1152]{1,0:T(8,128)(2,1)} custom-call(bf16[128,384]{1,0:T(8,128)(2,1)} %bitcast.31, bf16[128,384]{1,0:T(8,128)(2,1)} %bitcast.32, bf16[384,128]{1,0:T(8,128)(2,1)} %bitcast.33), custom_call_target="tpu_custom_call" | custom-call | tf_op jit(solution)/shard_map/weights/pack/pallas_call | solution.py:253
  8.9 6.1 %collective-permute-start = (bf16[128,1152]{1,0:T(8,128)(2,1)}, bf16[128,1152]{1,0:T(8,128)(2,1)}, u32[]{:S(2)}, u32[]{:S(2)}) collective-permute-start(bf16[128,1152]{1,0:T(8,128)(2,1)} %pack.1), channel_id=1, source_target_pairs={{0,16},{1,272},{8,24},{9,280},{16,256},{17,0},{24,264},{25,8},{256... | collective-permute-start | bytes 884744 | tf_op jit(solution)/shard_map/weights/ppermute | solution.py:267
  15.0 3.4 %dispatch.1 = (bf16[256,3072]{1,0:T(8,128)(2,1)}, bf16[256,256]{1,0:T(8,128)(2,1)}, bf16[256,512]{1,0:T(8,128)(2,1)}) custom-call(bf16[128,2048]{1,0:T(8,128)(2,1)} %bitcast.38, f32[1,2048]{1,0:T(1,128)} %bitcast.40, s32[8,128]{1,0:T(8,128)} %bitcast.41, f32[8,128]{1,0:T(8,128)} %bitcast.42), custom_call_target="tpu_custom_call" | custom-call | flops 536870912 | bytes 4194304 | tf_op jit(solution)/shard_map/dispatch/dispatch/pallas_call | solution.py:270
  18.5 0.0 copy-done.3
  18.5 0.0 copy-done.2
  18.5 3.8 %collective-permute-done = bf16[128,1152]{1,0:T(8,128)(2,1)} collective-permute-done((bf16[128,1152]{1,0:T(8,128)(2,1)}, bf16[128,1152]{1,0:T(8,128)(2,1)}, u32[]{:S(2)}, u32[]{:S(2)}) %collective-permute-start) | collective-permute-done | bytes 294944 | tf_op jit(solution)/shard_map/weights/ppermute | solution.py:267
  22.3 0.0 all-gather.7.cloned.1.call-update
  22.4 14.2 %all-to-all-start = ((bf16[32,8,3072]{2,1,0:T(8,128)(2,1)}), bf16[32,8,3072]{2,1,0:T(8,128)(2,1)S(1)}, u32[]{:S(2)}, u32[]{:S(2)}) async-start(bf16[32,8,3072]{2,1,0:T(8,128)(2,1)} %bitcast.27), calls=%async_computation | async-start | bytes 3145728 | tf_op jit(solution)/shard_map/dispatch/all_to_all | solution.py:283
  36.6 0.0 all-gather.5.cloned.1.call-start
  36.7 7.3 %collective-permute-start.1 = (bf16[128,512]{1,0:T(8,128)(2,1)S(1)}, bf16[128,512]{1,0:T(8,128)(2,1)S(1)}, u32[]{:S(2)}, u32[]{:S(2)}) collective-permute-start(bf16[128,512]{1,0:T(8,128)(2,1)S(1)} %pad_maximum_fusion.1), channel_id=1, source_target_pairs={{0,256},{1,257},{2,258},{3,259},{4,260},{5,261},{6,262},{7,263},{8... | collective-permute-start | bytes 393224 | tf_op jit(solution)/shard_map/keys/ppermute | solution.py:292
  44.0 26.9 %collective-permute-done.1 = bf16[128,512]{1,0:T(8,128)(2,1)S(1)} collective-permute-done((bf16[128,512]{1,0:T(8,128)(2,1)S(1)}, bf16[128,512]{1,0:T(8,128)(2,1)S(1)}, u32[]{:S(2)}, u32[]{:S(2)}) %collective-permute-start.1) | collective-permute-done | bytes 131104 | tf_op jit(solution)/shard_map/keys/ppermute | solution.py:292
  70.9 0.7 pad_maximum_fusion
  71.6 0.0 all-gather.5.cloned.1.call-update
  71.7 2.1 %all-to-all-done = bf16[32,8,3072]{2,1,0:T(8,128)(2,1)S(1)} async-done(((bf16[32,8,3072]{2,1,0:T(8,128)(2,1)}), bf16[32,8,3072]{2,1,0:T(8,128)(2,1)S(1)}, u32[]{:S(2)}, u32[]{:S(2)}) %all-to-all-start) | async-done | bytes 1572896 | tf_op jit(solution)/shard_map/dispatch/all_to_all | solution.py:283
  73.8 0.0 all-gather.7.cloned.1.call-done
  73.8 6.1 %experts.1 = bf16[256,3072]{1,0:T(8,128)(2,1)} custom-call(bf16[256,3072]{1,0:T(8,128)(2,1)S(1)} %bitcast.26, bf16[16,128,1152]{2,1,0:T(8,128)(2,1)} %bitcast.36), custom_call_target="tpu_custom_call" | custom-call | flops 2415919104 | bytes 8388608 | tf_op jit(solution)/shard_map/experts/experts/pallas_call | solution.py:298
  79.9 12.0 %all-to-all-start.1 = ((bf16[32,8,3072]{2,1,0:T(8,128)(2,1)}), bf16[32,8,3072]{2,1,0:T(8,128)(2,1)S(1)}, u32[]{:S(2)}, u32[]{:S(2)}) async-start(bf16[32,8,3072]{2,1,0:T(8,128)(2,1)} %bitcast.20), calls=%async_computation.1 | async-start | bytes 3145728 | tf_op jit(solution)/shard_map/experts/all_to_all | solution.py:308
  91.9 28.9 %all-gather.5.cloned.1.call-done = bf16[16,128,512]{2,1,0:T(8,128)(2,1)} async-done(((bf16[2,128,512]{2,1,0:T(8,128)(2,1)}), bf16[16,128,512]{2,1,0:T(8,128)(2,1)}) %all-gather.5.cloned.1.call-update) | async-done | bytes 2097168 | tf_op jit(solution)/shard_map/keys/all_gather | solution.py:294
  120.8 0.0 copy-start
  120.8 0.0 copy-start.1
  120.8 6.6 %attend.1 = bf16[128,2048]{1,0:T(8,128)(2,1)} custom-call(bf16[128,2048]{1,0:T(8,128)(2,1)} %bitcast.39, bf16[8,2,128,512]{3,2,1,0:T(8,128)(2,1)} %bitcast.37, s32[1]{0:T(128)} %bitcast.15.place_ref), custom_call_target="tpu_custom_call" | custom-call | flops 2147483648 | bytes 4194304 | tf_op jit(solution)/shard_map/attend/attend/pallas_call | solution.py:314
  127.4 2.6 %all-to-all-done.1 = bf16[32,8,3072]{2,1,0:T(8,128)(2,1)S(1)} async-done(((bf16[32,8,3072]{2,1,0:T(8,128)(2,1)}), bf16[32,8,3072]{2,1,0:T(8,128)(2,1)S(1)}, u32[]{:S(2)}, u32[]{:S(2)}) %all-to-all-start.1) | async-done | bytes 1572896 | tf_op jit(solution)/shard_map/experts/all_to_all | solution.py:308
  130.0 0.0 copy-done
  130.0 0.0 copy-done.1
  130.0 1.5 %combine.1 = bf16[128,2048]{1,0:T(8,128)(2,1)} custom-call(bf16[256,3072]{1,0:T(8,128)(2,1)S(1)} %bitcast.25, bf16[256,256]{1,0:T(8,128)(2,1)S(1)} %copy-done.1, bf16[256,512]{1,0:T(8,128)(2,1)S(1)} %copy-done), custom_call_target="tpu_custom_call" | custom-call | flops 536870912 | bytes 3145728 | tf_op jit(solution)/shard_map/combine/combine/pallas_call | solution.py:329
  (1 shorter events, 0.0 us)
Async XLA Ops:
  7.2 11.3 %copy-start.3 = (bf16[1,128,256]{2,1,0:T(8,128)(2,1)S(1)}, bf16[1,128,256]{2,1,0:T(8,128)(2,1)}, u32[]{:S(2)}) copy-start(bf16[1,128,256]{2,1,0:T(8,128)(2,1)} %param.11) | copy-start | bytes 196612
  7.2 11.3 %copy-start.2 = (bf16[1,128,256]{2,1,0:T(8,128)(2,1)S(1)}, bf16[1,128,256]{2,1,0:T(8,128)(2,1)}, u32[]{:S(2)}) copy-start(bf16[1,128,256]{2,1,0:T(8,128)(2,1)} %param.12) | copy-start | bytes 196612
  7.2 66.6 %all-gather.7.cloned.1.call-start = ((), (), s32[]{:S(2)}) async-start(), calls=%async_computation.3 | async-start | bytes 5013504 | tf_op jit(solution)/shard_map/keys/all_gather | solution.py:291
  8.9 13.4 %collective-permute-start = (bf16[128,1152]{1,0:T(8,128)(2,1)}, bf16[128,1152]{1,0:T(8,128)(2,1)}, u32[]{:S(2)}, u32[]{:S(2)}) collective-permute-start(bf16[128,1152]{1,0:T(8,128)(2,1)} %pack.1), channel_id=1, source_target_pairs={{0,16},{1,272},{8,24},{9,280},{16,256},{17,0},{24,264},{25,8},{256... | collective-permute-start | bytes 884744 | tf_op jit(solution)/shard_map/weights/ppermute | solution.py:267
  22.4 51.4 %all-to-all-start = ((bf16[32,8,3072]{2,1,0:T(8,128)(2,1)}), bf16[32,8,3072]{2,1,0:T(8,128)(2,1)S(1)}, u32[]{:S(2)}, u32[]{:S(2)}) async-start(bf16[32,8,3072]{2,1,0:T(8,128)(2,1)} %bitcast.27), calls=%async_computation | async-start | bytes 3145728 | tf_op jit(solution)/shard_map/dispatch/all_to_all | solution.py:283
  36.6 84.2 %all-gather.5.cloned.1.call-start = ((), (), s32[]{:S(2)}) async-start(), calls=%async_computation.2 | async-start | bytes 2359296 | tf_op jit(solution)/shard_map/keys/all_gather | solution.py:294
  36.7 34.2 %collective-permute-start.1 = (bf16[128,512]{1,0:T(8,128)(2,1)S(1)}, bf16[128,512]{1,0:T(8,128)(2,1)S(1)}, u32[]{:S(2)}, u32[]{:S(2)}) collective-permute-start(bf16[128,512]{1,0:T(8,128)(2,1)S(1)} %pad_maximum_fusion.1), channel_id=1, source_target_pairs={{0,256},{1,257},{2,258},{3,259},{4,260},{5,261},{6,262},{7,263},{8... | collective-permute-start | bytes 393224 | tf_op jit(solution)/shard_map/keys/ppermute | solution.py:292
  79.9 50.1 %all-to-all-start.1 = ((bf16[32,8,3072]{2,1,0:T(8,128)(2,1)}), bf16[32,8,3072]{2,1,0:T(8,128)(2,1)S(1)}, u32[]{:S(2)}, u32[]{:S(2)}) async-start(bf16[32,8,3072]{2,1,0:T(8,128)(2,1)} %bitcast.20), calls=%async_computation.1 | async-start | bytes 3145728 | tf_op jit(solution)/shard_map/experts/all_to_all | solution.py:308
  120.8 9.2 %copy-start = (bf16[256,512]{1,0:T(8,128)(2,1)S(1)}, bf16[256,512]{1,0:T(8,128)(2,1)}, u32[]{:S(2)}) copy-start(bf16[256,512]{1,0:T(8,128)(2,1)} %get-tuple-element.19.mix_b_ref) | copy-start | bytes 786436
  120.8 9.2 %copy-start.1 = (bf16[256,256]{1,0:T(8,128)(2,1)S(1)}, bf16[256,256]{1,0:T(8,128)(2,1)}, u32[]{:S(2)}) copy-start(bf16[256,256]{1,0:T(8,128)(2,1)} %get-tuple-element.18.mix_a_ref) | copy-start | bytes 393220
Sparse Core Ops, SparseCore 0:
  22.5 50.7 all-gather.6
  75.9 44.7 all-gather.4

commit v8 on v7

--- a/solution.py
+++ b/solution.py
@@ -289,7 +289,11 @@
         kv = jnp.concatenate([key_local, value_local], axis=1)
         part, kv = lax.optimization_barrier((part, kv))
         weights = lax.all_gather(part, ("y", "c"), axis=0)
-        kv_passed = lax.ppermute(kv, "zh", [(0, 1)])
+        deep = halves * depth
+        kv_passed = kv
+        for leg in range(2):
+            route = [((z - leg * depth // 2) % deep, (z - (leg + 1) * depth // 2) % deep) for z in range(depth)]
+            kv_passed = lax.ppermute(kv_passed, ("zh", "zl"), route)
         kv_pair = jnp.stack([kv, kv_passed])
         kv_all = lax.all_gather(kv_pair, "y", axis=0)
         arrived, kv_pair = lax.optimization_barrier((arrived, kv_pair))

time: 139 us -> 144 us (1.036)
  waiting for transfers between devices: 64.4 us -> 70.5 us
    ppermute x1 -> x2, waiting for transfers between devices: 26.9 us -> 37.7 us  [shards(): kv_passed = lax.ppermute(kv_passed, ('zh', 'zl'), route)]
    all_to_all x1, starting transfers between devices: 12 us -> 9.07 us  [shards(): lax.all_to_all(answers.reshape(owners, LOW, wide), CHIPS, split_axis=0, c...]
    all_to_all x1, waiting for transfers between devices: 2.64 us -> 0.01 us  [shards(): lax.all_to_all(answers.reshape(owners, LOW, wide), CHIPS, split_axis=0, c...]
    all_to_all x1, waiting for transfers between devices: 2.11 us -> 0.01 us  [shards(): lax.all_to_all(outgoing.reshape(owners, LOW, wide), CHIPS, split_axis=0,...]
    ppermute x1 -> x2, starting transfers between devices: 7.29 us -> 9.25 us  [shards(): kv_passed = lax.ppermute(kv_passed, ('zh', 'zl'), route)]
  transfers between devices with their start and end apart: 6 -> 7, of which waited for: 5 -> 4; matrix products, arithmetic and copies ran while one was open for 1% -> 1% of each run, Pallas kernels for 12% -> 11%
where the time goes in v8:
time: 144 us; the launch traced here: 143 us
  waiting for transfers between devices  70.5 us (49%)
  starting transfers between devices  38.7 us (27%)
  Pallas kernels  19.3 us (13%)
  between operations  14.2 us (10%)
    ppermute x2, waiting for transfers between devices, shards(): kv_passed = lax.ppermute(kv_passed, ('zh', 'zl'), route)  37.7 us
    all_gather x1, waiting for transfers between devices, shards(): kv_all = lax.all_gather(kv_pair, 'y', axis=0)  28.9 us
    all_to_all x1, starting transfers between devices, shards(): lax.all_to_all(outgoing.reshape(owners, LOW, wide), CHIPS, split_axis=0,...  14.2 us
    ppermute x2, starting transfers between devices, shards(): kv_passed = lax.ppermute(kv_passed, ('zh', 'zl'), route)  9.25 us
    all_to_all x1, starting transfers between devices, shards(): lax.all_to_all(answers.reshape(owners, LOW, wide), CHIPS, split_axis=0, c...  9.07 us
    pallas_call x1, Pallas kernels, shards(): pl.pallas_call(functools.partial(attend_kernel, halves, ring, heads_kv),...  6.57 us
    pallas_call x1, Pallas kernels, shards(): pl.pallas_call(functools.partial(expert_kernel, hidden_units), out_shape=...  6.12 us
    ppermute x1, starting transfers between devices, shards(): part = lax.ppermute(packed, ('zh', 'zl', 'c'), route)  6.09 us
  transfers between devices with their start and end apart: 7, of which 4 were waited for; matrix products, arithmetic and copies ran while one was open for 1% of the time, Pallas kernels for 11%

profile of v8, /device:TPU:6, one launch (start us, length us, event | category | flops | bytes accessed | tf_op | source)
XLA Modules:
  0.0 143.4 jit_solution(9326895202688974402)
XLA Ops:
  7.2 0.0 copy-start.3
  7.2 0.0 copy-start.2
  7.2 0.0 all-gather.7.cloned.1.call-start
  7.2 1.7 %pack.1 = bf16[128,1152]{1,0:T(8,128)(2,1)} custom-call(bf16[128,384]{1,0:T(8,128)(2,1)} %bitcast.31, bf16[128,384]{1,0:T(8,128)(2,1)} %bitcast.32, bf16[384,128]{1,0:T(8,128)(2,1)} %bitcast.33), custom_call_target="tpu_custom_call" | custom-call | tf_op jit(solution)/shard_map/weights/pack/pallas_call | solution.py:253
  8.9 6.1 %collective-permute-start = (bf16[128,1152]{1,0:T(8,128)(2,1)}, bf16[128,1152]{1,0:T(8,128)(2,1)}, u32[]{:S(2)}, u32[]{:S(2)}) collective-permute-start(bf16[128,1152]{1,0:T(8,128)(2,1)} %pack.1), channel_id=1, source_target_pairs={{0,16},{1,272},{8,24},{9,280},{16,256},{17,0},{24,264},{25,8},{256... | collective-permute-start | bytes 884744 | tf_op jit(solution)/shard_map/weights/ppermute | solution.py:267
  15.0 3.4 %dispatch.1 = (bf16[256,3072]{1,0:T(8,128)(2,1)}, bf16[256,256]{1,0:T(8,128)(2,1)}, bf16[256,512]{1,0:T(8,128)(2,1)}) custom-call(bf16[128,2048]{1,0:T(8,128)(2,1)} %bitcast.38, f32[1,2048]{1,0:T(1,128)} %bitcast.40, s32[8,128]{1,0:T(8,128)} %bitcast.41, f32[8,128]{1,0:T(8,128)} %bitcast.42), custom_call_target="tpu_custom_call" | custom-call | flops 536870912 | bytes 4194304 | tf_op jit(solution)/shard_map/dispatch/dispatch/pallas_call | solution.py:270
  18.5 0.0 copy-done.3
  18.5 0.0 copy-done.2
  18.5 3.8 %collective-permute-done = bf16[128,1152]{1,0:T(8,128)(2,1)} collective-permute-done((bf16[128,1152]{1,0:T(8,128)(2,1)}, bf16[128,1152]{1,0:T(8,128)(2,1)}, u32[]{:S(2)}, u32[]{:S(2)}) %collective-permute-start) | collective-permute-done | bytes 294944 | tf_op jit(solution)/shard_map/weights/ppermute | solution.py:267
  22.3 0.0 all-gather.7.cloned.1.call-update
  22.4 14.2 %all-to-all-start = ((bf16[32,8,3072]{2,1,0:T(8,128)(2,1)}), bf16[32,8,3072]{2,1,0:T(8,128)(2,1)S(1)}, u32[]{:S(2)}, u32[]{:S(2)}) async-start(bf16[32,8,3072]{2,1,0:T(8,128)(2,1)} %bitcast.27), calls=%async_computation | async-start | bytes 3145728 | tf_op jit(solution)/shard_map/dispatch/all_to_all | solution.py:283
  36.6 0.0 all-gather.5.cloned.1.call-start
  36.7 5.5 %collective-permute-start.1 = (bf16[128,512]{1,0:T(8,128)(2,1)S(1)}, bf16[128,512]{1,0:T(8,128)(2,1)S(1)}, u32[]{:S(2)}, u32[]{:S(2)}) collective-permute-start(bf16[128,512]{1,0:T(8,128)(2,1)S(1)} %pad_maximum_fusion.1), channel_id=1, source_target_pairs={{0,272},{8,280},{16,0},{24,8},{1,273},{9,281},{17,1},{25,9},{2,274... | collective-permute-start | bytes 393224 | tf_op jit(solution)/shard_map/keys/ppermute | solution.py:296
  42.2 34.8 %collective-permute-done.1 = bf16[128,512]{1,0:T(8,128)(2,1)S(1)} collective-permute-done((bf16[128,512]{1,0:T(8,128)(2,1)S(1)}, bf16[128,512]{1,0:T(8,128)(2,1)S(1)}, u32[]{:S(2)}, u32[]{:S(2)}) %collective-permute-start.1) | collective-permute-done | bytes 131104 | tf_op jit(solution)/shard_map/keys/ppermute | solution.py:296
  77.0 3.7 %collective-permute-start.2 = (bf16[128,512]{1,0:T(8,128)(2,1)S(1)}, bf16[128,512]{1,0:T(8,128)(2,1)S(1)}, u32[]{:S(2)}, u32[]{:S(2)}) collective-permute-start(bf16[128,512]{1,0:T(8,128)(2,1)S(1)} %collective-permute-done.1), channel_id=1, source_target_pairs={{272,256},{280,264},{0,272},{8,280},{273,257},{281,265},{1,273},{9... | collective-permute-start | bytes 393224 | tf_op jit(solution)/shard_map/keys/ppermute | solution.py:296
  80.7 2.9 %collective-permute-done.2 = bf16[128,512]{1,0:T(8,128)(2,1)S(1)} collective-permute-done((bf16[128,512]{1,0:T(8,128)(2,1)S(1)}, bf16[128,512]{1,0:T(8,128)(2,1)S(1)}, u32[]{:S(2)}, u32[]{:S(2)}) %collective-permute-start.2) | collective-permute-done | bytes 131104 | tf_op jit(solution)/shard_map/keys/ppermute | solution.py:296
  83.6 0.7 pad_maximum_fusion
  84.4 0.0 all-gather.5.cloned.1.call-update
  84.4 0.0 all-to-all-done
  84.4 0.0 all-gather.7.cloned.1.call-done
  84.4 6.1 %experts.1 = bf16[256,3072]{1,0:T(8,128)(2,1)} custom-call(bf16[256,3072]{1,0:T(8,128)(2,1)S(1)} %bitcast.26, bf16[16,128,1152]{2,1,0:T(8,128)(2,1)} %bitcast.36), custom_call_target="tpu_custom_call" | custom-call | flops 2415919104 | bytes 8388608 | tf_op jit(solution)/shard_map/experts/experts/pallas_call | solution.py:302
  90.5 9.1 %all-to-all-start.1 = ((bf16[32,8,3072]{2,1,0:T(8,128)(2,1)}), bf16[32,8,3072]{2,1,0:T(8,128)(2,1)S(1)}, u32[]{:S(2)}, u32[]{:S(2)}) async-start(bf16[32,8,3072]{2,1,0:T(8,128)(2,1)} %bitcast.20), calls=%async_computation.1 | async-start | bytes 3145728 | tf_op jit(solution)/shard_map/experts/all_to_all | solution.py:312
  99.6 28.9 %all-gather.5.cloned.1.call-done = bf16[16,128,512]{2,1,0:T(8,128)(2,1)} async-done(((bf16[2,128,512]{2,1,0:T(8,128)(2,1)}), bf16[16,128,512]{2,1,0:T(8,128)(2,1)}) %all-gather.5.cloned.1.call-update) | async-done | bytes 2097168 | tf_op jit(solution)/shard_map/keys/all_gather | solution.py:298
  128.5 0.0 copy-start
  128.5 0.0 copy-start.1
  128.5 6.6 %attend.1 = bf16[128,2048]{1,0:T(8,128)(2,1)} custom-call(bf16[128,2048]{1,0:T(8,128)(2,1)} %bitcast.39, bf16[8,2,128,512]{3,2,1,0:T(8,128)(2,1)} %bitcast.37, s32[1]{0:T(128)} %bitcast.15.place_ref), custom_call_target="tpu_custom_call" | custom-call | flops 2147483648 | bytes 4194304 | tf_op jit(solution)/shard_map/attend/attend/pallas_call | solution.py:318
  135.1 0.0 all-to-all-done.1
  135.1 0.0 copy-done
  135.1 0.0 copy-done.1
  135.1 1.5 %combine.1 = bf16[128,2048]{1,0:T(8,128)(2,1)} custom-call(bf16[256,3072]{1,0:T(8,128)(2,1)S(1)} %bitcast.25, bf16[256,256]{1,0:T(8,128)(2,1)S(1)} %copy-done.1, bf16[256,512]{1,0:T(8,128)(2,1)S(1)} %copy-done), custom_call_target="tpu_custom_call" | custom-call | flops 536870912 | bytes 3145728 | tf_op jit(solution)/shard_map/combine/combine/pallas_call | solution.py:333
  (1 shorter events, 0.0 us)
Async XLA Ops:
  7.2 11.3 %copy-start.3 = (bf16[1,128,256]{2,1,0:T(8,128)(2,1)S(1)}, bf16[1,128,256]{2,1,0:T(8,128)(2,1)}, u32[]{:S(2)}) copy-start(bf16[1,128,256]{2,1,0:T(8,128)(2,1)} %param.11) | copy-start | bytes 196612
  7.2 11.3 %copy-start.2 = (bf16[1,128,256]{2,1,0:T(8,128)(2,1)S(1)}, bf16[1,128,256]{2,1,0:T(8,128)(2,1)}, u32[]{:S(2)}) copy-start(bf16[1,128,256]{2,1,0:T(8,128)(2,1)} %param.12) | copy-start | bytes 196612
  7.2 77.2 %all-gather.7.cloned.1.call-start = ((), (), s32[]{:S(2)}) async-start(), calls=%async_computation.3 | async-start | bytes 5013504 | tf_op jit(solution)/shard_map/keys/all_gather | solution.py:291
  8.9 13.4 %collective-permute-start = (bf16[128,1152]{1,0:T(8,128)(2,1)}, bf16[128,1152]{1,0:T(8,128)(2,1)}, u32[]{:S(2)}, u32[]{:S(2)}) collective-permute-start(bf16[128,1152]{1,0:T(8,128)(2,1)} %pack.1), channel_id=1, source_target_pairs={{0,16},{1,272},{8,24},{9,280},{16,256},{17,0},{24,264},{25,8},{256... | collective-permute-start | bytes 884744 | tf_op jit(solution)/shard_map/weights/ppermute | solution.py:267
  22.4 62.0 %all-to-all-start = ((bf16[32,8,3072]{2,1,0:T(8,128)(2,1)}), bf16[32,8,3072]{2,1,0:T(8,128)(2,1)S(1)}, u32[]{:S(2)}, u32[]{:S(2)}) async-start(bf16[32,8,3072]{2,1,0:T(8,128)(2,1)} %bitcast.27), calls=%async_computation | async-start | bytes 3145728 | tf_op jit(solution)/shard_map/dispatch/all_to_all | solution.py:283
  36.6 91.9 %all-gather.5.cloned.1.call-start = ((), (), s32[]{:S(2)}) async-start(), calls=%async_computation.2 | async-start | bytes 2359296 | tf_op jit(solution)/shard_map/keys/all_gather | solution.py:298
  36.7 40.4 %collective-permute-start.1 = (bf16[128,512]{1,0:T(8,128)(2,1)S(1)}, bf16[128,512]{1,0:T(8,128)(2,1)S(1)}, u32[]{:S(2)}, u32[]{:S(2)}) collective-permute-start(bf16[128,512]{1,0:T(8,128)(2,1)S(1)} %pad_maximum_fusion.1), channel_id=1, source_target_pairs={{0,272},{8,280},{16,0},{24,8},{1,273},{9,281},{17,1},{25,9},{2,274... | collective-permute-start | bytes 393224 | tf_op jit(solution)/shard_map/keys/ppermute | solution.py:296
  77.0 6.6 %collective-permute-start.2 = (bf16[128,512]{1,0:T(8,128)(2,1)S(1)}, bf16[128,512]{1,0:T(8,128)(2,1)S(1)}, u32[]{:S(2)}, u32[]{:S(2)}) collective-permute-start(bf16[128,512]{1,0:T(8,128)(2,1)S(1)} %collective-permute-done.1), channel_id=1, source_target_pairs={{272,256},{280,264},{0,272},{8,280},{273,257},{281,265},{1,273},{9... | collective-permute-start | bytes 393224 | tf_op jit(solution)/shard_map/keys/ppermute | solution.py:296
  90.5 44.5 %all-to-all-start.1 = ((bf16[32,8,3072]{2,1,0:T(8,128)(2,1)}), bf16[32,8,3072]{2,1,0:T(8,128)(2,1)S(1)}, u32[]{:S(2)}, u32[]{:S(2)}) async-start(bf16[32,8,3072]{2,1,0:T(8,128)(2,1)} %bitcast.20), calls=%async_computation.1 | async-start | bytes 3145728 | tf_op jit(solution)/shard_map/experts/all_to_all | solution.py:312
  128.5 6.6 %copy-start = (bf16[256,512]{1,0:T(8,128)(2,1)S(1)}, bf16[256,512]{1,0:T(8,128)(2,1)}, u32[]{:S(2)}) copy-start(bf16[256,512]{1,0:T(8,128)(2,1)} %get-tuple-element.19.mix_b_ref) | copy-start | bytes 786436
  128.5 6.6 %copy-start.1 = (bf16[256,256]{1,0:T(8,128)(2,1)S(1)}, bf16[256,256]{1,0:T(8,128)(2,1)}, u32[]{:S(2)}) copy-start(bf16[256,256]{1,0:T(8,128)(2,1)} %get-tuple-element.18.mix_a_ref) | copy-start | bytes 393220
Sparse Core Ops, SparseCore 0:
  22.5 50.7 all-gather.6
  84.5 43.9 all-gather.4

commit v9 on v8

--- a/solution.py
+++ b/solution.py
@@ -292,7 +292,7 @@
         deep = halves * depth
         kv_passed = kv
         for leg in range(2):
-            route = [((z - leg * depth // 2) % deep, (z - (leg + 1) * depth // 2) % deep) for z in range(depth)]
+            route = [((z + leg * depth // 2) % deep, (z + (leg + 1) * depth // 2) % deep) for z in range(depth)]
             kv_passed = lax.ppermute(kv_passed, ("zh", "zl"), route)
         kv_pair = jnp.stack([kv, kv_passed])
         kv_all = lax.all_gather(kv_pair, "y", axis=0)

time: 144 us -> 149 us (1.035)
  starting transfers between devices: 38.7 us -> 45.9 us
  waiting for transfers between devices: 70.5 us -> 68.3 us
    all_to_all x1, starting transfers between devices: 9.07 us -> 20.5 us  [shards(): lax.all_to_all(answers.reshape(owners, LOW, wide), CHIPS, split_axis=0, c...]
    ppermute x2, waiting for transfers between devices: 37.7 us -> 30 us  [shards(): kv_passed = lax.ppermute(kv_passed, ('zh', 'zl'), route)]
    ppermute x2, starting transfers between devices: 9.25 us -> 4.93 us  [shards(): kv_passed = lax.ppermute(kv_passed, ('zh', 'zl'), route)]
    all_to_all x1, waiting for transfers between devices: 0.01 us -> 3.62 us  [shards(): lax.all_to_all(answers.reshape(owners, LOW, wide), CHIPS, split_axis=0, c...]
    all_to_all x1, waiting for transfers between devices: 0.01 us -> 2.28 us  [shards(): lax.all_to_all(outgoing.reshape(owners, LOW, wide), CHIPS, split_axis=0,...]
  transfers between devices with their start and end apart: 7 -> 7, of which waited for: 4 -> 5; matrix products, arithmetic and copies ran while one was open for 1% -> 0% of each run, Pallas kernels for 11% -> 11%
where the time goes in v9:
time: 149 us; the launch traced here: 148 us
  waiting for transfers between devices  68.3 us (46%)
  starting transfers between devices  45.9 us (31%)
  Pallas kernels  19.3 us (13%)
  between operations  14.1 us (9%)
    ppermute x2, waiting for transfers between devices, shards(): kv_passed = lax.ppermute(kv_passed, ('zh', 'zl'), route)  30 us
    all_gather x1, waiting for transfers between devices, shards(): kv_all = lax.all_gather(kv_pair, 'y', axis=0)  28.5 us
    all_to_all x1, starting transfers between devices, shards(): lax.all_to_all(answers.reshape(owners, LOW, wide), CHIPS, split_axis=0, c...  20.5 us
    all_to_all x1, starting transfers between devices, shards(): lax.all_to_all(outgoing.reshape(owners, LOW, wide), CHIPS, split_axis=0,...  14.2 us
    pallas_call x1, Pallas kernels, shards(): pl.pallas_call(functools.partial(attend_kernel, halves, ring, heads_kv),...  6.57 us
    pallas_call x1, Pallas kernels, shards(): pl.pallas_call(functools.partial(expert_kernel, hidden_units), out_shape=...  6.11 us
    ppermute x1, starting transfers between devices, shards(): part = lax.ppermute(packed, ('zh', 'zl', 'c'), route)  6.09 us
    ppermute x2, starting transfers between devices, shards(): kv_passed = lax.ppermute(kv_passed, ('zh', 'zl'), route)  4.93 us
  transfers between devices with their start and end apart: 7, of which 5 were waited for; matrix products, arithmetic and copies ran while one was open for 0% of the time, Pallas kernels for 11%

profile of v9, /device:TPU:6, one launch (start us, length us, event | category | flops | bytes accessed | tf_op | source)
XLA Modules:
  0.0 148.4 jit_solution(16863795037034536431)
XLA Ops:
  7.2 0.0 copy-start.3
  7.2 0.0 copy-start.2
  7.2 0.0 all-gather.7.cloned.1.call-start
  7.2 1.7 %pack.1 = bf16[128,1152]{1,0:T(8,128)(2,1)} custom-call(bf16[128,384]{1,0:T(8,128)(2,1)} %bitcast.31, bf16[128,384]{1,0:T(8,128)(2,1)} %bitcast.32, bf16[384,128]{1,0:T(8,128)(2,1)} %bitcast.33), custom_call_target="tpu_custom_call" | custom-call | tf_op jit(solution)/shard_map/weights/pack/pallas_call | solution.py:253
  8.9 6.1 %collective-permute-start = (bf16[128,1152]{1,0:T(8,128)(2,1)}, bf16[128,1152]{1,0:T(8,128)(2,1)}, u32[]{:S(2)}, u32[]{:S(2)}) collective-permute-start(bf16[128,1152]{1,0:T(8,128)(2,1)} %pack.1), channel_id=1, source_target_pairs={{0,16},{1,272},{8,24},{9,280},{16,256},{17,0},{24,264},{25,8},{256... | collective-permute-start | bytes 884744 | tf_op jit(solution)/shard_map/weights/ppermute | solution.py:267
  15.0 3.4 %dispatch.1 = (bf16[256,3072]{1,0:T(8,128)(2,1)}, bf16[256,256]{1,0:T(8,128)(2,1)}, bf16[256,512]{1,0:T(8,128)(2,1)}) custom-call(bf16[128,2048]{1,0:T(8,128)(2,1)} %bitcast.38, f32[1,2048]{1,0:T(1,128)} %bitcast.40, s32[8,128]{1,0:T(8,128)} %bitcast.41, f32[8,128]{1,0:T(8,128)} %bitcast.42), custom_call_target="tpu_custom_call" | custom-call | flops 536870912 | bytes 4194304 | tf_op jit(solution)/shard_map/dispatch/dispatch/pallas_call | solution.py:270
  18.5 0.0 copy-done.3
  18.5 0.0 copy-done.2
  18.5 3.8 %collective-permute-done = bf16[128,1152]{1,0:T(8,128)(2,1)} collective-permute-done((bf16[128,1152]{1,0:T(8,128)(2,1)}, bf16[128,1152]{1,0:T(8,128)(2,1)}, u32[]{:S(2)}, u32[]{:S(2)}) %collective-permute-start) | collective-permute-done | bytes 294944 | tf_op jit(solution)/shard_map/weights/ppermute | solution.py:267
  22.3 0.0 all-gather.7.cloned.1.call-update
  22.4 14.2 %all-to-all-start = ((bf16[32,8,3072]{2,1,0:T(8,128)(2,1)}), bf16[32,8,3072]{2,1,0:T(8,128)(2,1)S(1)}, u32[]{:S(2)}, u32[]{:S(2)}) async-start(bf16[32,8,3072]{2,1,0:T(8,128)(2,1)} %bitcast.27), calls=%async_computation | async-start | bytes 3145728 | tf_op jit(solution)/shard_map/dispatch/all_to_all | solution.py:283
  36.6 0.0 all-gather.5.cloned.1.call-start
  36.7 4.3 %collective-permute-start.1 = (bf16[128,512]{1,0:T(8,128)(2,1)S(1)}, bf16[128,512]{1,0:T(8,128)(2,1)S(1)}, u32[]{:S(2)}, u32[]{:S(2)}) collective-permute-start(bf16[128,512]{1,0:T(8,128)(2,1)S(1)} %pad_maximum_fusion.1), channel_id=1, source_target_pairs={{0,16},{8,24},{16,256},{24,264},{1,17},{9,25},{17,257},{25,265},{2... | collective-permute-start | bytes 393224 | tf_op jit(solution)/shard_map/keys/ppermute | solution.py:296
  40.9 30.0 %collective-permute-done.1 = bf16[128,512]{1,0:T(8,128)(2,1)S(1)} collective-permute-done((bf16[128,512]{1,0:T(8,128)(2,1)S(1)}, bf16[128,512]{1,0:T(8,128)(2,1)S(1)}, u32[]{:S(2)}, u32[]{:S(2)}) %collective-permute-start.1) | collective-permute-done | bytes 131104 | tf_op jit(solution)/shard_map/keys/ppermute | solution.py:296
  70.9 0.7 collective-permute-start.2
  71.6 0.0 collective-permute-done.2
  71.6 0.7 pad_maximum_fusion
  72.3 0.0 all-gather.5.cloned.1.call-update
  72.3 2.3 %all-to-all-done = bf16[32,8,3072]{2,1,0:T(8,128)(2,1)S(1)} async-done(((bf16[32,8,3072]{2,1,0:T(8,128)(2,1)}), bf16[32,8,3072]{2,1,0:T(8,128)(2,1)S(1)}, u32[]{:S(2)}, u32[]{:S(2)}) %all-to-all-start) | async-done | bytes 1572896 | tf_op jit(solution)/shard_map/dispatch/all_to_all | solution.py:283
  74.6 0.0 all-gather.7.cloned.1.call-done
  74.6 6.1 %experts.1 = bf16[256,3072]{1,0:T(8,128)(2,1)} custom-call(bf16[256,3072]{1,0:T(8,128)(2,1)S(1)} %bitcast.26, bf16[16,128,1152]{2,1,0:T(8,128)(2,1)} %bitcast.36), custom_call_target="tpu_custom_call" | custom-call | flops 2415919104 | bytes 8388608 | tf_op jit(solution)/shard_map/experts/experts/pallas_call | solution.py:302
  80.7 20.5 %all-to-all-start.1 = ((bf16[32,8,3072]{2,1,0:T(8,128)(2,1)}), bf16[32,8,3072]{2,1,0:T(8,128)(2,1)S(1)}, u32[]{:S(2)}, u32[]{:S(2)}) async-start(bf16[32,8,3072]{2,1,0:T(8,128)(2,1)} %bitcast.20), calls=%async_computation.1 | async-start | bytes 3145728 | tf_op jit(solution)/shard_map/experts/all_to_all | solution.py:312
  101.3 28.5 %all-gather.5.cloned.1.call-done = bf16[16,128,512]{2,1,0:T(8,128)(2,1)} async-done(((bf16[2,128,512]{2,1,0:T(8,128)(2,1)}), bf16[16,128,512]{2,1,0:T(8,128)(2,1)}) %all-gather.5.cloned.1.call-update) | async-done | bytes 2097168 | tf_op jit(solution)/shard_map/keys/all_gather | solution.py:298
  129.8 0.0 copy-start
  129.8 0.0 copy-start.1
  129.8 6.6 %attend.1 = bf16[128,2048]{1,0:T(8,128)(2,1)} custom-call(bf16[128,2048]{1,0:T(8,128)(2,1)} %bitcast.39, bf16[8,2,128,512]{3,2,1,0:T(8,128)(2,1)} %bitcast.37, s32[1]{0:T(128)} %bitcast.15.place_ref), custom_call_target="tpu_custom_call" | custom-call | flops 2147483648 | bytes 4194304 | tf_op jit(solution)/shard_map/attend/attend/pallas_call | solution.py:318
  136.4 3.6 %all-to-all-done.1 = bf16[32,8,3072]{2,1,0:T(8,128)(2,1)S(1)} async-done(((bf16[32,8,3072]{2,1,0:T(8,128)(2,1)}), bf16[32,8,3072]{2,1,0:T(8,128)(2,1)S(1)}, u32[]{:S(2)}, u32[]{:S(2)}) %all-to-all-start.1) | async-done | bytes 1572896 | tf_op jit(solution)/shard_map/experts/all_to_all | solution.py:312
  140.0 0.0 copy-done
  140.0 0.0 copy-done.1
  140.0 1.5 %combine.1 = bf16[128,2048]{1,0:T(8,128)(2,1)} custom-call(bf16[256,3072]{1,0:T(8,128)(2,1)S(1)} %bitcast.25, bf16[256,256]{1,0:T(8,128)(2,1)S(1)} %copy-done.1, bf16[256,512]{1,0:T(8,128)(2,1)S(1)} %copy-done), custom_call_target="tpu_custom_call" | custom-call | flops 536870912 | bytes 3145728 | tf_op jit(solution)/shard_map/combine/combine/pallas_call | solution.py:333
  (1 shorter events, 0.0 us)
Async XLA Ops:
  7.2 11.3 %copy-start.3 = (bf16[1,128,256]{2,1,0:T(8,128)(2,1)S(1)}, bf16[1,128,256]{2,1,0:T(8,128)(2,1)}, u32[]{:S(2)}) copy-start(bf16[1,128,256]{2,1,0:T(8,128)(2,1)} %param.11) | copy-start | bytes 196612
  7.2 11.3 %copy-start.2 = (bf16[1,128,256]{2,1,0:T(8,128)(2,1)S(1)}, bf16[1,128,256]{2,1,0:T(8,128)(2,1)}, u32[]{:S(2)}) copy-start(bf16[1,128,256]{2,1,0:T(8,128)(2,1)} %param.12) | copy-start | bytes 196612
  7.2 67.4 %all-gather.7.cloned.1.call-start = ((), (), s32[]{:S(2)}) async-start(), calls=%async_computation.3 | async-start | bytes 5013504 | tf_op jit(solution)/shard_map/keys/all_gather | solution.py:291
  8.9 13.4 %collective-permute-start = (bf16[128,1152]{1,0:T(8,128)(2,1)}, bf16[128,1152]{1,0:T(8,128)(2,1)}, u32[]{:S(2)}, u32[]{:S(2)}) collective-permute-start(bf16[128,1152]{1,0:T(8,128)(2,1)} %pack.1), channel_id=1, source_target_pairs={{0,16},{1,272},{8,24},{9,280},{16,256},{17,0},{24,264},{25,8},{256... | collective-permute-start | bytes 884744 | tf_op jit(solution)/shard_map/weights/ppermute | solution.py:267
  22.4 52.2 %all-to-all-start = ((bf16[32,8,3072]{2,1,0:T(8,128)(2,1)}), bf16[32,8,3072]{2,1,0:T(8,128)(2,1)S(1)}, u32[]{:S(2)}, u32[]{:S(2)}) async-start(bf16[32,8,3072]{2,1,0:T(8,128)(2,1)} %bitcast.27), calls=%async_computation | async-start | bytes 3145728 | tf_op jit(solution)/shard_map/dispatch/all_to_all | solution.py:283
  36.6 93.2 %all-gather.5.cloned.1.call-start = ((), (), s32[]{:S(2)}) async-start(), calls=%async_computation.2 | async-start | bytes 2359296 | tf_op jit(solution)/shard_map/keys/all_gather | solution.py:298
  36.7 34.2 %collective-permute-start.1 = (bf16[128,512]{1,0:T(8,128)(2,1)S(1)}, bf16[128,512]{1,0:T(8,128)(2,1)S(1)}, u32[]{:S(2)}, u32[]{:S(2)}) collective-permute-start(bf16[128,512]{1,0:T(8,128)(2,1)S(1)} %pad_maximum_fusion.1), channel_id=1, source_target_pairs={{0,16},{8,24},{16,256},{24,264},{1,17},{9,25},{17,257},{25,265},{2... | collective-permute-start | bytes 393224 | tf_op jit(solution)/shard_map/keys/ppermute | solution.py:296
  70.9 0.7 collective-permute-start.2
  80.7 59.3 %all-to-all-start.1 = ((bf16[32,8,3072]{2,1,0:T(8,128)(2,1)}), bf16[32,8,3072]{2,1,0:T(8,128)(2,1)S(1)}, u32[]{:S(2)}, u32[]{:S(2)}) async-start(bf16[32,8,3072]{2,1,0:T(8,128)(2,1)} %bitcast.20), calls=%async_computation.1 | async-start | bytes 3145728 | tf_op jit(solution)/shard_map/experts/all_to_all | solution.py:312
  129.8 10.2 %copy-start = (bf16[256,512]{1,0:T(8,128)(2,1)S(1)}, bf16[256,512]{1,0:T(8,128)(2,1)}, u32[]{:S(2)}) copy-start(bf16[256,512]{1,0:T(8,128)(2,1)} %get-tuple-element.19.mix_b_ref) | copy-start | bytes 786436
  129.8 10.2 %copy-start.1 = (bf16[256,256]{1,0:T(8,128)(2,1)S(1)}, bf16[256,256]{1,0:T(8,128)(2,1)}, u32[]{:S(2)}) copy-start(bf16[256,256]{1,0:T(8,128)(2,1)} %get-tuple-element.18.mix_a_ref) | copy-start | bytes 393220
Sparse Core Ops, SparseCore 0:
  22.5 50.7 all-gather.6
  76.0 53.8 all-gather.4

commit v10 on v7

--- a/solution.py
+++ b/solution.py
@@ -23,23 +23,21 @@
 SMEM = pl.BlockSpec(memory_space=pltpu.SMEM)
 
 
-def pack_kernel(gate_ref, up_ref, down_ref, out_ref, sems):
+def pack_kernel(gate_ref, up_ref, down_ref, out_ref, held_ref, in_sems, out_sems):
     rows, units = gate_ref.shape
-    copies = [
-        pltpu.make_async_copy(gate_ref, out_ref.at[:, pl.ds(0, units)], sems.at[0]),
-        pltpu.make_async_copy(up_ref, out_ref.at[:, pl.ds(units, units)], sems.at[1]),
-    ]
+    pieces = [(gate_ref, 0, units), (up_ref, units, units)]
     for j in range(units // rows):
-        copies.append(
-            pltpu.make_async_copy(
-                down_ref.at[pl.ds(j * rows, rows)],
-                out_ref.at[:, pl.ds(2 * units + j * rows, rows)],
-                sems.at[2 + j],
-            )
-        )
-    for copy in copies:
-        copy.start()
-    for copy in copies:
+        pieces.append((down_ref.at[pl.ds(j * rows, rows)], 2 * units + j * rows, rows))
+    arriving, leaving = [], []
+    for i, (source, start, columns) in enumerate(pieces):
+        held = held_ref.at[:, pl.ds(start, columns)]
+        arriving.append(pltpu.make_async_copy(source, held, in_sems.at[i]))
+        leaving.append(pltpu.make_async_copy(held, out_ref.at[:, pl.ds(start, columns)], out_sems.at[i]))
+        arriving[i].start()
+    for i in range(len(pieces)):
+        arriving[i].wait()
+        leaving[i].start()
+    for copy in leaving:
         copy.wait()
 
 
@@ -254,8 +252,12 @@
             pack_kernel,
             out_shape=jax.ShapeDtypeStruct((w_gate.shape[1], 3 * hidden_units), BF16),
             in_specs=[HBM] * 3,
-            out_specs=VMEM,
-            scratch_shapes=[pltpu.SemaphoreType.DMA((2 + hidden_units // tokens,))],
+            out_specs=HBM,
+            scratch_shapes=[
+                pltpu.VMEM((w_gate.shape[1], 3 * hidden_units), BF16),
+                pltpu.SemaphoreType.DMA((2 + hidden_units // tokens,)),
+                pltpu.SemaphoreType.DMA((2 + hidden_units // tokens,)),
+            ],
             name="pack",
         )(w_gate[0], w_up[0], w_down[0])
         route = []

time: 139 us -> 139 us (level)
  no operation moved by 1% of the time
where the time goes in v10:
time: 139 us; the launch traced here: 138 us
  waiting for transfers between devices  64.4 us (46%)
  starting transfers between devices  39.7 us (29%)
  Pallas kernels  19.3 us (14%)
  between operations  14.1 us (10%)
    all_gather x1, waiting for transfers between devices, shards(): kv_all = lax.all_gather(kv_pair, 'y', axis=0)  28.8 us
    ppermute x1, waiting for transfers between devices, shards(): kv_passed = lax.ppermute(kv, 'zh', [(0, 1)])  26.9 us
    all_to_all x1, starting transfers between devices, shards(): lax.all_to_all(outgoing.reshape(owners, LOW, wide), CHIPS, split_axis=0,...  14.2 us
    all_to_all x1, starting transfers between devices, shards(): lax.all_to_all(answers.reshape(owners, LOW, wide), CHIPS, split_axis=0, c...  12 us
    ppermute x1, starting transfers between devices, shards(): kv_passed = lax.ppermute(kv, 'zh', [(0, 1)])  7.29 us
    pallas_call x1, Pallas kernels, shards(): pl.pallas_call(functools.partial(attend_kernel, halves, ring, heads_kv),...  6.57 us
    pallas_call x1, Pallas kernels, shards(): pl.pallas_call(functools.partial(expert_kernel, hidden_units), out_shape=...  6.12 us
    ppermute x1, starting transfers between devices, shards(): part = lax.ppermute(packed, ('zh', 'zl', 'c'), route)  6.09 us
  transfers between devices with their start and end apart: 6, of which 5 were waited for; matrix products, arithmetic and copies ran while one was open for 1% of the time, Pallas kernels for 12%

profile of v10, /device:TPU:6, one launch (start us, length us, event | category | flops | bytes accessed | tf_op | source)
XLA Modules:
  0.0 138.3 jit_solution(4577709909506217640)
XLA Ops:
  7.2 0.0 copy-start.3
  7.2 0.0 copy-start.2
  7.2 0.0 all-gather.7.cloned.1.call-start
  7.2 1.7 %pack.1 = bf16[128,1152]{1,0:T(8,128)(2,1)} custom-call(bf16[128,384]{1,0:T(8,128)(2,1)} %bitcast.31, bf16[128,384]{1,0:T(8,128)(2,1)} %bitcast.32, bf16[384,128]{1,0:T(8,128)(2,1)} %bitcast.33), custom_call_target="tpu_custom_call" | custom-call | tf_op jit(solution)/shard_map/weights/pack/pallas_call | solution.py:251
  8.9 6.1 %collective-permute-start = (bf16[128,1152]{1,0:T(8,128)(2,1)}, bf16[128,1152]{1,0:T(8,128)(2,1)}, u32[]{:S(2)}, u32[]{:S(2)}) collective-permute-start(bf16[128,1152]{1,0:T(8,128)(2,1)} %pack.1), channel_id=1, source_target_pairs={{0,16},{1,272},{8,24},{9,280},{16,256},{17,0},{24,264},{25,8},{256... | collective-permute-start | bytes 884744 | tf_op jit(solution)/shard_map/weights/ppermute | solution.py:269
  15.0 3.4 %dispatch.1 = (bf16[256,3072]{1,0:T(8,128)(2,1)}, bf16[256,256]{1,0:T(8,128)(2,1)}, bf16[256,512]{1,0:T(8,128)(2,1)}) custom-call(bf16[128,2048]{1,0:T(8,128)(2,1)} %bitcast.38, f32[1,2048]{1,0:T(1,128)} %bitcast.40, s32[8,128]{1,0:T(8,128)} %bitcast.41, f32[8,128]{1,0:T(8,128)} %bitcast.42), custom_call_target="tpu_custom_call" | custom-call | flops 536870912 | bytes 4194304 | tf_op jit(solution)/shard_map/dispatch/dispatch/pallas_call | solution.py:272
  18.5 0.0 copy-done.3
  18.5 0.0 copy-done.2
  18.5 3.8 %collective-permute-done = bf16[128,1152]{1,0:T(8,128)(2,1)} collective-permute-done((bf16[128,1152]{1,0:T(8,128)(2,1)}, bf16[128,1152]{1,0:T(8,128)(2,1)}, u32[]{:S(2)}, u32[]{:S(2)}) %collective-permute-start) | collective-permute-done | bytes 294944 | tf_op jit(solution)/shard_map/weights/ppermute | solution.py:269
  22.3 0.0 all-gather.7.cloned.1.call-update
  22.4 14.2 %all-to-all-start = ((bf16[32,8,3072]{2,1,0:T(8,128)(2,1)}), bf16[32,8,3072]{2,1,0:T(8,128)(2,1)S(1)}, u32[]{:S(2)}, u32[]{:S(2)}) async-start(bf16[32,8,3072]{2,1,0:T(8,128)(2,1)} %bitcast.27), calls=%async_computation | async-start | bytes 3145728 | tf_op jit(solution)/shard_map/dispatch/all_to_all | solution.py:285
  36.6 0.0 all-gather.5.cloned.1.call-start
  36.7 7.3 %collective-permute-start.1 = (bf16[128,512]{1,0:T(8,128)(2,1)S(1)}, bf16[128,512]{1,0:T(8,128)(2,1)S(1)}, u32[]{:S(2)}, u32[]{:S(2)}) collective-permute-start(bf16[128,512]{1,0:T(8,128)(2,1)S(1)} %pad_maximum_fusion.1), channel_id=1, source_target_pairs={{0,256},{1,257},{2,258},{3,259},{4,260},{5,261},{6,262},{7,263},{8... | collective-permute-start | bytes 393224 | tf_op jit(solution)/shard_map/keys/ppermute | solution.py:294
  44.0 26.9 %collective-permute-done.1 = bf16[128,512]{1,0:T(8,128)(2,1)S(1)} collective-permute-done((bf16[128,512]{1,0:T(8,128)(2,1)S(1)}, bf16[128,512]{1,0:T(8,128)(2,1)S(1)}, u32[]{:S(2)}, u32[]{:S(2)}) %collective-permute-start.1) | collective-permute-done | bytes 131104 | tf_op jit(solution)/shard_map/keys/ppermute | solution.py:294
  70.9 0.7 pad_maximum_fusion
  71.6 0.0 all-gather.5.cloned.1.call-update
  71.6 2.1 %all-to-all-done = bf16[32,8,3072]{2,1,0:T(8,128)(2,1)S(1)} async-done(((bf16[32,8,3072]{2,1,0:T(8,128)(2,1)}), bf16[32,8,3072]{2,1,0:T(8,128)(2,1)S(1)}, u32[]{:S(2)}, u32[]{:S(2)}) %all-to-all-start) | async-done | bytes 1572896 | tf_op jit(solution)/shard_map/dispatch/all_to_all | solution.py:285
  73.8 0.0 all-gather.7.cloned.1.call-done
  73.8 6.1 %experts.1 = bf16[256,3072]{1,0:T(8,128)(2,1)} custom-call(bf16[256,3072]{1,0:T(8,128)(2,1)S(1)} %bitcast.26, bf16[16,128,1152]{2,1,0:T(8,128)(2,1)} %bitcast.36), custom_call_target="tpu_custom_call" | custom-call | flops 2415919104 | bytes 8388608 | tf_op jit(solution)/shard_map/experts/experts/pallas_call | solution.py:300
  79.9 12.0 %all-to-all-start.1 = ((bf16[32,8,3072]{2,1,0:T(8,128)(2,1)}), bf16[32,8,3072]{2,1,0:T(8,128)(2,1)S(1)}, u32[]{:S(2)}, u32[]{:S(2)}) async-start(bf16[32,8,3072]{2,1,0:T(8,128)(2,1)} %bitcast.20), calls=%async_computation.1 | async-start | bytes 3145728 | tf_op jit(solution)/shard_map/experts/all_to_all | solution.py:310
  91.9 28.8 %all-gather.5.cloned.1.call-done = bf16[16,128,512]{2,1,0:T(8,128)(2,1)} async-done(((bf16[2,128,512]{2,1,0:T(8,128)(2,1)}), bf16[16,128,512]{2,1,0:T(8,128)(2,1)}) %all-gather.5.cloned.1.call-update) | async-done | bytes 2097168 | tf_op jit(solution)/shard_map/keys/all_gather | solution.py:296
  120.8 0.0 copy-start
  120.8 0.0 copy-start.1
  120.8 6.6 %attend.1 = bf16[128,2048]{1,0:T(8,128)(2,1)} custom-call(bf16[128,2048]{1,0:T(8,128)(2,1)} %bitcast.39, bf16[8,2,128,512]{3,2,1,0:T(8,128)(2,1)} %bitcast.37, s32[1]{0:T(128)} %bitcast.15.place_ref), custom_call_target="tpu_custom_call" | custom-call | flops 2147483648 | bytes 4194304 | tf_op jit(solution)/shard_map/attend/attend/pallas_call | solution.py:316
  127.4 2.6 %all-to-all-done.1 = bf16[32,8,3072]{2,1,0:T(8,128)(2,1)S(1)} async-done(((bf16[32,8,3072]{2,1,0:T(8,128)(2,1)}), bf16[32,8,3072]{2,1,0:T(8,128)(2,1)S(1)}, u32[]{:S(2)}, u32[]{:S(2)}) %all-to-all-start.1) | async-done | bytes 1572896 | tf_op jit(solution)/shard_map/experts/all_to_all | solution.py:310
  130.0 0.0 copy-done
  130.0 0.0 copy-done.1
  130.0 1.5 %combine.1 = bf16[128,2048]{1,0:T(8,128)(2,1)} custom-call(bf16[256,3072]{1,0:T(8,128)(2,1)S(1)} %bitcast.25, bf16[256,256]{1,0:T(8,128)(2,1)S(1)} %copy-done.1, bf16[256,512]{1,0:T(8,128)(2,1)S(1)} %copy-done), custom_call_target="tpu_custom_call" | custom-call | flops 536870912 | bytes 3145728 | tf_op jit(solution)/shard_map/combine/combine/pallas_call | solution.py:331
  (1 shorter events, 0.0 us)
Async XLA Ops:
  7.2 11.3 %copy-start.3 = (bf16[1,128,256]{2,1,0:T(8,128)(2,1)S(1)}, bf16[1,128,256]{2,1,0:T(8,128)(2,1)}, u32[]{:S(2)}) copy-start(bf16[1,128,256]{2,1,0:T(8,128)(2,1)} %param.11) | copy-start | bytes 196612
  7.2 11.3 %copy-start.2 = (bf16[1,128,256]{2,1,0:T(8,128)(2,1)S(1)}, bf16[1,128,256]{2,1,0:T(8,128)(2,1)}, u32[]{:S(2)}) copy-start(bf16[1,128,256]{2,1,0:T(8,128)(2,1)} %param.12) | copy-start | bytes 196612
  7.2 66.6 %all-gather.7.cloned.1.call-start = ((), (), s32[]{:S(2)}) async-start(), calls=%async_computation.3 | async-start | bytes 5013504 | tf_op jit(solution)/shard_map/keys/all_gather | solution.py:293
  8.9 13.4 %collective-permute-start = (bf16[128,1152]{1,0:T(8,128)(2,1)}, bf16[128,1152]{1,0:T(8,128)(2,1)}, u32[]{:S(2)}, u32[]{:S(2)}) collective-permute-start(bf16[128,1152]{1,0:T(8,128)(2,1)} %pack.1), channel_id=1, source_target_pairs={{0,16},{1,272},{8,24},{9,280},{16,256},{17,0},{24,264},{25,8},{256... | collective-permute-start | bytes 884744 | tf_op jit(solution)/shard_map/weights/ppermute | solution.py:269
  22.4 51.4 %all-to-all-start = ((bf16[32,8,3072]{2,1,0:T(8,128)(2,1)}), bf16[32,8,3072]{2,1,0:T(8,128)(2,1)S(1)}, u32[]{:S(2)}, u32[]{:S(2)}) async-start(bf16[32,8,3072]{2,1,0:T(8,128)(2,1)} %bitcast.27), calls=%async_computation | async-start | bytes 3145728 | tf_op jit(solution)/shard_map/dispatch/all_to_all | solution.py:285
  36.6 84.2 %all-gather.5.cloned.1.call-start = ((), (), s32[]{:S(2)}) async-start(), calls=%async_computation.2 | async-start | bytes 2359296 | tf_op jit(solution)/shard_map/keys/all_gather | solution.py:296
  36.7 34.2 %collective-permute-start.1 = (bf16[128,512]{1,0:T(8,128)(2,1)S(1)}, bf16[128,512]{1,0:T(8,128)(2,1)S(1)}, u32[]{:S(2)}, u32[]{:S(2)}) collective-permute-start(bf16[128,512]{1,0:T(8,128)(2,1)S(1)} %pad_maximum_fusion.1), channel_id=1, source_target_pairs={{0,256},{1,257},{2,258},{3,259},{4,260},{5,261},{6,262},{7,263},{8... | collective-permute-start | bytes 393224 | tf_op jit(solution)/shard_map/keys/ppermute | solution.py:294
  79.9 50.1 %all-to-all-start.1 = ((bf16[32,8,3072]{2,1,0:T(8,128)(2,1)}), bf16[32,8,3072]{2,1,0:T(8,128)(2,1)S(1)}, u32[]{:S(2)}, u32[]{:S(2)}) async-start(bf16[32,8,3072]{2,1,0:T(8,128)(2,1)} %bitcast.20), calls=%async_computation.1 | async-start | bytes 3145728 | tf_op jit(solution)/shard_map/experts/all_to_all | solution.py:310
  120.8 9.2 %copy-start = (bf16[256,512]{1,0:T(8,128)(2,1)S(1)}, bf16[256,512]{1,0:T(8,128)(2,1)}, u32[]{:S(2)}) copy-start(bf16[256,512]{1,0:T(8,128)(2,1)} %get-tuple-element.19.mix_b_ref) | copy-start | bytes 786436
  120.8 9.2 %copy-start.1 = (bf16[256,256]{1,0:T(8,128)(2,1)S(1)}, bf16[256,256]{1,0:T(8,128)(2,1)}, u32[]{:S(2)}) copy-start(bf16[256,256]{1,0:T(8,128)(2,1)} %get-tuple-element.18.mix_a_ref) | copy-start | bytes 393220
Sparse Core Ops, SparseCore 0:
  22.5 50.7 all-gather.6
  75.9 44.7 all-gather.4
